TPU v7x, 32 devices: a whole 2x2x4 slice. The times are simulated.
32 devices in a mesh: gx: 4 (over y, x), gz: 8 (over z, core).
Axes of the slice: x: 2, y: 2, z: 4, core: 2. Of those that a mesh axis runs over, the one named last changes fastest.
Arguments:
- pop_ratio: float32 [19, 16, 64, 512], P(None, None, 'gz', 'gx'), may hold values from 0.6 to 1.4
- solid_blocks: int32 [4, 16, 128], P(None, 'gz', 'gx'), may hold values 0 or 1
- shift_whole: int32 [2], replicated, may hold values from 0 to 511
- shift_frac: int32 [2], replicated, may hold values from 0 to 4095
Outputs:
- populations: float32 [19, 16, 64, 512], P(None, None, 'gz', 'gx')
- accumulated: float32 [2, 16, 64, 512], P(None, None, 'gz', 'gx')
- profiles: float32 [2, 16, 64], P(None, None, 'gz')
Inputs may be any that keep to these rules, and one draw needn't show every extreme that they name: `shift_whole`: whole cells of the displacement, below 512.
All inputs are finite; a program needn't handle non-finite values. No bound on the sum of `solid_blocks` on one device may be relied on, other than what follows from the above.
Results may differ from a plain program's by a relative error of at most 0.00023.
Values sent between devices are 32-bit elements; how exact they have to be, the bound alone decides.
No kernel may reach another device: no remote copies, remote signals or barrier semaphores. Data moves between devices by JAX's collectives and lax.ppermute only.
A program may use at most 64 MiB of HBM per device.

v0:
```python
import jax
import jax.numpy as jnp
import numpy as np
from jax import lax
from jax.sharding import PartitionSpec as P

STEPS = 2
BLOCK = 4


velocity_list = [
    (0, 0, 0),
    (1, 0, 0),
    (-1, 0, 0),
    (0, 1, 0),
    (0, -1, 0),
    (0, 0, 1),
    (0, 0, -1),
    (1, 1, 0),
    (-1, -1, 0),
    (1, -1, 0),
    (-1, 1, 0),
    (1, 0, 1),
    (-1, 0, -1),
    (1, 0, -1),
    (-1, 0, 1),
    (0, 1, 1),
    (0, -1, -1),
    (0, 1, -1),
    (0, -1, 1),
]
velocities = np.array(velocity_list)
lattice_weights = np.array([1.0 / 3.0] + [1.0 / 18.0] * 6 + [1.0 / 36.0] * 12)
opposite = np.array(
    [velocity_list.index((-entry[0], -entry[1], -entry[2])) for entry in velocity_list]
)
rising = [index for index in range(19) if velocities[index, 1] == 1]
falling = [index for index in range(19) if velocities[index, 1] == -1]
wall_speed = 0.08
visc_rate = 1.25
fraction_unit = 4096.0
relax_rates = np.array(
    [
        0.0,
        1.19,
        1.4,
        0.0,
        1.2,
        0.0,
        1.2,
        0.0,
        1.2,
        1.25,
        1.4,
        1.25,
        1.4,
        1.25,
        1.25,
        1.25,
        1.98,
        1.98,
        1.98,
    ]
)


def extended(value, sides, width):
    for axis, dim in sides:
        count, length = (lax.axis_size(axis), value.shape[dim])
        up = [(i, (i + 1) % count) for i in range(count)]
        down = [(j, i) for i, j in up]
        last = lax.slice_in_dim(value, length - width, length, axis=dim)
        initial = lax.slice_in_dim(value, 0, width, axis=dim)
        before = lax.ppermute(last, axis, up)
        after = lax.ppermute(initial, axis, down)
        value = jnp.concatenate([before, value, after], axis=dim)
    return value


def moment_rows():
    vel_x = velocities[:, 0] * 1.0
    vel_y = velocities[:, 1] * 1.0
    vel_z = velocities[:, 2] * 1.0
    speed_sq = vel_x * vel_x + vel_y * vel_y + vel_z * vel_z
    rows = [
        np.ones(19),
        19 * speed_sq - 30,
        (21 * speed_sq * speed_sq - 53 * speed_sq + 24) / 2,
        vel_x,
        (5 * speed_sq - 9) * vel_x,
        vel_y,
        (5 * speed_sq - 9) * vel_y,
        vel_z,
        (5 * speed_sq - 9) * vel_z,
        3 * vel_x * vel_x - speed_sq,
        (3 * speed_sq - 5) * (3 * vel_x * vel_x - speed_sq),
        vel_y * vel_y - vel_z * vel_z,
        (3 * speed_sq - 5) * (vel_y * vel_y - vel_z * vel_z),
        vel_x * vel_y,
        vel_y * vel_z,
        vel_x * vel_z,
        (vel_y * vel_y - vel_z * vel_z) * vel_x,
        (vel_z * vel_z - vel_x * vel_x) * vel_y,
        (vel_x * vel_x - vel_y * vel_y) * vel_z,
    ]
    return np.stack(rows)


def relax_matrix():
    moments = moment_rows()
    scaled = moments.T / np.sum(moments * moments, axis=1)
    return (scaled @ (relax_rates[:, None] * moments)).astype(np.float32)


def column(values):
    return jnp.asarray(np.asarray(values, dtype=np.float32).reshape(-1, 1, 1, 1))


def plane_column(values):
    return jnp.asarray(np.asarray(values, dtype=np.float32).reshape(-1, 1, 1))


def expand(blocks):
    deep, tall, wide = blocks.shape
    big = jnp.broadcast_to(
        blocks[:, None, :, None, :, None], (deep, BLOCK, tall, BLOCK, wide, BLOCK)
    )
    return big.reshape(deep * BLOCK, tall * BLOCK, wide * BLOCK).astype(jnp.float32)


def collide(popul, solid):
    rho = jnp.sum(popul, axis=0)
    mom_x = jnp.sum(column(velocities[:, 0]) * popul, axis=0)
    mom_y = jnp.sum(column(velocities[:, 1]) * popul, axis=0)
    mom_z = jnp.sum(column(velocities[:, 2]) * popul, axis=0)
    inverse = 1.0 / rho
    vel_x = mom_x * inverse
    vel_y = mom_y * inverse
    vel_z = mom_z * inverse
    along = (
        column(velocities[:, 0]) * vel_x
        + column(velocities[:, 1]) * vel_y
        + column(velocities[:, 2]) * vel_z
    )
    speed_sq = vel_x * vel_x + vel_y * vel_y + vel_z * vel_z
    equil = (
        column(lattice_weights) * rho * (1.0 + 3.0 * along + 4.5 * along * along - 1.5 * speed_sq)
    )
    noneq = popul - equil
    relaxed = jnp.dot(
        jnp.asarray(relax_matrix()), noneq.reshape(19, -1), precision=lax.Precision.HIGHEST
    ).reshape(popul.shape)
    post = jnp.where(solid > 0, popul[opposite], popul - relaxed)
    fluid = 1.0 - solid
    stress = -(1.0 - 0.5 * visc_rate) * jnp.sum(
        column(velocities[:, 0] * velocities[:, 1]) * noneq, axis=0
    )
    return (post, jnp.stack([fluid * mom_x, fluid * stress]))


def assemble(shifted, le_top, le_bot):
    pieces = []
    for index in range(19):
        lift = velocities[index, 1]
        if lift == 0:
            pieces.append(shifted[index])
        elif lift > 0:
            pieces.append(
                jnp.concatenate([le_top[rising.index(index)][None], shifted[index, :-1]], axis=0)
            )
        else:
            pieces.append(
                jnp.concatenate([shifted[index, 1:], le_bot[falling.index(index)][None]], axis=0)
            )
    return jnp.stack(pieces)


def stream_across(post):
    depth_z = post.shape[2]
    width_x = post.shape[3]
    padded = extended(post, (("gx", 3), ("gz", 2)), 1)
    pieces = []
    for index in range(19):
        start_z = 1 - int(velocities[index, 2])
        start_x = 1 - int(velocities[index, 0])
        pieces.append(padded[index, :, start_z : start_z + depth_z, start_x : start_x + width_x])
    return jnp.stack(pieces)


def displaced_windows(planes, whole):
    width_x = planes.shape[3]
    count = lax.axis_size("gx")
    total = count * width_x
    offset_top = whole % total
    offset_bot = (total - whole - 1) % total
    full = lax.all_gather(planes, "gx", axis=3, tiled=True)
    doubled = jnp.concatenate([full, full[:, :, :, : width_x + 1]], axis=3)
    anchor = lax.axis_index("gx") * width_x
    start_top = (anchor + offset_top) % total
    start_bot = (anchor + offset_bot) % total
    win_top = lax.dynamic_slice_in_dim(doubled[0], start_top, width_x + 1, 2)
    win_bot = lax.dynamic_slice_in_dim(doubled[1], start_bot, width_x + 1, 2)
    return (win_top, win_bot)


def local(pop_ratio, solid_blocks, shift_whole, shift_frac):
    popul = pop_ratio * column(lattice_weights)
    solid = expand(solid_blocks)
    width_x = popul.shape[3]
    planes_y = popul.shape[1]
    accumulated = jnp.zeros((2,) + popul.shape[1:], jnp.float32)
    top_fix = plane_column(6.0 * lattice_weights[rising] * velocities[rising, 0] * wall_speed)
    bot_fix = plane_column(6.0 * lattice_weights[falling] * velocities[falling, 0] * wall_speed)
    for step in range(STEPS):
        post, fields = collide(popul, solid)
        accumulated = accumulated + fields
        shifted = stream_across(post)
        whole = shift_whole[step]
        weight = shift_frac[step].astype(jnp.float32) / fraction_unit
        planes = jnp.stack([shifted[np.array(rising), planes_y - 1], shifted[np.array(falling), 0]])
        win_top, win_bot = displaced_windows(planes, whole)
        le_top = (1.0 - weight) * win_top[:, :, :width_x] + weight * win_top[:, :, 1:] - top_fix
        le_bot = (1.0 - weight) * win_bot[:, :, 1:] + weight * win_bot[:, :, :width_x] + bot_fix
        popul = assemble(shifted, le_top, le_bot)
    profiles = lax.psum(jnp.sum(accumulated, axis=3), "gx")
    return (popul, accumulated, profiles)


def solution(mesh):
    return jax.shard_map(
        local,
        mesh=mesh,
        in_specs=(P(None, None, "gz", "gx"), P(None, "gz", "gx"), P(), P()),
        out_specs=(P(None, None, "gz", "gx"), P(None, None, "gz", "gx"), P(None, None, "gz")),
        check_vma=False,
    )
```

profile of v0, /device:TPU:0, one launch (start us, length us, event | category | flops | bytes accessed | tf_op | source)
XLA Modules:
  0.0 189.6 jit_solution(16554818729477392936)
XLA Ops:
  0.7 0.8 pad_clamp_fusion
  1.5 1.9 %multiply_reduce_fusion.6 = (f32[16,8,128]{2,1,0:T(8,128)S(1)}, f32[16,8,128]{2,1,0:T(8,128)S(1)}, f32[16,8,128]{2,1,0:T(8,128)S(1)}, f32[16,8,128]{2,1,0:T(8,128)S(1)}) fusion(f32[19]{0:T(128)} %constant.136, f32[19,16,8,128]{3,2,1,0:T(8,128)} %param.36, f32[19]{0:T(128)} %constant.134, f32[19]{0:T(128)} %constant.137, f32[19]{0:T(128)} %constant.138), kind=kLoop, calls=%fused_computation.42 | loop fusion | flops 2424832 | bytes 1507632 | tf_op jit(solution)/shard_map/reduce_sum | solution.py:133
  4.0 2.2 %fusion.17 = (f32[19,16,8,128]{3,2,1,0:T(8,128)S(1)}, f32[19,16,8,128]{3,2,1,0:T(8,128)}) fusion(f32[16,8,128]{2,1,0:T(8,128)S(1)} %get-tuple-element.47, f32[16,8,128]{2,1,0:T(8,128)S(1)} %get-tuple-element.50, f32[19]{0:T(128)S(1)} %copy-done.68, f32[16,8,128]{2,1,0:T(8,128)S(1)} %get-tuple-element.49, f32[19]{0:T(128)S(1)} %copy-done.65, ...), kind=kLoop, calls=%fused_computation.25 | loop fusion | flops 4669440 | bytes 4063536 | tf_op jit(solution)/shard_map/sub | solution.py:149
  6.4 0.9 copy-done.8
  7.3 0.9 copy.52
  8.2 1.4 fusion.92
  9.6 1.4 copy.53
  11.3 1.8 gt.9
  13.1 1.7 gather_fusion
  14.8 1.9 fusion.25
  16.6 1.5 fusion.85
  18.1 2.2 %copy.39 = f32[19,16,8,1]{0,2,3,1:T(8,128)S(1)} copy(f32[19,16,8,1]{3,2,1,0:T(8,128)} %get-tuple-element.90) | data formatting | bytes 19456 | tf_op jit(solution)/shard_map/slice | solution.py:72
  20.3 3.0 %collective-permute-start = (f32[19,16,8,1]{0,2,3,1:T(8,128)S(1)}, f32[19,16,8,1]{0,2,3,1:T(8,128)S(1)}, u32[]{:S(2)}, u32[]{:S(2)}) collective-permute-start(f32[19,16,8,1]{0,2,3,1:T(8,128)S(1)} %copy.39), channel_id=1, source_target_pairs={{0,8},{8,16},{16,24},{24,0},{1,9},{9,17},{17,25},{25,1},{2,10},{10... | collective-permute-start | bytes 29192 | tf_op jit(solution)/shard_map/ppermute | solution.py:74
  23.3 1.6 copy.41
  24.9 1.0 collective-permute-start.1
  33.8 2.3 %sub.117 = f32[1,16,8,128]{3,2,1,0:T(8,128)} reshape(f32[4,4,2,4,32,4]{5,4,3,2,1,0:T(8,128)S(1)} %broadcast_in_dim.49) | data formatting | bytes 131072 | tf_op jit(solution)/shard_map/sub | solution.py:154
  36.7 1.3 copy.40
  38.0 3.1 %copy.42 = f32[19,16,8,1]{3,2,1,0:T(8,128)} copy(f32[19,16,8,1]{0,2,3,1:T(8,128)} %collective-permute-done.1) | data formatting | bytes 19456 | tf_op jit(solution)/shard_map/ppermute | solution.py:75
  41.1 1.8 fusion.50
  42.8 2.0 %pad_maximum_fusion.3 = (f32[19,16,1,130]{3,2,1,0:T(1,128)S(1)}, f32[19,16,1,130]{3,2,1,0:T(1,128)S(1)}) fusion(f32[19,16,8,1]{3,2,1,0:T(8,128)S(1)} %copy-done.2, f32[19,16,8,128]{3,2,1,0:T(8,128)S(1)} %fusion.25, f32[19,16,8,1]{3,2,1,0:T(8,128)S(1)} %copy.40), kind=kLoop, calls=%fused_computation.59 | loop fusion | flops 158080 | bytes 1580800 | tf_op jit(solution)/shard_map/concatenate | solution.py:76
  44.8 0.7 constant_dynamic-update-slice_fusion.34
  45.6 0.8 constant_dynamic-update-slice_fusion.33
  46.3 2.5 %copy.71 = f32[19,16,8,128]{3,2,1,0:T(8,128)} copy(f32[19,16,8,128]{3,2,1,0:T(8,128)} %get-tuple-element.43) | data formatting | bytes 2490368
  48.8 3.5 %collective-permute-start.3 = (f32[19,16,1,130]{3,2,1,0:T(1,128)S(1)}, f32[19,16,1,130]{3,2,1,0:T(1,128)S(1)}, u32[]{:S(2)}, u32[]{:S(2)}) collective-permute-start(f32[19,16,1,130]{3,2,1,0:T(1,128)S(1)} %get-tuple-element.65), channel_id=1, source_target_pairs={{1,0},{2,1},{3,2},{4,3},{5,4},{6,5},{7,6},{0,7},{9,8},{10,9},{11,1... | collective-permute-start | bytes 474248 | tf_op jit(solution)/shard_map/ppermute | solution.py:75
  53.0 4.7 %collective-permute-done.2 = f32[19,16,1,130]{3,2,1,0:T(1,128)S(1)} collective-permute-done((f32[19,16,1,130]{3,2,1,0:T(1,128)S(1)}, f32[19,16,1,130]{3,2,1,0:T(1,128)S(1)}, u32[]{:S(2)}, u32[]{:S(2)}) %collective-permute-start.2) | collective-permute-done | bytes 158112 | tf_op jit(solution)/shard_map/ppermute | solution.py:74
  58.4 0.7 constant_dynamic-update-slice_fusion.11
  62.8 0.8 constant_dynamic-update-slice_fusion.5
  64.3 0.8 constant_dynamic-update-slice_fusion.3
  65.8 0.8 constant_dynamic-update-slice_fusion.1
  67.3 1.9 gather_fusion.2
  69.2 2.5 %gather_fusion.1 = f32[5,8,128]{2,1,0:T(8,128)} fusion(f32[19,16,8,128]{3,2,1,0:T(8,128)} %constant_dynamic-update-slice_fusion, s32[5]{0:T(128)S(1)} %copy-done.47), kind=kCustom, calls=%fused_computation.1 | custom fusion | bytes 41000 | tf_op jit(solution)/shard_map/gather | solution.py:220
  71.7 0.8 pad_maximum_fusion.48
  72.5 10.9 %all_gather.6 = f32[2,5,8,512]{3,2,1,0:T(8,128)S(1)} all-gather(f32[2,5,8,128]{3,2,1,0:T(8,128)S(1)} %pad_maximum_fusion.48), channel_id=1, replica_groups=mesh['gx'=4,'gz'=8] {'gx'}, dimensions={3}, use_global_device_ids=true | all-gather | bytes 204800 | tf_op jit(solution)/shard_map/all_gather | solution.py:196
  85.6 1.1 copy-done.4
  87.0 1.0 copy-done.5
  88.0 1.0 multiply_reduce_fusion.1
  89.1 2.2 %gather_fusion.3 = f32[19,16,8,128]{3,2,1,0:T(8,128)S(1)} fusion(f32[19,16,8,128]{3,2,1,0:T(8,128)} %copy-done.5, s32[1024]{0:T(1024)} %copy-done.71), kind=kCustom, calls=%fused_computation.3 | custom fusion | bytes 2490444 | tf_op jit(solution)/shard_map/gather | solution.py:153
  92.1 1.4 pad_maximum_fusion.23
  93.5 1.3 pad_maximum_fusion.25
  96.2 0.8 fusion.69
  97.7 6.3 %stack.178 = f32[19,16384]{1,0:T(8,128)} concatenate(f32[1,16384]{1,0:T(1,128)} %bitcast.276, f32[1,16384]{1,0:T(1,128)} %bitcast.272, f32[1,16384]{1,0:T(1,128)} %bitcast.273, f32[1,16384]{1,0:T(1,128)} %bitcast.277, f32[1,16384]{1,0:T(1,128)} %bitcast.279, f32[1,16384]{1,0:T(1,128)S(1)} %bitcast.264, f32[1,16384]{1,0:T(1,128)S(1)} %bitcast.265, f32[1,16384]{1,0:T(1,128)} %bitcast.278, ...), dimensions={0} | concatenate | bytes 2490368 | tf_op jit(solution)/shard_map/stack | solution.py:175
  104.1 3.5 %fusion.4 = f32[19,16384]{1,0:T(8,128)S(1)} fusion(f32[19,19]{1,0:T(8,128)S(1)} %copy-done.59, f32[19,16384]{1,0:T(8,128)} %stack.178, f32[16384]{0:T(1024)S(1)} %bitcast.274, f32[16384]{0:T(1024)S(1)} %get-tuple-element.93, f32[19]{0:T(128)S(1)} %copy-done.70, f32[16384]{0:T(1024)S(1)} %get-tuple-element.96, f32[19]{0:T(128)S(1)} %copy-done.67, ...), kind=kOutput, calls=%fused_computation.13 | convolution fusion | flops 75333632 | bytes 2819796 | tf_op jit(solution)/shard_map/dot_general | solution.py:150
  107.9 1.0 copy-done.6
  109.2 1.3 fusion.23
  110.5 1.5 fusion.83
  112.0 2.2 %copy.47 = f32[19,16,8,1]{0,2,3,1:T(8,128)S(1)} copy(f32[19,16,8,1]{3,2,1,0:T(8,128)} %get-tuple-element.82) | data formatting | bytes 19456 | tf_op jit(solution)/shard_map/slice | solution.py:73
  114.2 1.5 collective-permute-start.5
  115.7 1.0 copy.45
  117.9 16.0 %psum.7 = f32[2,16,8]{2,1,0:T(8,128)S(1)} all-reduce(f32[2,16,8]{2,1,0:T(8,128)S(1)} %get-tuple-element.15), channel_id=1, replica_groups=mesh['gx'=4,'gz'=8] {'gx'}, use_global_device_ids=true, to_apply=%region_10.11 | all-reduce | flops 256 | bytes 2048 | tf_op jit(solution)/shard_map/psum | solution.py:225
  134.6 1.3 copy.48
  135.9 2.2 %copy.46 = f32[19,16,8,1]{3,2,1,0:T(8,128)} copy(f32[19,16,8,1]{0,2,3,1:T(8,128)S(1)} %collective-permute-done.4) | data formatting | bytes 19456 | tf_op jit(solution)/shard_map/ppermute | solution.py:74
  138.1 1.6 pad_maximum_fusion.12
  139.7 0.8 fusion.46
  140.5 2.0 %pad_maximum_fusion = (f32[19,16,1,130]{3,2,1,0:T(1,128)S(1)}, f32[19,16,1,130]{3,2,1,0:T(1,128)S(1)}) fusion(f32[19,16,8,1]{3,2,1,0:T(8,128)S(1)} %copy.48, f32[19,16,8,128]{3,2,1,0:T(8,128)S(1)} %get-tuple-element.75, f32[19,16,8,1]{3,2,1,0:T(8,128)S(1)} %copy-done), kind=kLoop, calls=%fused_computation.56 | loop fusion | flops 158080 | bytes 1580800 | tf_op jit(solution)/shard_map/concatenate | solution.py:76
  143.8 2.4 %copy.103 = f32[19,16,8,128]{3,2,1,0:T(8,128)} copy(f32[19,16,8,128]{3,2,1,0:T(8,128)} %constant_dynamic-update-slice_fusion.69) | data formatting | bytes 2490368
  146.2 3.5 %collective-permute-start.7 = (f32[19,16,1,130]{3,2,1,0:T(1,128)S(1)}, f32[19,16,1,130]{3,2,1,0:T(1,128)S(1)}, u32[]{:S(2)}, u32[]{:S(2)}) collective-permute-start(f32[19,16,1,130]{3,2,1,0:T(1,128)S(1)} %get-tuple-element.61), channel_id=1, source_target_pairs={{1,0},{2,1},{3,2},{4,3},{5,4},{6,5},{7,6},{0,7},{9,8},{10,9},{11,1... | collective-permute-start | bytes 474248 | tf_op jit(solution)/shard_map/ppermute | solution.py:75
  150.4 5.4 %collective-permute-done.6 = f32[19,16,1,130]{3,2,1,0:T(1,128)S(1)} collective-permute-done((f32[19,16,1,130]{3,2,1,0:T(1,128)S(1)}, f32[19,16,1,130]{3,2,1,0:T(1,128)S(1)}, u32[]{:S(2)}, u32[]{:S(2)}) %collective-permute-start.6) | collective-permute-done | bytes 158112 | tf_op jit(solution)/shard_map/ppermute | solution.py:74
  160.8 0.7 constant_dynamic-update-slice_fusion.41
  162.3 0.8 constant_dynamic-update-slice_fusion.39
  163.7 0.8 constant_dynamic-update-slice_fusion.37
  165.3 1.9 gather_fusion.5
  167.1 2.5 %gather_fusion.4 = f32[5,8,128]{2,1,0:T(8,128)} fusion(f32[19,16,8,128]{3,2,1,0:T(8,128)} %constant_dynamic-update-slice_fusion.36, s32[5]{0:T(128)S(1)} %copy-done.47), kind=kCustom, calls=%fused_computation.4 | custom fusion | bytes 41000 | tf_op jit(solution)/shard_map/gather | solution.py:220
  169.6 0.8 pad_maximum_fusion.49
  170.4 8.3 %all_gather.7 = f32[2,5,8,512]{3,2,1,0:T(8,128)S(1)} all-gather(f32[2,5,8,128]{3,2,1,0:T(8,128)S(1)} %pad_maximum_fusion.49), channel_id=1, replica_groups=mesh['gx'=4,'gz'=8] {'gx'}, dimensions={3}, use_global_device_ids=true | all-gather | bytes 204800 | tf_op jit(solution)/shard_map/all_gather | solution.py:196
  (253 shorter events, 37.7 us)
Async XLA Ops:
  0.6 3.4 %copy-start.60 = (f32[19]{0:T(128)S(1)}, f32[19]{0:T(128)}, u32[]{:S(2)}) copy-start(f32[19]{0:T(128)} %constant.136) | copy-start | bytes 232
  0.6 3.4 %copy-start.63 = (f32[19]{0:T(128)S(1)}, f32[19]{0:T(128)}, u32[]{:S(2)}) copy-start(f32[19]{0:T(128)} %constant.134) | copy-start | bytes 232
  0.7 3.4 %copy-start.65 = (f32[19]{0:T(128)S(1)}, f32[19]{0:T(128)}, u32[]{:S(2)}) copy-start(f32[19]{0:T(128)} %constant.137) | copy-start | bytes 232
  0.7 3.4 %copy-start.68 = (f32[19]{0:T(128)S(1)}, f32[19]{0:T(128)}, u32[]{:S(2)}) copy-start(f32[19]{0:T(128)} %constant.138) | copy-start | bytes 232
  0.7 3.3 %copy-start.7 = (f32[19,16,8,128]{3,2,1,0:T(8,128)S(1)}, f32[19,16,8,128]{3,2,1,0:T(8,128)}, u32[]{:S(2)}) copy-start(f32[19,16,8,128]{3,2,1,0:T(8,128)} %param.36) | copy-start | bytes 3735556
  1.5 11.6 %copy-start.71 = (s32[1024]{0:T(1024)}, s32[1024]{0:T(1024)S(1)}, u32[]{:S(2)}) copy-start(s32[1024]{0:T(1024)S(1)} %pad_clamp_fusion) | copy-start | bytes 12292
  9.6 3.5 %copy-start.10 = (f32[19,16,8,128]{3,2,1,0:T(8,128)S(1)}, f32[19,16,8,128]{3,2,1,0:T(8,128)}, u32[]{:S(2)}) copy-start(f32[19,16,8,128]{3,2,1,0:T(8,128)} %get-tuple-element.74) | copy-start | bytes 3735556
  18.1 8.4 %copy-start.75 = (s32[2]{0:T(128)S(1)}, s32[2]{0:T(128)}, u32[]{:S(2)}) copy-start(s32[2]{0:T(128)} %param.38) | copy-start | bytes 28
  18.1 9.0 %copy-start.76 = (s32[2]{0:T(128)S(1)}, s32[2]{0:T(128)}, u32[]{:S(2)}) copy-start(s32[2]{0:T(128)} %param.39) | copy-start | bytes 28
  20.3 16.4 %collective-permute-start = (f32[19,16,8,1]{0,2,3,1:T(8,128)S(1)}, f32[19,16,8,1]{0,2,3,1:T(8,128)S(1)}, u32[]{:S(2)}, u32[]{:S(2)}) collective-permute-start(f32[19,16,8,1]{0,2,3,1:T(8,128)S(1)} %copy.39), channel_id=1, source_target_pairs={{0,8},{8,16},{16,24},{24,0},{1,9},{9,17},{17,25},{25,1},{2,10},{10... | collective-permute-start | bytes 29192 | tf_op jit(solution)/shard_map/ppermute | solution.py:74
  24.9 13.1 %collective-permute-start.1 = (f32[19,16,8,1]{0,2,3,1:T(8,128)}, f32[19,16,8,1]{0,2,3,1:T(8,128)}, u32[]{:S(2)}, u32[]{:S(2)}) collective-permute-start(f32[19,16,8,1]{0,2,3,1:T(8,128)} %copy.41), channel_id=1, source_target_pairs={{8,0},{16,8},{24,16},{0,24},{9,1},{17,9},{25,17},{1,25},{10,2},{18... | collective-permute-start | bytes 29192 | tf_op jit(solution)/shard_map/ppermute | solution.py:75
  41.1 1.8 copy-start.2
  48.8 8.9 %collective-permute-start.2 = (f32[19,16,1,130]{3,2,1,0:T(1,128)S(1)}, f32[19,16,1,130]{3,2,1,0:T(1,128)S(1)}, u32[]{:S(2)}, u32[]{:S(2)}) collective-permute-start(f32[19,16,1,130]{3,2,1,0:T(1,128)S(1)} %get-tuple-element.66), channel_id=1, source_target_pairs={{0,1},{1,2},{2,3},{3,4},{4,5},{5,6},{6,7},{7,0},{8,9},{9,10},{10,1... | collective-permute-start | bytes 474248 | tf_op jit(solution)/shard_map/ppermute | solution.py:74
  48.8 9.6 %collective-permute-start.3 = (f32[19,16,1,130]{3,2,1,0:T(1,128)S(1)}, f32[19,16,1,130]{3,2,1,0:T(1,128)S(1)}, u32[]{:S(2)}, u32[]{:S(2)}) collective-permute-start(f32[19,16,1,130]{3,2,1,0:T(1,128)S(1)} %get-tuple-element.65), channel_id=1, source_target_pairs={{1,0},{2,1},{3,2},{4,3},{5,4},{6,5},{7,6},{0,7},{9,8},{10,9},{11,1... | collective-permute-start | bytes 474248 | tf_op jit(solution)/shard_map/ppermute | solution.py:75
  66.6 2.6 %copy-start.47 = (s32[5]{0:T(128)S(1)}, s32[5]{0:T(128)}, u32[]{:S(2)}) copy-start(s32[5]{0:T(128)} %constant.208) | copy-start | bytes 64
  67.3 17.1 %copy-start.72 = (f32[5]{0:T(128)S(1)}, f32[5]{0:T(128)}, u32[]{:S(2)}) copy-start(f32[5]{0:T(128)} %constant.144) | copy-start | bytes 64
  71.7 12.9 %copy-start.17 = (f32[15,8,128]{2,1,0:T(8,128)S(1)}, f32[15,8,128]{2,1,0:T(8,128)}, u32[]{:S(2)}) copy-start(f32[15,8,128]{2,1,0:T(8,128)} %get-tuple-element.88) | copy-start | bytes 184324
  71.7 13.5 %copy-start.3 = (f32[19,16,8,1]{3,2,1,0:T(8,128)S(1)}, f32[19,16,8,1]{3,2,1,0:T(8,128)}, u32[]{:S(2)}) copy-start(f32[19,16,8,1]{3,2,1,0:T(8,128)} %copy.42) | copy-start | bytes 29188
  84.6 2.2 %copy-start.53 = (f32[1,8,128]{2,1,0:T(8,128)}, f32[1,8,128]{2,1,0:T(8,128)S(1)}, u32[]{:S(2)}) copy-start(f32[1,8,128]{2,1,0:T(8,128)S(1)} %get-tuple-element.114) | copy-start | bytes 12292
  84.6 2.2 %copy-start.51 = (f32[1,8,128]{2,1,0:T(8,128)}, f32[1,8,128]{2,1,0:T(8,128)S(1)}, u32[]{:S(2)}) copy-start(f32[1,8,128]{2,1,0:T(8,128)S(1)} %get-tuple-element.113) | copy-start | bytes 12292
  84.6 2.3 %copy-start.49 = (f32[1,8,128]{2,1,0:T(8,128)}, f32[1,8,128]{2,1,0:T(8,128)S(1)}, u32[]{:S(2)}) copy-start(f32[1,8,128]{2,1,0:T(8,128)S(1)} %get-tuple-element.112) | copy-start | bytes 12292
  85.5 2.5 %copy-start.61 = (f32[19]{0:T(128)S(1)}, f32[19]{0:T(128)}, u32[]{:S(2)}) copy-start(f32[19]{0:T(128)} %constant.136) | copy-start | bytes 232
  85.5 2.5 %copy-start.66 = (f32[19]{0:T(128)S(1)}, f32[19]{0:T(128)}, u32[]{:S(2)}) copy-start(f32[19]{0:T(128)} %constant.137) | copy-start | bytes 232
  85.5 2.5 %copy-start.69 = (f32[19]{0:T(128)S(1)}, f32[19]{0:T(128)}, u32[]{:S(2)}) copy-start(f32[19]{0:T(128)} %constant.138) | copy-start | bytes 232
  89.0 2.3 %copy-start.16 = (f32[15,8,128]{2,1,0:T(8,128)S(1)}, f32[15,8,128]{2,1,0:T(8,128)}, u32[]{:S(2)}) copy-start(f32[15,8,128]{2,1,0:T(8,128)} %get-tuple-element.87) | copy-start | bytes 184324
  89.0 2.3 %copy-start.18 = (f32[15,8,128]{2,1,0:T(8,128)S(1)}, f32[15,8,128]{2,1,0:T(8,128)}, u32[]{:S(2)}) copy-start(f32[15,8,128]{2,1,0:T(8,128)} %get-tuple-element.88) | copy-start | bytes 184324
  89.0 3.0 %copy-start.28 = (f32[15,8,128]{2,1,0:T(8,128)S(1)}, f32[15,8,128]{2,1,0:T(8,128)}, u32[]{:S(2)}) copy-start(f32[15,8,128]{2,1,0:T(8,128)} %copy-done.27) | copy-start | bytes 184324
  89.1 3.0 %copy-start.30 = (f32[15,8,128]{2,1,0:T(8,128)S(1)}, f32[15,8,128]{2,1,0:T(8,128)}, u32[]{:S(2)}) copy-start(f32[15,8,128]{2,1,0:T(8,128)} %copy-done.29) | copy-start | bytes 184324
  89.1 3.0 %copy-start.52 = (f32[1,8,128]{2,1,0:T(8,128)S(1)}, f32[1,8,128]{2,1,0:T(8,128)}, u32[]{:S(2)}) copy-start(f32[1,8,128]{2,1,0:T(8,128)} %copy-done.51) | copy-start | bytes 12292
  89.1 4.4 %copy-start.12 = (f32[15,8,128]{2,1,0:T(8,128)S(1)}, f32[15,8,128]{2,1,0:T(8,128)}, u32[]{:S(2)}) copy-start(f32[15,8,128]{2,1,0:T(8,128)} %get-tuple-element.71) | copy-start | bytes 184324
  89.1 4.4 %copy-start.14 = (f32[15,8,128]{2,1,0:T(8,128)S(1)}, f32[15,8,128]{2,1,0:T(8,128)}, u32[]{:S(2)}) copy-start(f32[15,8,128]{2,1,0:T(8,128)} %get-tuple-element.72) | copy-start | bytes 184324
  89.1 5.7 %copy-start.22 = (f32[15,8,128]{2,1,0:T(8,128)S(1)}, f32[15,8,128]{2,1,0:T(8,128)}, u32[]{:S(2)}) copy-start(f32[15,8,128]{2,1,0:T(8,128)} %copy-done.21) | copy-start | bytes 184324
  89.1 5.7 %copy-start.26 = (f32[15,8,128]{2,1,0:T(8,128)S(1)}, f32[15,8,128]{2,1,0:T(8,128)}, u32[]{:S(2)}) copy-start(f32[15,8,128]{2,1,0:T(8,128)} %copy-done.25) | copy-start | bytes 184324
  89.1 6.4 %copy-start.20 = (f32[15,8,128]{2,1,0:T(8,128)S(1)}, f32[15,8,128]{2,1,0:T(8,128)}, u32[]{:S(2)}) copy-start(f32[15,8,128]{2,1,0:T(8,128)} %copy-done.19) | copy-start | bytes 184324
  89.1 6.4 %copy-start.24 = (f32[15,8,128]{2,1,0:T(8,128)S(1)}, f32[15,8,128]{2,1,0:T(8,128)}, u32[]{:S(2)}) copy-start(f32[15,8,128]{2,1,0:T(8,128)} %copy-done.23) | copy-start | bytes 184324
  89.1 6.4 %copy-start.50 = (f32[1,8,128]{2,1,0:T(8,128)S(1)}, f32[1,8,128]{2,1,0:T(8,128)}, u32[]{:S(2)}) copy-start(f32[1,8,128]{2,1,0:T(8,128)} %copy-done.49) | copy-start | bytes 12292
  91.3 4.8 %copy-start.35 = (f32[16,8,128]{2,1,0:T(8,128)S(1)}, f32[16,8,128]{2,1,0:T(8,128)}, u32[]{:S(2)}) copy-start(f32[16,8,128]{2,1,0:T(8,128)} %get-tuple-element.12) | copy-start | bytes 196612
  91.3 4.8 %copy-start.38 = (f32[1,16,8,128]{3,2,1,0:T(8,128)S(1)}, f32[1,16,8,128]{3,2,1,0:T(8,128)}, u32[]{:S(2)}) copy-start(f32[1,16,8,128]{3,2,1,0:T(8,128)} %get-tuple-element.46) | copy-start | bytes 196612
  91.3 4.8 %copy-start.39 = (f32[1,16,8,128]{3,2,1,0:T(8,128)S(1)}, f32[1,16,8,128]{3,2,1,0:T(8,128)}, u32[]{:S(2)}) copy-start(f32[1,16,8,128]{3,2,1,0:T(8,128)} %get-tuple-element.44) | copy-start | bytes 196612
  91.4 4.8 %copy-start.54 = (f32[1,8,128]{2,1,0:T(8,128)S(1)}, f32[1,8,128]{2,1,0:T(8,128)}, u32[]{:S(2)}) copy-start(f32[1,8,128]{2,1,0:T(8,128)} %copy-done.53) | copy-start | bytes 12292
  91.4 4.8 %copy-start.56 = (f32[1,8,128]{2,1,0:T(8,128)S(1)}, f32[1,8,128]{2,1,0:T(8,128)}, u32[]{:S(2)}) copy-start(f32[1,8,128]{2,1,0:T(8,128)} %copy-done.55) | copy-start | bytes 12292
  92.0 5.5 %copy-start.33 = (f32[1,16,8,128]{3,2,1,0:T(8,128)S(1)}, f32[1,16,8,128]{3,2,1,0:T(8,128)}, u32[]{:S(2)}) copy-start(f32[1,16,8,128]{3,2,1,0:T(8,128)} %sub.117) | copy-start | bytes 196612
  92.1 5.5 %copy-start.37 = (f32[16,8,128]{2,1,0:T(8,128)S(1)}, f32[16,8,128]{2,1,0:T(8,128)}, u32[]{:S(2)}) copy-start(f32[16,8,128]{2,1,0:T(8,128)} %copy-done.36) | copy-start | bytes 196612
  92.1 5.5 %copy-start.41 = (f32[16,8,128]{2,1,0:T(8,128)S(1)}, f32[16,8,128]{2,1,0:T(8,128)}, u32[]{:S(2)}) copy-start(f32[16,8,128]{2,1,0:T(8,128)} %get-tuple-element.10) | copy-start | bytes 196612
  92.1 5.5 %copy-start.42 = (f32[16,8,128]{2,1,0:T(8,128)S(1)}, f32[16,8,128]{2,1,0:T(8,128)}, u32[]{:S(2)}) copy-start(f32[16,8,128]{2,1,0:T(8,128)} %get-tuple-element.11) | copy-start | bytes 196612
  97.6 6.4 %copy-start.32 = (f32[1,16,8,128]{3,2,1,0:T(8,128)S(1)}, f32[1,16,8,128]{3,2,1,0:T(8,128)}, u32[]{:S(2)}) copy-start(f32[1,16,8,128]{3,2,1,0:T(8,128)} %copy-done.31) | copy-start | bytes 196612
  97.6 6.4 %copy-start.59 = (f32[19,19]{1,0:T(8,128)S(1)}, f32[19,19]{1,0:T(8,128)}, u32[]{:S(2)}) copy-start(f32[19,19]{1,0:T(8,128)} %constant.119.clone) | copy-start | bytes 4336
  97.6 6.4 %copy-start.62 = (f32[19]{0:T(128)S(1)}, f32[19]{0:T(128)}, u32[]{:S(2)}) copy-start(f32[19]{0:T(128)} %constant.136) | copy-start | bytes 232
  97.6 6.4 %copy-start.64 = (f32[19]{0:T(128)S(1)}, f32[19]{0:T(128)}, u32[]{:S(2)}) copy-start(f32[19]{0:T(128)} %constant.134) | copy-start | bytes 232
  97.7 6.4 %copy-start.67 = (f32[19]{0:T(128)S(1)}, f32[19]{0:T(128)}, u32[]{:S(2)}) copy-start(f32[19]{0:T(128)} %constant.137) | copy-start | bytes 232
  97.7 6.4 %copy-start.70 = (f32[19]{0:T(128)S(1)}, f32[19]{0:T(128)}, u32[]{:S(2)}) copy-start(f32[19]{0:T(128)} %constant.138) | copy-start | bytes 232
  107.6 1.7 copy-start.9
  112.0 5.2 %copy-start.34 = (f32[1,16,8,128]{3,2,1,0:T(8,128)S(1)}, f32[1,16,8,128]{3,2,1,0:T(8,128)}, u32[]{:S(2)}) copy-start(f32[1,16,8,128]{3,2,1,0:T(8,128)} %sub.117) | copy-start | bytes 196612
  114.2 20.4 %collective-permute-start.5 = (f32[19,16,8,1]{0,2,3,1:T(8,128)S(1)}, f32[19,16,8,1]{0,2,3,1:T(8,128)S(1)}, u32[]{:S(2)}, u32[]{:S(2)}) collective-permute-start(f32[19,16,8,1]{0,2,3,1:T(8,128)S(1)} %copy.47), channel_id=1, source_target_pairs={{8,0},{16,8},{24,16},{0,24},{9,1},{17,9},{25,17},{1,25},{10,2},{18... | collective-permute-start | bytes 29192 | tf_op jit(solution)/shard_map/ppermute | solution.py:75
  116.7 19.2 %collective-permute-start.4 = (f32[19,16,8,1]{0,2,3,1:T(8,128)S(1)}, f32[19,16,8,1]{0,2,3,1:T(8,128)S(1)}, u32[]{:S(2)}, u32[]{:S(2)}) collective-permute-start(f32[19,16,8,1]{0,2,3,1:T(8,128)S(1)} %copy.45), channel_id=1, source_target_pairs={{0,8},{8,16},{16,24},{24,0},{1,9},{9,17},{17,25},{25,1},{2,10},{10... | collective-permute-start | bytes 29192 | tf_op jit(solution)/shard_map/ppermute | solution.py:74
  146.2 9.6 %collective-permute-start.6 = (f32[19,16,1,130]{3,2,1,0:T(1,128)S(1)}, f32[19,16,1,130]{3,2,1,0:T(1,128)S(1)}, u32[]{:S(2)}, u32[]{:S(2)}) collective-permute-start(f32[19,16,1,130]{3,2,1,0:T(1,128)S(1)} %get-tuple-element.62), channel_id=1, source_target_pairs={{0,1},{1,2},{2,3},{3,4},{4,5},{5,6},{6,7},{7,0},{8,9},{9,10},{10,1... | collective-permute-start | bytes 474248 | tf_op jit(solution)/shard_map/ppermute | solution.py:74
  146.2 10.3 %collective-permute-start.7 = (f32[19,16,1,130]{3,2,1,0:T(1,128)S(1)}, f32[19,16,1,130]{3,2,1,0:T(1,128)S(1)}, u32[]{:S(2)}, u32[]{:S(2)}) collective-permute-start(f32[19,16,1,130]{3,2,1,0:T(1,128)S(1)} %get-tuple-element.61), channel_id=1, source_target_pairs={{1,0},{2,1},{3,2},{4,3},{5,4},{6,5},{7,6},{0,7},{9,8},{10,9},{11,1... | collective-permute-start | bytes 474248 | tf_op jit(solution)/shard_map/ppermute | solution.py:75
  164.5 14.3 %copy-start.74 = (f32[5]{0:T(128)S(1)}, f32[5]{0:T(128)}, u32[]{:S(2)}) copy-start(f32[5]{0:T(128)} %constant.146) | copy-start | bytes 64
  165.3 13.8 %copy-start.73 = (f32[5]{0:T(128)S(1)}, f32[5]{0:T(128)}, u32[]{:S(2)}) copy-start(f32[5]{0:T(128)} %constant.144) | copy-start | bytes 64
  169.6 9.6 %copy-start.46 = (f32[15,8,128]{2,1,0:T(8,128)S(1)}, f32[15,8,128]{2,1,0:T(8,128)}, u32[]{:S(2)}) copy-start(f32[15,8,128]{2,1,0:T(8,128)} %get-tuple-element.78) | copy-start | bytes 184324
  169.6 10.2 %copy-start.1 = (f32[19,16,8,1]{3,2,1,0:T(8,128)S(1)}, f32[19,16,8,1]{3,2,1,0:T(8,128)}, u32[]{:S(2)}) copy-start(f32[19,16,8,1]{3,2,1,0:T(8,128)} %copy.46) | copy-start | bytes 29188
  179.8 2.1 %copy-start.45 = (f32[15,8,128]{2,1,0:T(8,128)S(1)}, f32[15,8,128]{2,1,0:T(8,128)}, u32[]{:S(2)}) copy-start(f32[15,8,128]{2,1,0:T(8,128)} %get-tuple-element.77) | copy-start | bytes 184324
  179.8 2.8 %copy-start.44 = (f32[15,8,128]{2,1,0:T(8,128)S(1)}, f32[15,8,128]{2,1,0:T(8,128)}, u32[]{:S(2)}) copy-start(f32[15,8,128]{2,1,0:T(8,128)} %get-tuple-element.69) | copy-start | bytes 184324
  179.8 4.0 %copy-start.43 = (f32[15,8,128]{2,1,0:T(8,128)S(1)}, f32[15,8,128]{2,1,0:T(8,128)}, u32[]{:S(2)}) copy-start(f32[15,8,128]{2,1,0:T(8,128)} %get-tuple-element.68) | copy-start | bytes 184324
  (22 other events, 28.3 us)
where the time goes:
time: 191 us; the launch traced here: 190 us
  local copies, waits for them, and re-layouts  63.7 us (33%)
  other arithmetic  54.5 us (29%)
  blocking collectives  35.1 us (18%)
  starting transfers between devices  13.1 us (7%)
  waiting for transfers between devices  10.1 us (5%)
  between operations  8.13 us (4%)
  matrix products  4.87 us (3%)
    unnamed x44, other arithmetic  25.5 us
    unnamed x179, local copies, waits for them, and re-layouts  20.6 us
    all_gather x2, blocking collectives, displaced_windows(): full = lax.all_gather(planes, 'gx', axis=3, tiled=True)  19.2 us
    psum x1, blocking collectives, local(): profiles = lax.psum(jnp.sum(accumulated, axis=3), 'gx')  16 us
    ppermute x4, waiting for transfers between devices, extended(): before = lax.ppermute(last, axis, up)  10.1 us
    ppermute x4, starting transfers between devices, extended(): after = lax.ppermute(initial, axis, down)  9.53 us
    slice x4, local copies, waits for them, and re-layouts, extended(): initial = lax.slice_in_dim(value, 0, width, axis=dim)  6.71 us
    another operation x1, local copies, waits for them, and re-layouts, assemble(): return jnp.stack(pieces)  6.33 us
  transfers between devices with their start and end apart: 8, of which 2 were waited for; matrix products, arithmetic and copies ran while one was open for 7% of the time, Pallas kernels for 0%

commit v1 on v0

v1 whole, which is shorter than its diff:
```python
import functools

import jax
import jax.numpy as jnp
import numpy as np
from jax import lax
from jax.experimental import pallas as pl
from jax.experimental.pallas import tpu as pltpu
from jax.sharding import PartitionSpec as P

BLOCK = 4
velocity_list = [
    (0, 0, 0),
    (1, 0, 0),
    (-1, 0, 0),
    (0, 1, 0),
    (0, -1, 0),
    (0, 0, 1),
    (0, 0, -1),
    (1, 1, 0),
    (-1, -1, 0),
    (1, -1, 0),
    (-1, 1, 0),
    (1, 0, 1),
    (-1, 0, -1),
    (1, 0, -1),
    (-1, 0, 1),
    (0, 1, 1),
    (0, -1, -1),
    (0, 1, -1),
    (0, -1, 1),
]
Q = len(velocity_list)
weights = [1.0 / 3.0] + [1.0 / 18.0] * 6 + [1.0 / 36.0] * 12
CX = [v[0] for v in velocity_list]
CY = [v[1] for v in velocity_list]
CZ = [v[2] for v in velocity_list]
opposite = [velocity_list.index((-x, -y, -z)) for x, y, z in velocity_list]
mirror = [velocity_list.index((x, y, -z)) for x, y, z in velocity_list]
rising = [i for i in range(Q) if CY[i] == 1]
falling = [i for i in range(Q) if CY[i] == -1]
eastward = [i for i in range(Q) if CX[i] == 1]
westward = [i for i in range(Q) if CX[i] == -1]
upward = [i for i in range(Q) if CZ[i] == 1]
level = [i for i in range(Q) if CZ[i] == 0]
near_list = level + upward
near_slot = {i: s for s, i in enumerate(near_list)}
far_slot = {i: len(near_list) + s for s, i in enumerate(upward)}
MASK_SLOT = Q
wall_speed = 0.08
visc_rate = 1.25
fraction_unit = 4096.0
relax_rates = [0.0, 1.19, 1.4, 0.0, 1.2, 0.0, 1.2, 0.0, 1.2, 1.25, 1.4, 1.25, 1.4]
relax_rates += [1.25, 1.25, 1.25, 1.98, 1.98, 1.98]


def row_norms():
    v = np.array(velocity_list, dtype=np.float64)
    x, y, z = v[:, 0], v[:, 1], v[:, 2]
    s = x * x + y * y + z * z
    rows = [
        np.ones(Q),
        19 * s - 30,
        (21 * s * s - 53 * s + 24) / 2,
        x,
        (5 * s - 9) * x,
        y,
        (5 * s - 9) * y,
        z,
        (5 * s - 9) * z,
        3 * x * x - s,
        (3 * s - 5) * (3 * x * x - s),
        y * y - z * z,
        (3 * s - 5) * (y * y - z * z),
        x * y,
        y * z,
        x * z,
        (y * y - z * z) * x,
        (z * z - x * x) * y,
        (x * x - y * y) * z,
    ]
    return [float(np.sum(row * row)) for row in rows]


RATE = [rate / norm for rate, norm in zip(relax_rates, row_norms())]


def collide(f, solid):
    sums = {i: f[i] + f[i + 1] for i in range(1, Q, 2)}
    difs = {i: f[i] - f[i + 1] for i in range(1, Q, 2)}
    p1, d1 = sums[7] + sums[9], sums[7] - sums[9]
    p2, d2 = sums[11] + sums[13], sums[11] - sums[13]
    p3, d3 = sums[15] + sums[17], sums[15] - sums[17]
    s23 = sums[3] + sums[5]
    axis = sums[1] + s23
    p12 = p1 + p2
    diag = p12 + p3
    rho = f[0] + axis + diag
    inverse = 1.0 / rho
    a, c = difs[7] + difs[9], difs[7] - difs[9]
    b, e = difs[11] + difs[13], difs[11] - difs[13]
    d, g = difs[15] + difs[17], difs[15] - difs[17]
    ab, cd, eg = a + b, c + d, e + g
    jx, jy, jz = difs[1] + ab, difs[3] + cd, difs[5] + eg
    ux, uy, uz = jx * inverse, jy * inverse, jz * inverse
    xx, yy, zz = jx * ux, jy * uy, jz * uz
    yz_sum, yz_dif = yy + zz, yy - zz
    square = xx + yz_sum

    even_e = RATE[1] * (8.0 * diag - 11.0 * axis - 30.0 * f[0] + 11.0 * rho - 19.0 * square)
    even_s = RATE[2] * (12.0 * f[0] - 4.0 * axis + diag - 3.0 * rho + 5.5 * square)
    axis_x, diag_x = 2.0 * sums[1] - s23, p12 - 2.0 * p3
    eq_x = 2.0 * xx - yz_sum
    even_x = RATE[9] * (axis_x + diag_x - eq_x)
    even_px = RATE[10] * (diag_x - 2.0 * axis_x + 0.5 * eq_x)
    axis_w, diag_w = sums[3] - sums[5], p1 - p2
    even_w = RATE[11] * (axis_w + diag_w - yz_dif)
    even_pw = RATE[12] * (diag_w - 2.0 * axis_w + 0.5 * yz_dif)
    moment_xy = d1 - jx * uy
    even_xy = RATE[13] * moment_xy
    even_yz = RATE[14] * (d3 - jy * uz)
    even_xz = RATE[15] * (d2 - jx * uz)
    flow_x = RATE[4] * (ab - 4.0 * difs[1] + (2.0 / 3.0) * jx)
    flow_y = RATE[6] * (cd - 4.0 * difs[3] + (2.0 / 3.0) * jy)
    flow_z = RATE[8] * (eg - 4.0 * difs[5] + (2.0 / 3.0) * jz)
    twist_x = RATE[16] * (a - b)
    twist_y = RATE[17] * (d - c)
    twist_z = RATE[18] * (e - g)

    base_axis = -11.0 * even_e - 4.0 * even_s
    base_diag = 8.0 * even_e + even_s
    lean = even_x - 2.0 * even_px
    tilt = even_w - 2.0 * even_pw
    side_x = even_x + even_px
    side_w = even_w + even_pw
    flat = base_diag + side_x
    diag_xy, diag_xz = flat + side_w, flat - side_w
    diag_yz = base_diag - 2.0 * side_x
    low = base_axis - lean
    even = {
        1: base_axis + 2.0 * lean,
        3: low + tilt,
        5: low - tilt,
        7: diag_xy + even_xy,
        9: diag_xy - even_xy,
        11: diag_xz + even_xz,
        13: diag_xz - even_xz,
        15: diag_yz + even_yz,
        17: diag_yz - even_yz,
    }
    x_up, x_down = flow_x + twist_x, flow_x - twist_x
    y_up, y_down = flow_y + twist_y, flow_y - twist_y
    z_up, z_down = flow_z + twist_z, flow_z - twist_z
    odd = {
        1: -4.0 * flow_x,
        3: -4.0 * flow_y,
        5: -4.0 * flow_z,
        7: x_up + y_down,
        9: x_up - y_down,
        11: x_down + z_up,
        13: x_down - z_up,
        15: y_up + z_down,
        17: y_up - z_down,
    }
    post = [None] * Q
    post[0] = jnp.where(solid, f[0], f[0] + 30.0 * even_e - 12.0 * even_s)
    for i in range(1, Q, 2):
        post[i] = jnp.where(solid, f[i + 1], f[i] - (even[i] + odd[i]))
        post[i + 1] = jnp.where(solid, f[i], f[i + 1] - (even[i] - odd[i]))
    return post, jx, moment_xy


class Sizes:
    def __init__(self, planes, depth, width, count):
        self.planes, self.depth, self.width, self.count = planes, depth, width, count
        self.deep, self.wide = depth // BLOCK, width // BLOCK
        assert count >= 4 and count & (count - 1) == 0
        assert len(eastward) * planes + 4 <= width and 2 * planes <= width

    def slots(self, delta):
        return (2 if delta == self.count // 2 else 1) * len(rising) + 1

    def tile(self, ref, i, y):
        return ref[i, pl.ds(y * self.depth, self.depth), :]

    def lanes(self):
        return lax.broadcasted_iota(jnp.int32, (self.depth, self.width), 1)

    def rows(self):
        return lax.broadcasted_iota(jnp.int32, (self.depth, self.width), 0)

    def spread(self, row):
        return jnp.broadcast_to(row, (self.depth, self.width))

    def solid_tile(self, mask_ref, y):
        base = y // BLOCK * self.deep
        out = self.spread(mask_ref[base : base + 1, :])
        rows = self.rows()
        for step in range(1, self.deep):
            line = self.spread(mask_ref[base + step : base + step + 1, :])
            out = jnp.where(rows >= step * BLOCK, line, out)
        return out


def roll(value, shift, axis=1):
    shift = shift % value.shape[axis]
    return pltpu.roll(value, shift, axis) if shift else value


def edge_columns(z):
    return [
        (7, z.planes - 1, True),
        (10, z.planes - 1, False),
        (9, 0, True),
        (8, 0, False),
    ]


def wall_columns(z, ref, lanes):
    out = jnp.zeros((z.depth, z.width), jnp.float32)
    start = len(eastward) * z.planes
    for k, (i, y, right) in enumerate(edge_columns(z)):
        at = start + k
        moved = roll(z.tile(ref, i, y), at - (z.width - 1 if right else 0))
        out = jnp.where(lanes == at, moved, out)
    return out


def pack_x(z, whole, ref, sends, extra=None):
    me = lax.axis_index("gx")
    lanes = z.lanes()
    right_edge = wall_columns(z, ref, lanes)
    left_edge = right_edge
    for j in range(len(eastward)):
        for y in range(z.planes):
            at = j * z.planes + y
            hit = lanes == at
            moved = roll(z.tile(ref, eastward[j], y), at - (z.width - 1))
            right_edge = jnp.where(hit, moved, right_edge)
            moved = roll(z.tile(ref, westward[j], y), at)
            left_edge = jnp.where(hit, moved, left_edge)
    far = lax.div(whole, z.width)
    for delta in range(1, z.count):
        send = sends[delta - 1]
        partner = jnp.bitwise_xor(me, delta)
        ahead = lax.rem(me - partner + z.count, z.count)
        at_top = (ahead == far) | (ahead == lax.rem(far + 1, z.count))
        for s in range(len(rising)):
            top = z.tile(ref, rising[s], z.planes - 1)
            bottom = z.tile(ref, falling[s], 0)
            if delta == z.count // 2:
                send[s] = top
                send[len(rising) + s] = bottom
            else:
                send[s] = jnp.where(at_top, top, bottom)
        to_right = partner == lax.rem(me + 1, z.count)
        slots = z.slots(delta)
        send[slots - 1] = jnp.where(to_right, right_edge, left_edge)
        if extra is not None:
            send[slots] = extra


def shift_xy(z, whole, part, ref, gets, out, tops, bottoms, edges):
    me = lax.axis_index("gx")
    lanes = z.lanes()
    last = z.width - 1
    for s in range(len(rising)):
        tops[me, s] = z.tile(ref, rising[s], z.planes - 1)
        bottoms[me, s] = z.tile(ref, falling[s], 0)
    edges[me] = wall_columns(z, ref, lanes)
    for delta in range(1, z.count):
        get = gets[delta - 1]
        partner = jnp.bitwise_xor(me, delta)
        for s in range(len(rising)):
            tops[partner, s] = get[s]
            second = len(rising) + s if delta == z.count // 2 else s
            bottoms[partner, s] = get[second]
        edges[partner] = get[z.slots(delta) - 1]

    left = edges[lax.rem(me + z.count - 1, z.count)]
    right = edges[lax.rem(me + 1, z.count)]

    def moved(i, y):
        value = z.tile(ref, i, y)
        if CX[i] == 1:
            at = eastward.index(i) * z.planes + y
            return jnp.where(lanes == 0, roll(left, -at), roll(value, 1))
        if CX[i] == -1:
            at = westward.index(i) * z.planes + y
            return jnp.where(lanes == last, roll(right, last - at), roll(value, -1))
        return value

    for i in range(Q):
        for y in range(z.planes):
            source = y - CY[i]
            if 0 <= source < z.planes:
                out[i, pl.ds(y * z.depth, z.depth), :] = moved(i, source)

    weight = part.astype(jnp.float32) / fraction_unit
    far = lax.div(whole, z.width)
    rest = lax.rem(whole, z.width)
    start = len(eastward) * z.planes
    columns = {i: start + k for k, (i, _, _) in enumerate(edge_columns(z))}

    def window(i, planes, s, block, offset):
        pair = []
        for step in range(2):
            here = lax.rem(block + step, z.count)
            value = planes[here, s]
            if CX[i] == 1:
                side = edges[lax.rem(here + z.count - 1, z.count)]
                value = jnp.where(lanes == 0, roll(side, -columns[i]), roll(value, 1))
            elif CX[i] == -1:
                side = edges[lax.rem(here + 1, z.count)]
                value = jnp.where(lanes == last, roll(side, last - columns[i]), roll(value, -1))
            pair.append(value)
        first = jnp.where(lanes >= offset, pair[0], pair[1])
        second = jnp.where(lanes > offset, pair[0], pair[1])
        first = pltpu.roll(first, lax.rem(z.width - offset, z.width), 1)
        second = pltpu.roll(second, last - offset, 1)
        return first, second

    for s, i in enumerate(rising):
        near, next_one = window(i, tops, s, lax.rem(me + far, z.count), rest)
        fix = 6.0 * weights[i] * CX[i] * wall_speed
        value = (1.0 - weight) * near + weight * next_one
        out[i, pl.ds(0, z.depth), :] = value - fix if CX[i] else value
    for s, i in enumerate(falling):
        block = lax.rem(me + 2 * z.count - far - 1, z.count)
        next_one, near = window(i, bottoms, s, block, last - rest)
        fix = 6.0 * weights[i] * CX[i] * wall_speed
        value = (1.0 - weight) * near + weight * next_one
        out[i, pl.ds((z.planes - 1) * z.depth, z.depth), :] = value + fix if CX[i] else value


def first_kernel(z, whole_ref, pop_ref, solid_ref, post_ref, acc_ref, mask_ref, *sends):
    grow = lax.broadcasted_iota(jnp.int32, (z.wide, z.width), 1) // BLOCK
    grow = grow == lax.broadcasted_iota(jnp.int32, (z.wide, z.width), 0)
    grow = grow.astype(jnp.float32)
    for k in range(solid_ref.shape[0]):
        flags = jnp.where(solid_ref[k] > 0, 1.0, 0.0)
        line = jnp.dot(flags, grow, preferred_element_type=jnp.float32)
        mask_ref[pl.ds(k * z.deep, z.deep), :] = line
    for y in range(z.planes):
        solid = z.solid_tile(mask_ref, y) > 0.5
        f = [z.tile(pop_ref, i, y) * np.float32(weights[i]) for i in range(Q)]
        post, jx, moment_xy = collide(f, solid)
        here = pl.ds(y * z.depth, z.depth)
        for i in range(Q):
            post_ref[i, here, :] = post[i]
        acc_ref[0, here, :] = jnp.where(solid, 0.0, jx)
        acc_ref[1, here, :] = jnp.where(solid, 0.0, -(1.0 - 0.5 * visc_rate) * moment_xy)
    pack_x(z, whole_ref[0], post_ref, sends)


def second_kernel(z, whole_ref, part_ref, post_ref, mask_ref, *refs):
    gets, (h_ref, inner_ref, outer_ref), scratch = refs[: z.count - 1], refs[z.count - 1 : z.count + 2], refs[z.count + 2 :]
    shift_xy(z, whole_ref[0], part_ref[0], post_ref, gets, h_ref, *scratch)
    even = lax.rem(lax.axis_index("gz"), 2) == 0

    def line(i, row):
        return h_ref[i, pl.ds(row, z.planes, stride=z.depth), :]

    def put(slot, up, down):
        inner_ref[slot] = jnp.where(even, up, down)
        outer_ref[slot] = jnp.where(even, down, up)

    for i in near_list:
        put(near_slot[i], line(i, z.depth - 1), line(mirror[i], 0))
    for i in upward:
        put(far_slot[i], line(i, z.depth - 2), line(mirror[i], 1))
    for k in range(z.planes // BLOCK):
        up = mask_ref[(k + 1) * z.deep - 1 : (k + 1) * z.deep, :]
        down = mask_ref[k * z.deep : k * z.deep + 1, :]
        shape = (BLOCK, z.width)
        here = pl.ds(k * BLOCK, BLOCK)
        inner_ref[MASK_SLOT, here, :] = jnp.broadcast_to(jnp.where(even, up, down), shape)
        outer_ref[MASK_SLOT, here, :] = jnp.broadcast_to(jnp.where(even, down, up), shape)


def third_kernel(z, whole_ref, h_ref, inner_ref, outer_ref, mask_ref, old_ref, *refs):
    (g_ref, acc_ref, part_ref), sends = refs[:3], refs[3 : 2 + z.count]
    sides, extra = refs[2 + z.count :]
    even = lax.rem(lax.axis_index("gz"), 2) == 0
    sides[jnp.where(even, 1, 0)] = inner_ref[...]
    sides[jnp.where(even, 0, 1)] = outer_ref[...]
    chunk = min(8, z.planes)
    for side in range(2):
        for start in range(0, z.planes, chunk):
            here = pl.ds(start, chunk)
            f = [None] * Q
            for i in range(Q):
                k = i if side == 0 else mirror[i]
                if CZ[k] == 0:
                    f[i] = sides[side, near_slot[k], here, :]
                elif CZ[k] == 1:
                    f[i] = sides[side, far_slot[k], here, :]
                else:
                    row = start * z.depth + (0 if side == 0 else z.depth - 1)
                    f[i] = h_ref[i, pl.ds(row, chunk, stride=z.depth), :]
            post, _, _ = collide(f, sides[side, MASK_SLOT, here, :] > 0.5)
            for s, i in enumerate(upward):
                extra[side, s, here, :] = post[i if side == 0 else mirror[i]]
    rows, lanes = z.rows(), z.lanes()

    def moved(i, y, value, table, slot):
        if CZ[i] == 1:
            line = z.spread(table[0, slot(i), pl.ds(y, 1), :])
            return jnp.where(rows == 0, line, roll(value, 1, 0))
        if CZ[i] == -1:
            line = z.spread(table[1, slot(mirror[i]), pl.ds(y, 1), :])
            return jnp.where(rows == z.depth - 1, line, roll(value, -1, 0))
        return value

    sums = jnp.zeros((z.depth, z.width), jnp.float32)
    for y in range(z.planes):
        solid = z.solid_tile(mask_ref, y) > 0.5
        f = [moved(i, y, z.tile(h_ref, i, y), sides, near_slot.get) for i in range(Q)]
        post, jx, moment_xy = collide(f, solid)
        here = pl.ds(y * z.depth, z.depth)
        for i in range(Q):
            g_ref[i, here, :] = moved(i, y, post[i], extra, upward.index)
        fields = [jx, -(1.0 - 0.5 * visc_rate) * moment_xy]
        for k in range(2):
            value = old_ref[k, here, :] + jnp.where(solid, 0.0, fields[k])
            acc_ref[k, here, :] = value
            total = z.spread(jnp.sum(value, axis=1, keepdims=True))
            sums = jnp.where(lanes == k * z.planes + y, total, sums)
    part_ref[...] = sums
    pack_x(z, whole_ref[1], g_ref, sends, sums)


def fourth_kernel(z, whole_ref, part_ref, g_ref, own_ref, *refs):
    gets, (out_ref, profile_ref), scratch = refs[: z.count - 1], refs[z.count - 1 : z.count + 1], refs[z.count + 1 :]
    shift_xy(z, whole_ref[1], part_ref[1], g_ref, gets, out_ref, *scratch)
    terms = [own_ref[...]] + [gets[d - 1][z.slots(d)] for d in range(1, z.count)]
    while len(terms) > 1:
        terms = [terms[k] + terms[k + 1] for k in range(0, len(terms), 2)]
    profile_ref[...] = terms[0].T[: profile_ref.shape[0], :]


def local(count, ranks, pop_ratio, solid_blocks, shift_whole, shift_frac):
    _, planes, depth, width = pop_ratio.shape
    z = Sizes(planes, depth, width, count)
    assert ranks % 2 == 0
    f32 = lambda *shape: jax.ShapeDtypeStruct(shape, jnp.float32)
    vmem = pl.BlockSpec(memory_space=pltpu.VMEM)
    smem = pl.BlockSpec(memory_space=pltpu.SMEM)
    cells = f32(Q, planes * depth, width)
    fields = f32(2, planes * depth, width)
    halo = f32(Q + 1, planes, width)
    shifts = [pltpu.VMEM((count, len(rising), depth, width), jnp.float32)] * 2
    shifts.append(pltpu.VMEM((count, depth, width), jnp.float32))

    def buffers(more):
        return [f32(z.slots(d) + more, depth, width) for d in range(1, count)]

    def call(body, ins, outs, scratch=()):
        return pl.pallas_call(
            functools.partial(body, z),
            out_shape=outs,
            in_specs=ins,
            out_specs=[vmem] * len(outs),
            scratch_shapes=list(scratch),
            name=body.__name__,
        )

    def swap_x(values):
        return [
            lax.ppermute(values[d - 1], "gx", [(i, i ^ d) for i in range(count)])
            for d in range(1, count)
        ]

    pairs = [(i, i ^ 1) for i in range(ranks)]
    across = [(i, (i - 1 if i % 2 == 0 else i + 1) % ranks) for i in range(ranks)]

    pop = pop_ratio.reshape(cells.shape)
    post, old, mask, *sends = call(
        first_kernel, [smem, vmem, vmem], [cells, fields, f32(planes // BLOCK * z.deep, width)] + buffers(0)
    )(shift_whole, pop, solid_blocks)
    gets = swap_x(sends)
    h, inner, outer = call(
        second_kernel, [smem, smem] + [vmem] * (1 + count), [cells, halo, halo], shifts
    )(shift_whole, shift_frac, post, mask, *gets)
    outer = lax.ppermute(outer, "gz", across)
    inner = lax.ppermute(inner, "gz", pairs)
    g, acc, own, *sends = call(
        third_kernel,
        [smem] + [vmem] * 5,
        [cells, fields, f32(depth, width)] + buffers(1),
        [
            pltpu.VMEM((2, Q + 1, planes, width), jnp.float32),
            pltpu.VMEM((2, len(upward), planes, width), jnp.float32),
        ],
    )(shift_whole, h, inner, outer, mask, old)
    gets = swap_x(sends)
    out, profile = call(
        fourth_kernel, [smem, smem] + [vmem] * (1 + count), [cells, f32(2 * planes, depth)], shifts
    )(shift_whole, shift_frac, g, own, *gets)
    return (
        out.reshape(pop_ratio.shape),
        acc.reshape(2, planes, depth, width),
        profile.reshape(2, planes, depth),
    )


def solution(mesh):
    return jax.shard_map(
        functools.partial(local, mesh.shape["gx"], mesh.shape["gz"]),
        mesh=mesh,
        in_specs=(P(None, None, "gz", "gx"), P(None, "gz", "gx"), P(), P()),
        out_specs=(P(None, None, "gz", "gx"), P(None, None, "gz", "gx"), P(None, None, "gz")),
        check_vma=False,
    )
```

time: 191 us -> 40.3 us (0.21)
  local copies, waits for them, and re-layouts: 63.7 us -> 3.3 us
  other arithmetic: 54.5 us -> 0 us
  blocking collectives: 35.1 us -> 0 us
  Pallas kernels: 0 us -> 12.6 us
  between operations: 8.13 us -> 0.66 us
  matrix products: 4.87 us -> 0 us
    unnamed x44 -> x0, other arithmetic: 25.5 us -> none
    all_gather x2 -> x0, blocking collectives: 19.2 us -> none  [displaced_windows(): full = lax.all_gather(planes, 'gx', axis=3, tiled=True)]
    unnamed x179 -> x17, local copies, waits for them, and re-layouts: 20.6 us -> 3.3 us
    psum x1 -> x0, blocking collectives: 16 us -> none  [local(): profiles = lax.psum(jnp.sum(accumulated, axis=3), 'gx')]
    pallas_call x0 -> x4, Pallas kernels: none -> 12.6 us  [the longest x1 3.47 us: local(): call(third_kernel, [smem] + [vmem] * 5, [cells, fields, f32(depth, width)...]
    gather x6 -> x0, local copies, waits for them, and re-layouts: 12.5 us -> none  [the longest x2 4.94 us: local(): shifted[np.array(rising), planes_y - 1]]
    slice x19 -> x0, local copies, waits for them, and re-layouts: 11.8 us -> none  [the longest x4 6.71 us: extended(): initial = lax.slice_in_dim(value, 0, width, axis=dim)]
    concatenate x7 -> x0, other arithmetic: 8.66 us -> none  [the longest x2 3.97 us: extended(): value = jnp.concatenate([before, value, after], axis=dim)]
  transfers between devices with their start and end apart: 8 -> 8, of which waited for: 2 -> 5; matrix products, arithmetic and copies ran while one was open for 7% -> 0% of each run, Pallas kernels for 0% -> 0%
where the time goes in v1:
time: 40.3 us; the launch traced here: 40 us
  Pallas kernels  12.6 us (31%)
  starting transfers between devices  11.7 us (29%)
  waiting for transfers between devices  11.6 us (29%)
  local copies, waits for them, and re-layouts  3.3 us (8%)
  between operations  0.66 us (2%)
    ppermute x6, starting transfers between devices, swap_x(): lax.ppermute(values[d - 1], 'gx', [(i, i ^ d) for i in range(count)])  8.02 us
    ppermute x6, waiting for transfers between devices, swap_x(): lax.ppermute(values[d - 1], 'gx', [(i, i ^ d) for i in range(count)])  7.42 us
    ppermute x1, waiting for transfers between devices, local(): outer = lax.ppermute(outer, 'gz', across)  4.22 us
    ppermute x1, starting transfers between devices, local(): outer = lax.ppermute(outer, 'gz', across)  3.71 us
    pallas_call x1, Pallas kernels, local(): call(third_kernel, [smem] + [vmem] * 5, [cells, fields, f32(depth, width)...  3.47 us
    unnamed x17, local copies, waits for them, and re-layouts  3.3 us
    pallas_call x1, Pallas kernels, local(): call(second_kernel, [smem, smem] + [vmem] * (1 + count), [cells, halo, ha...  3.12 us
    pallas_call x1, Pallas kernels, local(): call(first_kernel, [smem, vmem, vmem], [cells, fields, f32(planes // BLOC...  3.12 us
  transfers between devices with their start and end apart: 8, of which 5 were waited for; matrix products, arithmetic and copies ran while one was open for 0% of the time, Pallas kernels for 0%

profile of v1, /device:TPU:0, one launch (start us, length us, event | category | flops | bytes accessed | tf_op | source)
XLA Modules:
  0.0 40.0 jit_solution(9370816754488200896)
XLA Ops:
  0.6 3.1 %first_kernel.1 = (f32[19,128,128]{2,1,0:T(8,128)}, f32[2,128,128]{2,1,0:T(8,128)}, f32[8,128]{1,0:T(8,128)}, f32[6,8,128]{2,1,0:T(8,128)}, f32[11,8,128]{2,1,0:T(8,128)}, /*index=5*/f32[6,8,128]{2,1,0:T(8,128)}) custom-call(s32[2]{0:T(128)} %whole_ref.7, f32[19,128,128]{2,1,0:T(8,128)} %bitcast.4, s32[4,2,32]{2,1,0:T(2,128)} %solid_ref.1), custom_call_target="tpu_custom_call" | custom-call | tf_op jit(solution)/shard_map/first_kernel/pallas_call | solution.py:478
  3.8 3.0 %collective-permute-start.1 = (f32[11,8,128]{2,1,0:T(8,128)}, f32[11,8,128]{2,1,0:T(8,128)S(1)}, u32[]{:S(2)}, u32[]{:S(2)}) collective-permute-start(f32[11,8,128]{2,1,0:T(8,128)} %get-tuple-element.23), channel_id=1, source_target_pairs={{0,16},{8,24},{16,0},{24,8},{1,17},{9,25},{17,1},{25,9},{2,18},{10... | collective-permute-start | bytes 135176 | tf_op jit(solution)/shard_map/ppermute | solution.py:470
  6.7 1.5 %collective-permute-start = (f32[6,8,128]{2,1,0:T(8,128)}, f32[6,8,128]{2,1,0:T(8,128)S(1)}, u32[]{:S(2)}, u32[]{:S(2)}) collective-permute-start(f32[6,8,128]{2,1,0:T(8,128)} %get-tuple-element.22), channel_id=1, source_target_pairs={{0,8},{8,0},{16,24},{24,16},{1,9},{9,1},{17,25},{25,17},{2,10},{10... | collective-permute-start | bytes 73736 | tf_op jit(solution)/shard_map/ppermute | solution.py:470
  8.2 0.0 collective-permute-start.2
  8.3 2.5 %collective-permute-done.refs_0_ = f32[6,8,128]{2,1,0:T(8,128)S(1)} collective-permute-done((f32[6,8,128]{2,1,0:T(8,128)}, f32[6,8,128]{2,1,0:T(8,128)S(1)}, u32[]{:S(2)}, u32[]{:S(2)}) %collective-permute-start) | collective-permute-done | bytes 24608 | tf_op jit(solution)/shard_map/ppermute | solution.py:470
  10.8 0.0 copy-start.6
  10.8 2.4 %collective-permute-done.2.refs_2_ = f32[6,8,128]{2,1,0:T(8,128)S(1)} collective-permute-done((f32[6,8,128]{2,1,0:T(8,128)}, f32[6,8,128]{2,1,0:T(8,128)S(1)}, u32[]{:S(2)}, u32[]{:S(2)}) %collective-permute-start.2) | collective-permute-done | bytes 24608 | tf_op jit(solution)/shard_map/ppermute | solution.py:470
  13.2 0.0 copy-start.7
  13.2 0.0 collective-permute-done.1.refs_1_
  13.2 0.0 copy-start.3
  13.2 0.0 copy-done.6
  13.2 0.6 %copy-done.7 = f32[6,8,128]{2,1,0:T(8,128)} copy-done((f32[6,8,128]{2,1,0:T(8,128)}, f32[6,8,128]{2,1,0:T(8,128)S(1)}, u32[]{:S(2)}) %copy-start.7) | copy-done | bytes 24600
  13.8 0.0 copy-done.3
  13.8 3.1 %second_kernel.1 = (f32[19,128,128]{2,1,0:T(8,128)}, f32[20,16,128]{2,1,0:T(8,128)}, f32[20,16,128]{2,1,0:T(8,128)}) custom-call(s32[2]{0:T(128)} %whole_ref.7, s32[2]{0:T(128)} %part_ref.3, f32[19,128,128]{2,1,0:T(8,128)} %get-tuple-element.20.post_ref, f32[8,128]{1,0:T(8,128)} %get-tuple-element.21.mask_ref, f32[6,8,128]{2,1,0:T(8,128)} %copy-done.6, ...), custom_call_target="tpu_custom_call" | custom-call | tf_op jit(solution)/shard_map/second_kernel/pallas_call | solution.py:482
  16.9 0.0 collective-permute-start.3
  16.9 3.7 %collective-permute-start.4 = (f32[20,16,128]{2,1,0:T(8,128)}, f32[20,16,128]{2,1,0:T(8,128)S(1)}, u32[]{:S(2)}, u32[]{:S(2)}) collective-permute-start(f32[20,16,128]{2,1,0:T(8,128)} %get-tuple-element.27), channel_id=1, source_target_pairs={{0,7},{1,2},{2,1},{3,4},{4,3},{5,6},{6,5},{7,0},{8,15},{9,10},{10,... | collective-permute-start | bytes 491528 | tf_op jit(solution)/shard_map/ppermute | solution.py:485
  20.6 0.0 collective-permute-done.3.inner_ref
  20.6 0.0 copy-start
  20.6 4.2 %collective-permute-done.4.outer_ref = f32[20,16,128]{2,1,0:T(8,128)S(1)} collective-permute-done((f32[20,16,128]{2,1,0:T(8,128)}, f32[20,16,128]{2,1,0:T(8,128)S(1)}, u32[]{:S(2)}, u32[]{:S(2)}) %collective-permute-start.4) | collective-permute-done | bytes 163872 | tf_op jit(solution)/shard_map/ppermute | solution.py:485
  24.9 0.0 copy-start.1
  24.9 0.0 copy-done
  24.9 0.7 %copy-done.1 = f32[20,16,128]{2,1,0:T(8,128)} copy-done((f32[20,16,128]{2,1,0:T(8,128)}, f32[20,16,128]{2,1,0:T(8,128)S(1)}, u32[]{:S(2)}) %copy-start.1) | copy-done | bytes 163864
  25.5 3.5 %third_kernel.1 = (f32[19,128,128]{2,1,0:T(8,128)}, f32[2,128,128]{2,1,0:T(8,128)}, f32[8,128]{1,0:T(8,128)}, f32[7,8,128]{2,1,0:T(8,128)}, f32[12,8,128]{2,1,0:T(8,128)}, /*index=5*/f32[7,8,128]{2,1,0:T(8,128)}) custom-call(s32[2]{0:T(128)} %whole_ref.7, f32[19,128,128]{2,1,0:T(8,128)} %get-tuple-element.25.h_ref, f32[20,16,128]{2,1,0:T(8,128)} %copy-done, ...), custom_call_target="tpu_custom_call" | custom-call | tf_op jit(solution)/shard_map/third_kernel/pallas_call | solution.py:487
  29.0 0.5 %collective-permute-start.6 = (f32[12,8,128]{2,1,0:T(8,128)}, f32[12,8,128]{2,1,0:T(8,128)S(1)}, u32[]{:S(2)}, u32[]{:S(2)}) collective-permute-start(f32[12,8,128]{2,1,0:T(8,128)} %get-tuple-element.32), channel_id=1, source_target_pairs={{0,16},{8,24},{16,0},{24,8},{1,17},{9,25},{17,1},{25,9},{2,18},{10... | collective-permute-start | bytes 147464 | tf_op jit(solution)/shard_map/ppermute | solution.py:470
  29.5 0.5 %collective-permute-start.5 = (f32[7,8,128]{2,1,0:T(8,128)}, f32[7,8,128]{2,1,0:T(8,128)S(1)}, u32[]{:S(2)}, u32[]{:S(2)}) collective-permute-start(f32[7,8,128]{2,1,0:T(8,128)} %get-tuple-element.31), channel_id=1, source_target_pairs={{0,8},{8,0},{16,24},{24,16},{1,9},{9,1},{17,25},{25,17},{2,10},{10... | collective-permute-start | bytes 86024 | tf_op jit(solution)/shard_map/ppermute | solution.py:470
  30.0 2.4 %collective-permute-start.7 = (f32[7,8,128]{2,1,0:T(8,128)}, f32[7,8,128]{2,1,0:T(8,128)S(1)}, u32[]{:S(2)}, u32[]{:S(2)}) collective-permute-start(f32[7,8,128]{2,1,0:T(8,128)} %get-tuple-element.33), channel_id=1, source_target_pairs={{0,24},{8,16},{16,8},{24,0},{1,25},{9,17},{17,9},{25,1},{2,26},{10... | collective-permute-start | bytes 86024 | tf_op jit(solution)/shard_map/ppermute | solution.py:470
  32.5 1.1 %collective-permute-done.5.refs_0_ = f32[7,8,128]{2,1,0:T(8,128)S(1)} collective-permute-done((f32[7,8,128]{2,1,0:T(8,128)}, f32[7,8,128]{2,1,0:T(8,128)S(1)}, u32[]{:S(2)}, u32[]{:S(2)}) %collective-permute-start.5) | collective-permute-done | bytes 28704 | tf_op jit(solution)/shard_map/ppermute | solution.py:470
  33.6 0.0 copy-start.4
  33.6 1.4 %collective-permute-done.7.refs_2_ = f32[7,8,128]{2,1,0:T(8,128)S(1)} collective-permute-done((f32[7,8,128]{2,1,0:T(8,128)}, f32[7,8,128]{2,1,0:T(8,128)S(1)}, u32[]{:S(2)}, u32[]{:S(2)}) %collective-permute-start.7) | collective-permute-done | bytes 28704 | tf_op jit(solution)/shard_map/ppermute | solution.py:470
  35.0 0.0 copy-start.5
  35.0 0.0 collective-permute-done.6.refs_1_
  35.0 0.0 copy-start.2
  35.0 0.0 copy-done.4
  35.0 0.6 %copy-done.5 = f32[7,8,128]{2,1,0:T(8,128)} copy-done((f32[7,8,128]{2,1,0:T(8,128)}, f32[7,8,128]{2,1,0:T(8,128)S(1)}, u32[]{:S(2)}) %copy-start.5) | copy-done | bytes 28696
  35.6 0.0 copy-done.2
  35.7 2.9 %fourth_kernel.1 = (f32[19,128,128]{2,1,0:T(8,128)}, f32[32,8]{1,0:T(8,128)}) custom-call(s32[2]{0:T(128)} %whole_ref.7, s32[2]{0:T(128)} %part_ref.3, f32[19,128,128]{2,1,0:T(8,128)} %get-tuple-element.29.g_ref, f32[8,128]{1,0:T(8,128)} %get-tuple-element.30.own_ref, f32[7,8,128]{2,1,0:T(8,128)} %copy-done.4, f32[12,8,128]{2,1,0:T(8,128)} %copy-done.2, ...), custom_call_target="tpu_custom_call" | custom-call | tf_op jit(solution)/shard_map/fourth_kernel/pallas_call | solution.py:497
  38.6 1.4 %copy.7 = f32[2,16,8]{1,2,0:T(8,128)} copy(f32[2,16,8]{2,1,0:T(8,128)} %bitcast.5) | data formatting | bytes 2048
Async XLA Ops:
  3.8 9.4 %collective-permute-start.1 = (f32[11,8,128]{2,1,0:T(8,128)}, f32[11,8,128]{2,1,0:T(8,128)S(1)}, u32[]{:S(2)}, u32[]{:S(2)}) collective-permute-start(f32[11,8,128]{2,1,0:T(8,128)} %get-tuple-element.23), channel_id=1, source_target_pairs={{0,16},{8,24},{16,0},{24,8},{1,17},{9,25},{17,1},{25,9},{2,18},{10... | collective-permute-start | bytes 135176 | tf_op jit(solution)/shard_map/ppermute | solution.py:470
  6.7 4.0 %collective-permute-start = (f32[6,8,128]{2,1,0:T(8,128)}, f32[6,8,128]{2,1,0:T(8,128)S(1)}, u32[]{:S(2)}, u32[]{:S(2)}) collective-permute-start(f32[6,8,128]{2,1,0:T(8,128)} %get-tuple-element.22), channel_id=1, source_target_pairs={{0,8},{8,0},{16,24},{24,16},{1,9},{9,1},{17,25},{25,17},{2,10},{10... | collective-permute-start | bytes 73736 | tf_op jit(solution)/shard_map/ppermute | solution.py:470
  8.2 4.9 %collective-permute-start.2 = (f32[6,8,128]{2,1,0:T(8,128)}, f32[6,8,128]{2,1,0:T(8,128)S(1)}, u32[]{:S(2)}, u32[]{:S(2)}) collective-permute-start(f32[6,8,128]{2,1,0:T(8,128)} %get-tuple-element.24), channel_id=1, source_target_pairs={{0,24},{8,16},{16,8},{24,0},{1,25},{9,17},{17,9},{25,1},{2,26},{10... | collective-permute-start | bytes 73736 | tf_op jit(solution)/shard_map/ppermute | solution.py:470
  10.8 2.4 %copy-start.6 = (f32[6,8,128]{2,1,0:T(8,128)}, f32[6,8,128]{2,1,0:T(8,128)S(1)}, u32[]{:S(2)}) copy-start(f32[6,8,128]{2,1,0:T(8,128)S(1)} %collective-permute-done.refs_0_) | copy-start | bytes 73732
  13.2 0.6 %copy-start.7 = (f32[6,8,128]{2,1,0:T(8,128)}, f32[6,8,128]{2,1,0:T(8,128)S(1)}, u32[]{:S(2)}) copy-start(f32[6,8,128]{2,1,0:T(8,128)S(1)} %collective-permute-done.2.refs_2_) | copy-start | bytes 73732
  13.2 0.6 %copy-start.3 = (f32[11,8,128]{2,1,0:T(8,128)}, f32[11,8,128]{2,1,0:T(8,128)S(1)}, u32[]{:S(2)}) copy-start(f32[11,8,128]{2,1,0:T(8,128)S(1)} %collective-permute-done.1.refs_1_) | copy-start | bytes 135172
  16.9 3.7 %collective-permute-start.3 = (f32[20,16,128]{2,1,0:T(8,128)}, f32[20,16,128]{2,1,0:T(8,128)S(1)}, u32[]{:S(2)}, u32[]{:S(2)}) collective-permute-start(f32[20,16,128]{2,1,0:T(8,128)} %get-tuple-element.26), channel_id=1, source_target_pairs={{0,1},{1,0},{2,3},{3,2},{4,5},{5,4},{6,7},{7,6},{8,9},{9,8},{10,11... | collective-permute-start | bytes 491528 | tf_op jit(solution)/shard_map/ppermute | solution.py:486
  16.9 7.9 %collective-permute-start.4 = (f32[20,16,128]{2,1,0:T(8,128)}, f32[20,16,128]{2,1,0:T(8,128)S(1)}, u32[]{:S(2)}, u32[]{:S(2)}) collective-permute-start(f32[20,16,128]{2,1,0:T(8,128)} %get-tuple-element.27), channel_id=1, source_target_pairs={{0,7},{1,2},{2,1},{3,4},{4,3},{5,6},{6,5},{7,0},{8,15},{9,10},{10,... | collective-permute-start | bytes 491528 | tf_op jit(solution)/shard_map/ppermute | solution.py:485
  20.6 4.2 %copy-start = (f32[20,16,128]{2,1,0:T(8,128)}, f32[20,16,128]{2,1,0:T(8,128)S(1)}, u32[]{:S(2)}) copy-start(f32[20,16,128]{2,1,0:T(8,128)S(1)} %collective-permute-done.3.inner_ref) | copy-start | bytes 491524
  24.9 0.7 %copy-start.1 = (f32[20,16,128]{2,1,0:T(8,128)}, f32[20,16,128]{2,1,0:T(8,128)S(1)}, u32[]{:S(2)}) copy-start(f32[20,16,128]{2,1,0:T(8,128)S(1)} %collective-permute-done.4.outer_ref) | copy-start | bytes 491524
  29.0 6.0 %collective-permute-start.6 = (f32[12,8,128]{2,1,0:T(8,128)}, f32[12,8,128]{2,1,0:T(8,128)S(1)}, u32[]{:S(2)}, u32[]{:S(2)}) collective-permute-start(f32[12,8,128]{2,1,0:T(8,128)} %get-tuple-element.32), channel_id=1, source_target_pairs={{0,16},{8,24},{16,0},{24,8},{1,17},{9,25},{17,1},{25,9},{2,18},{10... | collective-permute-start | bytes 147464 | tf_op jit(solution)/shard_map/ppermute | solution.py:470
  29.5 4.1 %collective-permute-start.5 = (f32[7,8,128]{2,1,0:T(8,128)}, f32[7,8,128]{2,1,0:T(8,128)S(1)}, u32[]{:S(2)}, u32[]{:S(2)}) collective-permute-start(f32[7,8,128]{2,1,0:T(8,128)} %get-tuple-element.31), channel_id=1, source_target_pairs={{0,8},{8,0},{16,24},{24,16},{1,9},{9,1},{17,25},{25,17},{2,10},{10... | collective-permute-start | bytes 86024 | tf_op jit(solution)/shard_map/ppermute | solution.py:470
  30.0 5.0 %collective-permute-start.7 = (f32[7,8,128]{2,1,0:T(8,128)}, f32[7,8,128]{2,1,0:T(8,128)S(1)}, u32[]{:S(2)}, u32[]{:S(2)}) collective-permute-start(f32[7,8,128]{2,1,0:T(8,128)} %get-tuple-element.33), channel_id=1, source_target_pairs={{0,24},{8,16},{16,8},{24,0},{1,25},{9,17},{17,9},{25,1},{2,26},{10... | collective-permute-start | bytes 86024 | tf_op jit(solution)/shard_map/ppermute | solution.py:470
  33.6 1.4 %copy-start.4 = (f32[7,8,128]{2,1,0:T(8,128)}, f32[7,8,128]{2,1,0:T(8,128)S(1)}, u32[]{:S(2)}) copy-start(f32[7,8,128]{2,1,0:T(8,128)S(1)} %collective-permute-done.5.refs_0_) | copy-start | bytes 86020
  35.0 0.6 %copy-start.5 = (f32[7,8,128]{2,1,0:T(8,128)}, f32[7,8,128]{2,1,0:T(8,128)S(1)}, u32[]{:S(2)}) copy-start(f32[7,8,128]{2,1,0:T(8,128)S(1)} %collective-permute-done.7.refs_2_) | copy-start | bytes 86020
  35.0 0.6 %copy-start.2 = (f32[12,8,128]{2,1,0:T(8,128)}, f32[12,8,128]{2,1,0:T(8,128)S(1)}, u32[]{:S(2)}) copy-start(f32[12,8,128]{2,1,0:T(8,128)S(1)} %collective-permute-done.6.refs_1_) | copy-start | bytes 147460

commit v2 on v1

--- a/solution.py
+++ b/solution.py
@@ -39,6 +39,7 @@
 mirror = [velocity_list.index((x, y, -z)) for x, y, z in velocity_list]
 rising = [i for i in range(Q) if CY[i] == 1]
 falling = [i for i in range(Q) if CY[i] == -1]
+level_y = [i for i in range(Q) if CY[i] == 0]
 eastward = [i for i in range(Q) if CX[i] == 1]
 westward = [i for i in range(Q) if CX[i] == -1]
 upward = [i for i in range(Q) if CZ[i] == 1]
@@ -170,6 +171,9 @@
     return post, jx, moment_xy
 
 
+CHUNKS = 4
+
+
 class Sizes:
     def __init__(self, planes, depth, width, count):
         self.planes, self.depth, self.width, self.count = planes, depth, width, count
@@ -260,7 +264,7 @@
             send[slots] = extra
 
 
-def shift_xy(z, whole, part, ref, gets, out, tops, bottoms, edges):
+def shift_xy(z, step, scalars, ref, gets, out, tops, bottoms, edges, finish=None):
     me = lax.axis_index("gx")
     lanes = z.lanes()
     last = z.width - 1
@@ -290,12 +294,21 @@
             return jnp.where(lanes == last, roll(right, last - at), roll(value, -1))
         return value
 
-    for i in range(Q):
-        for y in range(z.planes):
-            source = y - CY[i]
-            if 0 <= source < z.planes:
-                out[i, pl.ds(y * z.depth, z.depth), :] = moved(i, source)
-
+    def interior(start, stop):
+        for i in range(Q):
+            for y in range(start, stop):
+                if 0 <= y - CY[i] < z.planes:
+                    out[i, pl.ds(y * z.depth, z.depth), :] = moved(i, y - CY[i])
+
+    group = z.planes // CHUNKS
+    for k in range(1, CHUNKS - 1):
+        interior(k * group, (k + 1) * group)
+        if finish is not None:
+            finish(k)
+    interior(0, group)
+    interior(z.planes - group, z.planes)
+    whole_ref, part_ref = scalars()
+    whole, part = whole_ref[step], part_ref[step]
     weight = part.astype(jnp.float32) / fraction_unit
     far = lax.div(whole, z.width)
     rest = lax.rem(whole, z.width)
@@ -325,15 +338,29 @@
         fix = 6.0 * weights[i] * CX[i] * wall_speed
         value = (1.0 - weight) * near + weight * next_one
         out[i, pl.ds(0, z.depth), :] = value - fix if CX[i] else value
+    if finish is not None:
+        finish(0)
     for s, i in enumerate(falling):
         block = lax.rem(me + 2 * z.count - far - 1, z.count)
         next_one, near = window(i, bottoms, s, block, last - rest)
         fix = 6.0 * weights[i] * CX[i] * wall_speed
         value = (1.0 - weight) * near + weight * next_one
         out[i, pl.ds((z.planes - 1) * z.depth, z.depth), :] = value + fix if CX[i] else value
-
-
-def first_kernel(z, whole_ref, pop_ref, solid_ref, post_ref, acc_ref, mask_ref, *sends):
+    if finish is not None:
+        finish(CHUNKS - 1)
+
+
+def first_kernel(z, whole_hbm, pop_hbm, solid_hbm, post_ref, acc_ref, mask_ref, *refs):
+    sends, (whole_ref, pop_ref, solid_ref, sems) = refs[: z.count - 1], refs[z.count - 1 :]
+    group = z.planes // CHUNKS * z.depth
+    copies = [pltpu.make_async_copy(solid_hbm, solid_ref, sems.at[CHUNKS])]
+    for k in range(CHUNKS):
+        part = (slice(None), pl.ds(k * group, group), slice(None))
+        copies.append(pltpu.make_async_copy(pop_hbm.at[part], pop_ref.at[part], sems.at[k]))
+    copies.append(pltpu.make_async_copy(whole_hbm, whole_ref, sems.at[CHUNKS + 1]))
+    for copy in copies:
+        copy.start()
+    copies[0].wait()
     grow = lax.broadcasted_iota(jnp.int32, (z.wide, z.width), 1) // BLOCK
     grow = grow == lax.broadcasted_iota(jnp.int32, (z.wide, z.width), 0)
     grow = grow.astype(jnp.float32)
@@ -342,6 +369,8 @@
         line = jnp.dot(flags, grow, preferred_element_type=jnp.float32)
         mask_ref[pl.ds(k * z.deep, z.deep), :] = line
     for y in range(z.planes):
+        if y % (z.planes // CHUNKS) == 0:
+            copies[1 + y // (z.planes // CHUNKS)].wait()
         solid = z.solid_tile(mask_ref, y) > 0.5
         f = [z.tile(pop_ref, i, y) * np.float32(weights[i]) for i in range(Q)]
         post, jx, moment_xy = collide(f, solid)
@@ -350,12 +379,31 @@
             post_ref[i, here, :] = post[i]
         acc_ref[0, here, :] = jnp.where(solid, 0.0, jx)
         acc_ref[1, here, :] = jnp.where(solid, 0.0, -(1.0 - 0.5 * visc_rate) * moment_xy)
+    copies[-1].wait()
     pack_x(z, whole_ref[0], post_ref, sends)
 
 
-def second_kernel(z, whole_ref, part_ref, post_ref, mask_ref, *refs):
-    gets, (h_ref, inner_ref, outer_ref), scratch = refs[: z.count - 1], refs[z.count - 1 : z.count + 2], refs[z.count + 2 :]
-    shift_xy(z, whole_ref[0], part_ref[0], post_ref, gets, h_ref, *scratch)
+def fetch_scalars(whole_hbm, part_hbm, whole_ref, part_ref, sems):
+    copies = [
+        pltpu.make_async_copy(whole_hbm, whole_ref, sems.at[0]),
+        pltpu.make_async_copy(part_hbm, part_ref, sems.at[1]),
+    ]
+    for copy in copies:
+        copy.start()
+
+    def scalars():
+        for copy in copies:
+            copy.wait()
+        return whole_ref, part_ref
+
+    return scalars
+
+
+def second_kernel(z, whole_hbm, part_hbm, post_ref, mask_ref, *refs):
+    gets, (h_ref, inner_ref, outer_ref) = refs[: z.count - 1], refs[z.count - 1 : z.count + 2]
+    scratch = refs[z.count + 2 :]
+    scalars = fetch_scalars(whole_hbm, part_hbm, *scratch[3:])
+    shift_xy(z, 0, scalars, post_ref, gets, h_ref, *scratch[:3])
     even = lax.rem(lax.axis_index("gz"), 2) == 0
 
     def line(i, row):
@@ -378,9 +426,12 @@
         outer_ref[MASK_SLOT, here, :] = jnp.broadcast_to(jnp.where(even, down, up), shape)
 
 
-def third_kernel(z, whole_ref, h_ref, inner_ref, outer_ref, mask_ref, old_ref, *refs):
-    (g_ref, acc_ref, part_ref), sends = refs[:3], refs[3 : 2 + z.count]
-    sides, extra = refs[2 + z.count :]
+def third_kernel(z, whole_hbm, h_ref, inner_ref, outer_ref, mask_ref, old_ref, *refs):
+    (g_ref, acc_hbm, part_ref), sends = refs[:3], refs[3 : 2 + z.count]
+    sides, extra, acc_ref, whole_ref, sems = refs[2 + z.count :]
+    whole_copy = pltpu.make_async_copy(whole_hbm, whole_ref, sems.at[0])
+    whole_copy.start()
+    acc_copy = pltpu.make_async_copy(acc_ref, acc_hbm, sems.at[1])
     even = lax.rem(lax.axis_index("gz"), 2) == 0
     sides[jnp.where(even, 1, 0)] = inner_ref[...]
     sides[jnp.where(even, 0, 1)] = outer_ref[...]
@@ -426,42 +477,69 @@
             acc_ref[k, here, :] = value
             total = z.spread(jnp.sum(value, axis=1, keepdims=True))
             sums = jnp.where(lanes == k * z.planes + y, total, sums)
+    acc_copy.start()
     part_ref[...] = sums
+    whole_copy.wait()
     pack_x(z, whole_ref[1], g_ref, sends, sums)
-
-
-def fourth_kernel(z, whole_ref, part_ref, g_ref, own_ref, *refs):
-    gets, (out_ref, profile_ref), scratch = refs[: z.count - 1], refs[z.count - 1 : z.count + 1], refs[z.count + 1 :]
-    shift_xy(z, whole_ref[1], part_ref[1], g_ref, gets, out_ref, *scratch)
+    acc_copy.wait()
+
+
+def fourth_kernel(z, whole_hbm, part_hbm, g_ref, own_ref, *refs):
+    gets, (out_hbm, profile_hbm) = refs[: z.count - 1], refs[z.count - 1 : z.count + 1]
+    scratch = refs[z.count + 1 :]
+    scalars = fetch_scalars(whole_hbm, part_hbm, *scratch[3:6])
+    out_ref, profile_ref, sems = scratch[6:]
     terms = [own_ref[...]] + [gets[d - 1][z.slots(d)] for d in range(1, z.count)]
     while len(terms) > 1:
         terms = [terms[k] + terms[k + 1] for k in range(0, len(terms), 2)]
-    profile_ref[...] = terms[0].T[: profile_ref.shape[0], :]
+    for k in range(2):
+        profile_ref[k] = terms[0][:, k * z.planes : (k + 1) * z.planes]
+    copies = [pltpu.make_async_copy(profile_ref, profile_hbm, sems.at[CHUNKS])]
+    copies[0].start()
+
+    def finish(k):
+        group = z.planes // CHUNKS * z.depth
+        part = (slice(None), pl.ds(k * group, group), slice(None))
+        copies.append(pltpu.make_async_copy(out_ref.at[part], out_hbm.at[part], sems.at[k]))
+        copies[-1].start()
+
+    shift_xy(z, 1, scalars, g_ref, gets, out_ref, *scratch[:3], finish)
+    for copy in copies:
+        copy.wait()
 
 
 def local(count, ranks, pop_ratio, solid_blocks, shift_whole, shift_frac):
     _, planes, depth, width = pop_ratio.shape
     z = Sizes(planes, depth, width, count)
     assert ranks % 2 == 0
-    f32 = lambda *shape: jax.ShapeDtypeStruct(shape, jnp.float32)
+    f32 = lambda *shape: pltpu.VMEM(shape, jnp.float32)
+    hbm = lambda ref: jax.ShapeDtypeStruct(ref.shape, ref.dtype)
+    keep = lambda *values: [pltpu.with_memory_space_constraint(v, pltpu.VMEM) for v in values]
     vmem = pl.BlockSpec(memory_space=pltpu.VMEM)
-    smem = pl.BlockSpec(memory_space=pltpu.SMEM)
+    outside = pl.BlockSpec(memory_space=pl.ANY)
     cells = f32(Q, planes * depth, width)
     fields = f32(2, planes * depth, width)
     halo = f32(Q + 1, planes, width)
     shifts = [pltpu.VMEM((count, len(rising), depth, width), jnp.float32)] * 2
     shifts.append(pltpu.VMEM((count, depth, width), jnp.float32))
+    pair = pltpu.SMEM(shift_whole.shape, jnp.int32)
+    sems = lambda number: pltpu.SemaphoreType.DMA((number,))
+    shifts += [pair, pair, sems(2)]
+    outer_keep = lambda *values: [pltpu.with_memory_space_constraint(v, pltpu.HBM) for v in values]
+    shift_whole, shift_frac, solid_blocks = outer_keep(shift_whole, shift_frac, solid_blocks)
 
     def buffers(more):
         return [f32(z.slots(d) + more, depth, width) for d in range(1, count)]
 
-    def call(body, ins, outs, scratch=()):
+    def call(body, ins, outs, scratch=(), direct=()):
+        specs = [outside if k in direct else vmem for k in range(len(outs))]
         return pl.pallas_call(
             functools.partial(body, z),
             out_shape=outs,
             in_specs=ins,
-            out_specs=[vmem] * len(outs),
+            out_specs=specs,
             scratch_shapes=list(scratch),
+            compiler_params=pltpu.CompilerParams(vmem_limit_bytes=8 << 20),
             name=body.__name__,
         )
 
@@ -474,33 +552,44 @@
     pairs = [(i, i ^ 1) for i in range(ranks)]
     across = [(i, (i - 1 if i % 2 == 0 else i + 1) % ranks) for i in range(ranks)]
 
-    pop = pop_ratio.reshape(cells.shape)
+    (pop,) = outer_keep(pop_ratio.reshape(cells.shape))
     post, old, mask, *sends = call(
-        first_kernel, [smem, vmem, vmem], [cells, fields, f32(planes // BLOCK * z.deep, width)] + buffers(0)
+        first_kernel,
+        [outside] * 3,
+        [cells, fields, f32(planes // BLOCK * z.deep, width)] + buffers(0),
+        [pair, cells, pltpu.VMEM(solid_blocks.shape, jnp.int32), sems(CHUNKS + 2)],
     )(shift_whole, pop, solid_blocks)
     gets = swap_x(sends)
     h, inner, outer = call(
-        second_kernel, [smem, smem] + [vmem] * (1 + count), [cells, halo, halo], shifts
-    )(shift_whole, shift_frac, post, mask, *gets)
+        second_kernel, [outside] * 2 + [vmem] * (1 + count), [cells, halo, halo], shifts
+    )(shift_whole, shift_frac, *keep(post, mask, *gets))
     outer = lax.ppermute(outer, "gz", across)
     inner = lax.ppermute(inner, "gz", pairs)
     g, acc, own, *sends = call(
         third_kernel,
-        [smem] + [vmem] * 5,
-        [cells, fields, f32(depth, width)] + buffers(1),
+        [outside] + [vmem] * 5,
+        [cells, hbm(fields), f32(depth, width)] + buffers(1),
         [
             pltpu.VMEM((2, Q + 1, planes, width), jnp.float32),
             pltpu.VMEM((2, len(upward), planes, width), jnp.float32),
+            fields,
+            pair,
+            sems(2),
         ],
-    )(shift_whole, h, inner, outer, mask, old)
+        [1],
+    )(shift_whole, *keep(h, inner, outer, mask, old))
     gets = swap_x(sends)
     out, profile = call(
-        fourth_kernel, [smem, smem] + [vmem] * (1 + count), [cells, f32(2 * planes, depth)], shifts
-    )(shift_whole, shift_frac, g, own, *gets)
+        fourth_kernel,
+        [outside] * 2 + [vmem] * (1 + count),
+        [hbm(cells), hbm(f32(2, depth, planes))],
+        shifts + [cells, f32(2, depth, planes), sems(CHUNKS + 1)],
+        [0, 1],
+    )(shift_whole, shift_frac, *keep(g, own, *gets))
     return (
         out.reshape(pop_ratio.shape),
         acc.reshape(2, planes, depth, width),
-        profile.reshape(2, planes, depth),
+        jnp.swapaxes(profile, 1, 2),
     )
 
 

time: 40.3 us -> 30 us (0.74)
  Pallas kernels: 12.6 us -> 6.2 us
  local copies, waits for them, and re-layouts: 3.3 us -> 0 us
  waiting for transfers between devices: 11.6 us -> 11 us
    pallas_call x4, Pallas kernels: 12.6 us -> 6.2 us  [the longest x1 2.06 us: local(): call(fourth_kernel, [outside] * 2 + [vmem] * (1 + count), [hbm(cells), hb...]
    unnamed x17 -> x0, local copies, waits for them, and re-layouts: 3.3 us -> none
    ppermute x6, waiting for transfers between devices: 7.42 us -> 7 us  [swap_x(): lax.ppermute(values[d - 1], 'gx', [(i, i ^ d) for i in range(count)])]
where the time goes in v2:
time: 30 us; the launch traced here: 29.8 us
  starting transfers between devices  11.9 us (40%)
  waiting for transfers between devices  11 us (37%)
  Pallas kernels  6.2 us (21%)
  between operations  0.67 us (2%)
    ppermute x6, starting transfers between devices, swap_x(): lax.ppermute(values[d - 1], 'gx', [(i, i ^ d) for i in range(count)])  8.15 us
    ppermute x6, waiting for transfers between devices, swap_x(): lax.ppermute(values[d - 1], 'gx', [(i, i ^ d) for i in range(count)])  7 us
    ppermute x1, waiting for transfers between devices, local(): outer = lax.ppermute(outer, 'gz', across)  4.01 us
    ppermute x1, starting transfers between devices, local(): outer = lax.ppermute(outer, 'gz', across)  3.7 us
    pallas_call x1, Pallas kernels, local(): call(fourth_kernel, [outside] * 2 + [vmem] * (1 + count), [hbm(cells), hb...  2.06 us
    pallas_call x1, Pallas kernels, local(): call(first_kernel, [outside] * 3, [cells, fields, f32(planes // BLOCK * z...  1.92 us
    pallas_call x1, Pallas kernels, local(): call(second_kernel, [outside] * 2 + [vmem] * (1 + count), [cells, halo, h...  1.15 us
    pallas_call x1, Pallas kernels, local(): call(third_kernel, [outside] + [vmem] * 5, [cells, hbm(fields), f32(depth...  1.07 us
  transfers between devices with their start and end apart: 8, of which 5 were waited for; matrix products, arithmetic and copies ran while one was open for 0% of the time, Pallas kernels for 0%

profile of v2, /device:TPU:0, one launch (start us, length us, event | category | flops | bytes accessed | tf_op | source)
XLA Modules:
  0.0 29.8 jit_solution(6131946727398364972)
XLA Ops:
  0.6 1.9 %first_kernel.1 = (f32[19,128,128]{2,1,0:T(8,128)S(1)}, f32[2,128,128]{2,1,0:T(8,128)S(1)}, f32[8,128]{1,0:T(8,128)S(1)}, f32[6,8,128]{2,1,0:T(8,128)S(1)}, f32[...) custom-call(s32[2]{0:T(128)} %whole_hbm.7, f32[19,128,128]{2,1,0:T(8,128)} %bitcast.4, s32[4,2,32]{2,1,0:T(2,128)} %solid_hbm.1), custom_call_target="tpu_custom_call" | custom-call | tf_op jit(solution)/shard_map/first_kernel/pallas_call | solution.py:556
  2.6 3.1 %collective-permute-start.1 = (f32[11,8,128]{2,1,0:T(8,128)S(1)}, f32[11,8,128]{2,1,0:T(8,128)S(1)}, u32[]{:S(2)}, u32[]{:S(2)}) collective-permute-start(f32[11,8,128]{2,1,0:T(8,128)S(1)} %get-tuple-element.23), channel_id=1, source_target_pairs={{0,16},{8,24},{16,0},{24,8},{1,17},{9,25},{17,1},{25,9},{2,18},{10... | collective-permute-start | bytes 135176 | tf_op jit(solution)/shard_map/ppermute | solution.py:548
  5.6 1.5 %collective-permute-start = (f32[6,8,128]{2,1,0:T(8,128)S(1)}, f32[6,8,128]{2,1,0:T(8,128)S(1)}, u32[]{:S(2)}, u32[]{:S(2)}) collective-permute-start(f32[6,8,128]{2,1,0:T(8,128)S(1)} %get-tuple-element.22), channel_id=1, source_target_pairs={{0,8},{8,0},{16,24},{24,16},{1,9},{9,1},{17,25},{25,17},{2,10},{10... | collective-permute-start | bytes 73736 | tf_op jit(solution)/shard_map/ppermute | solution.py:548
  7.1 0.0 collective-permute-start.2
  7.2 2.3 %collective-permute-done.refs_0_ = f32[6,8,128]{2,1,0:T(8,128)S(1)} collective-permute-done((f32[6,8,128]{2,1,0:T(8,128)S(1)}, f32[6,8,128]{2,1,0:T(8,128)S(1)}, u32[]{:S(2)}, u32[]{:S(2)}) %collective-permute-start) | collective-permute-done | bytes 24608 | tf_op jit(solution)/shard_map/ppermute | solution.py:548
  9.4 2.4 %collective-permute-done.2.refs_2_ = f32[6,8,128]{2,1,0:T(8,128)S(1)} collective-permute-done((f32[6,8,128]{2,1,0:T(8,128)S(1)}, f32[6,8,128]{2,1,0:T(8,128)S(1)}, u32[]{:S(2)}, u32[]{:S(2)}) %collective-permute-start.2) | collective-permute-done | bytes 24608 | tf_op jit(solution)/shard_map/ppermute | solution.py:548
  11.8 0.0 collective-permute-done.1.refs_1_
  11.8 1.2 %second_kernel.1 = (f32[19,128,128]{2,1,0:T(8,128)S(1)}, f32[20,16,128]{2,1,0:T(8,128)S(1)}, f32[20,16,128]{2,1,0:T(8,128)S(1)}) custom-call(s32[2]{0:T(128)} %whole_hbm.7, s32[2]{0:T(128)} %part_hbm.3, f32[19,128,128]{2,1,0:T(8,128)S(1)} %get-tuple-element.20.post_ref, f32[8,128]{1,0:T(8,128)S(1)} %get-tuple-element.21.mask_ref, ...), custom_call_target="tpu_custom_call" | custom-call | tf_op jit(solution)/shard_map/second_kernel/pallas_call | solution.py:563
  13.0 0.1 collective-permute-start.3
  13.1 3.7 %collective-permute-start.4 = (f32[20,16,128]{2,1,0:T(8,128)S(1)}, f32[20,16,128]{2,1,0:T(8,128)S(1)}, u32[]{:S(2)}, u32[]{:S(2)}) collective-permute-start(f32[20,16,128]{2,1,0:T(8,128)S(1)} %get-tuple-element.27), channel_id=1, source_target_pairs={{0,7},{1,2},{2,1},{3,4},{4,3},{5,6},{6,5},{7,0},{8,15},{9,10},{10,... | collective-permute-start | bytes 491528 | tf_op jit(solution)/shard_map/ppermute | solution.py:566
  16.8 0.0 collective-permute-done.3.inner_ref
  16.8 4.0 %collective-permute-done.4.outer_ref = f32[20,16,128]{2,1,0:T(8,128)S(1)} collective-permute-done((f32[20,16,128]{2,1,0:T(8,128)S(1)}, f32[20,16,128]{2,1,0:T(8,128)S(1)}, u32[]{:S(2)}, u32[]{:S(2)}) %collective-permute-start.4) | collective-permute-done | bytes 163872 | tf_op jit(solution)/shard_map/ppermute | solution.py:566
  20.8 1.1 %third_kernel.1 = (f32[19,128,128]{2,1,0:T(8,128)S(1)}, f32[2,128,128]{2,1,0:T(8,128)}, f32[8,128]{1,0:T(8,128)S(1)}, f32[7,8,128]{2,1,0:T(8,128)S(1)}, f32[12,8...) custom-call(s32[2]{0:T(128)} %whole_hbm.7, f32[19,128,128]{2,1,0:T(8,128)S(1)} %get-tuple-element.25.h_ref, ...), custom_call_target="tpu_custom_call" | custom-call | tf_op jit(solution)/shard_map/third_kernel/pallas_call | solution.py:568
  21.9 0.6 %collective-permute-start.6 = (f32[12,8,128]{2,1,0:T(8,128)S(1)}, f32[12,8,128]{2,1,0:T(8,128)S(1)}, u32[]{:S(2)}, u32[]{:S(2)}) collective-permute-start(f32[12,8,128]{2,1,0:T(8,128)S(1)} %get-tuple-element.32), channel_id=1, source_target_pairs={{0,16},{8,24},{16,0},{24,8},{1,17},{9,25},{17,1},{25,9},{2,18},{10... | collective-permute-start | bytes 147464 | tf_op jit(solution)/shard_map/ppermute | solution.py:548
  22.4 0.5 %collective-permute-start.5 = (f32[7,8,128]{2,1,0:T(8,128)S(1)}, f32[7,8,128]{2,1,0:T(8,128)S(1)}, u32[]{:S(2)}, u32[]{:S(2)}) collective-permute-start(f32[7,8,128]{2,1,0:T(8,128)S(1)} %get-tuple-element.31), channel_id=1, source_target_pairs={{0,8},{8,0},{16,24},{24,16},{1,9},{9,1},{17,25},{25,17},{2,10},{10... | collective-permute-start | bytes 86024 | tf_op jit(solution)/shard_map/ppermute | solution.py:548
  23.0 2.4 %collective-permute-start.7 = (f32[7,8,128]{2,1,0:T(8,128)S(1)}, f32[7,8,128]{2,1,0:T(8,128)S(1)}, u32[]{:S(2)}, u32[]{:S(2)}) collective-permute-start(f32[7,8,128]{2,1,0:T(8,128)S(1)} %get-tuple-element.33), channel_id=1, source_target_pairs={{0,24},{8,16},{16,8},{24,0},{1,25},{9,17},{17,9},{25,1},{2,26},{10... | collective-permute-start | bytes 86024 | tf_op jit(solution)/shard_map/ppermute | solution.py:548
  25.4 0.9 %collective-permute-done.5.refs_0_ = f32[7,8,128]{2,1,0:T(8,128)S(1)} collective-permute-done((f32[7,8,128]{2,1,0:T(8,128)S(1)}, f32[7,8,128]{2,1,0:T(8,128)S(1)}, u32[]{:S(2)}, u32[]{:S(2)}) %collective-permute-start.5) | collective-permute-done | bytes 28704 | tf_op jit(solution)/shard_map/ppermute | solution.py:548
  26.3 1.4 %collective-permute-done.7.refs_2_ = f32[7,8,128]{2,1,0:T(8,128)S(1)} collective-permute-done((f32[7,8,128]{2,1,0:T(8,128)S(1)}, f32[7,8,128]{2,1,0:T(8,128)S(1)}, u32[]{:S(2)}, u32[]{:S(2)}) %collective-permute-start.7) | collective-permute-done | bytes 28704 | tf_op jit(solution)/shard_map/ppermute | solution.py:548
  27.8 0.0 collective-permute-done.6.refs_1_
  27.8 2.1 %fourth_kernel.1 = (f32[19,128,128]{2,1,0:T(8,128)}, f32[2,8,16]{2,1,0:T(8,128)}) custom-call(s32[2]{0:T(128)} %whole_hbm.7, s32[2]{0:T(128)} %part_hbm.3, f32[19,128,128]{2,1,0:T(8,128)S(1)} %get-tuple-element.29.g_ref, f32[8,128]{1,0:T(8,128)S(1)} %get-tuple-element.30.own_ref, f32[7,8,128]{2,1,0:T(8,128)S(1)} %collective-permute-done.5.refs_0_, ...), custom_call_target="tpu_custom_call" | custom-call | tf_op jit(solution)/shard_map/fourth_kernel/pallas_call | solution.py:582
Async XLA Ops:
  2.6 9.3 %collective-permute-start.1 = (f32[11,8,128]{2,1,0:T(8,128)S(1)}, f32[11,8,128]{2,1,0:T(8,128)S(1)}, u32[]{:S(2)}, u32[]{:S(2)}) collective-permute-start(f32[11,8,128]{2,1,0:T(8,128)S(1)} %get-tuple-element.23), channel_id=1, source_target_pairs={{0,16},{8,24},{16,0},{24,8},{1,17},{9,25},{17,1},{25,9},{2,18},{10... | collective-permute-start | bytes 135176 | tf_op jit(solution)/shard_map/ppermute | solution.py:548
  5.6 3.8 %collective-permute-start = (f32[6,8,128]{2,1,0:T(8,128)S(1)}, f32[6,8,128]{2,1,0:T(8,128)S(1)}, u32[]{:S(2)}, u32[]{:S(2)}) collective-permute-start(f32[6,8,128]{2,1,0:T(8,128)S(1)} %get-tuple-element.22), channel_id=1, source_target_pairs={{0,8},{8,0},{16,24},{24,16},{1,9},{9,1},{17,25},{25,17},{2,10},{10... | collective-permute-start | bytes 73736 | tf_op jit(solution)/shard_map/ppermute | solution.py:548
  7.1 4.7 %collective-permute-start.2 = (f32[6,8,128]{2,1,0:T(8,128)S(1)}, f32[6,8,128]{2,1,0:T(8,128)S(1)}, u32[]{:S(2)}, u32[]{:S(2)}) collective-permute-start(f32[6,8,128]{2,1,0:T(8,128)S(1)} %get-tuple-element.24), channel_id=1, source_target_pairs={{0,24},{8,16},{16,8},{24,0},{1,25},{9,17},{17,9},{25,1},{2,26},{10... | collective-permute-start | bytes 73736 | tf_op jit(solution)/shard_map/ppermute | solution.py:548
  13.0 3.8 %collective-permute-start.3 = (f32[20,16,128]{2,1,0:T(8,128)S(1)}, f32[20,16,128]{2,1,0:T(8,128)S(1)}, u32[]{:S(2)}, u32[]{:S(2)}) collective-permute-start(f32[20,16,128]{2,1,0:T(8,128)S(1)} %get-tuple-element.26), channel_id=1, source_target_pairs={{0,1},{1,0},{2,3},{3,2},{4,5},{5,4},{6,7},{7,6},{8,9},{9,8},{10,11... | collective-permute-start | bytes 491528 | tf_op jit(solution)/shard_map/ppermute | solution.py:567
  13.1 7.7 %collective-permute-start.4 = (f32[20,16,128]{2,1,0:T(8,128)S(1)}, f32[20,16,128]{2,1,0:T(8,128)S(1)}, u32[]{:S(2)}, u32[]{:S(2)}) collective-permute-start(f32[20,16,128]{2,1,0:T(8,128)S(1)} %get-tuple-element.27), channel_id=1, source_target_pairs={{0,7},{1,2},{2,1},{3,4},{4,3},{5,6},{6,5},{7,0},{8,15},{9,10},{10,... | collective-permute-start | bytes 491528 | tf_op jit(solution)/shard_map/ppermute | solution.py:566
  21.9 5.9 %collective-permute-start.6 = (f32[12,8,128]{2,1,0:T(8,128)S(1)}, f32[12,8,128]{2,1,0:T(8,128)S(1)}, u32[]{:S(2)}, u32[]{:S(2)}) collective-permute-start(f32[12,8,128]{2,1,0:T(8,128)S(1)} %get-tuple-element.32), channel_id=1, source_target_pairs={{0,16},{8,24},{16,0},{24,8},{1,17},{9,25},{17,1},{25,9},{2,18},{10... | collective-permute-start | bytes 147464 | tf_op jit(solution)/shard_map/ppermute | solution.py:548
  22.4 3.9 %collective-permute-start.5 = (f32[7,8,128]{2,1,0:T(8,128)S(1)}, f32[7,8,128]{2,1,0:T(8,128)S(1)}, u32[]{:S(2)}, u32[]{:S(2)}) collective-permute-start(f32[7,8,128]{2,1,0:T(8,128)S(1)} %get-tuple-element.31), channel_id=1, source_target_pairs={{0,8},{8,0},{16,24},{24,16},{1,9},{9,1},{17,25},{25,17},{2,10},{10... | collective-permute-start | bytes 86024 | tf_op jit(solution)/shard_map/ppermute | solution.py:548
  23.0 4.8 %collective-permute-start.7 = (f32[7,8,128]{2,1,0:T(8,128)S(1)}, f32[7,8,128]{2,1,0:T(8,128)S(1)}, u32[]{:S(2)}, u32[]{:S(2)}) collective-permute-start(f32[7,8,128]{2,1,0:T(8,128)S(1)} %get-tuple-element.33), channel_id=1, source_target_pairs={{0,24},{8,16},{16,8},{24,0},{1,25},{9,17},{17,9},{25,1},{2,26},{10... | collective-permute-start | bytes 86024 | tf_op jit(solution)/shard_map/ppermute | solution.py:548

commit v3 on v2

--- a/solution.py
+++ b/solution.py
@@ -7,6 +7,7 @@
 from jax.experimental import pallas as pl
 from jax.experimental.pallas import tpu as pltpu
 from jax.sharding import PartitionSpec as P
+
 
 BLOCK = 4
 velocity_list = [
@@ -39,15 +40,17 @@
 mirror = [velocity_list.index((x, y, -z)) for x, y, z in velocity_list]
 rising = [i for i in range(Q) if CY[i] == 1]
 falling = [i for i in range(Q) if CY[i] == -1]
-level_y = [i for i in range(Q) if CY[i] == 0]
 eastward = [i for i in range(Q) if CX[i] == 1]
 westward = [i for i in range(Q) if CX[i] == -1]
 upward = [i for i in range(Q) if CZ[i] == 1]
 level = [i for i in range(Q) if CZ[i] == 0]
-near_list = level + upward
-near_slot = {i: s for s, i in enumerate(near_list)}
-far_slot = {i: len(near_list) + s for s, i in enumerate(upward)}
-MASK_SLOT = Q
+downward = [mirror[i] for i in upward]
+straight = [i for i in range(Q) if CX[i] == 0]
+slanted = [i for i in range(Q) if CX[i] != 0]
+SPANS = [(i, next(k for k in range(i, Q + 1) if k == Q or CX[k] == 0)) for i in slanted if CX[i - 1] == 0]
+PART, SUMS = len(upward), 2 * len(upward)
+MASK = SUMS + 4
+SLOTS = MASK + 1
 wall_speed = 0.08
 visc_rate = 1.25
 fraction_unit = 4096.0
@@ -86,89 +89,127 @@
 RATE = [rate / norm for rate, norm in zip(relax_rates, row_norms())]
 
 
-def collide(f, solid):
-    sums = {i: f[i] + f[i + 1] for i in range(1, Q, 2)}
-    difs = {i: f[i] - f[i + 1] for i in range(1, Q, 2)}
-    p1, d1 = sums[7] + sums[9], sums[7] - sums[9]
-    p2, d2 = sums[11] + sums[13], sums[11] - sums[13]
-    p3, d3 = sums[15] + sums[17], sums[15] - sums[17]
-    s23 = sums[3] + sums[5]
-    axis = sums[1] + s23
-    p12 = p1 + p2
-    diag = p12 + p3
-    rho = f[0] + axis + diag
+def plus(a, b):
+    return b if a is None else a if b is None else a + b
+
+
+def minus(a, b):
+    return a if b is None else -b if a is None else a - b
+
+
+def scaled(factor, a):
+    return None if a is None else factor * a
+
+
+def moments(f):
+    sums = {i: plus(f[i], f[i + 1]) for i in range(1, Q, 2)}
+    difs = {i: minus(f[i], f[i + 1]) for i in range(1, Q, 2)}
+    p1, d1 = plus(sums[7], sums[9]), minus(sums[7], sums[9])
+    p2, d2 = plus(sums[11], sums[13]), minus(sums[11], sums[13])
+    p3, d3 = plus(sums[15], sums[17]), minus(sums[15], sums[17])
+    s23 = plus(sums[3], sums[5])
+    axis = plus(sums[1], s23)
+    p12 = plus(p1, p2)
+    diag = plus(p12, p3)
+    a, c = plus(difs[7], difs[9]), minus(difs[7], difs[9])
+    b, e = plus(difs[11], difs[13]), minus(difs[11], difs[13])
+    d, g = plus(difs[15], difs[17]), minus(difs[15], difs[17])
+    ab, cd, eg = plus(a, b), plus(c, d), plus(e, g)
+    axis_x, diag_x = minus(scaled(2.0, sums[1]), s23), minus(p12, scaled(2.0, p3))
+    axis_w, diag_w = minus(sums[3], sums[5]), minus(p1, p2)
+    kept = [
+        plus(f[0], plus(axis, diag)),
+        plus(difs[1], ab),
+        plus(difs[3], cd),
+        plus(difs[5], eg),
+    ]
+    others = [
+        minus(minus(scaled(8.0, diag), scaled(11.0, axis)), scaled(30.0, f[0])),
+        plus(scaled(12.0, f[0]), minus(diag, scaled(4.0, axis))),
+        minus(ab, scaled(4.0, difs[1])),
+        minus(cd, scaled(4.0, difs[3])),
+        minus(eg, scaled(4.0, difs[5])),
+        plus(axis_x, diag_x),
+        minus(diag_x, scaled(2.0, axis_x)),
+        plus(axis_w, diag_w),
+        minus(diag_w, scaled(2.0, axis_w)),
+        d1,
+        d3,
+        d2,
+        minus(a, b),
+        minus(d, c),
+        minus(e, g),
+    ]
+    return kept, others
+
+
+ORDER = [1, 2, 4, 6, 8, 9, 10, 11, 12, 13, 14, 15, 16, 17, 18]
+
+
+def equilibrium(rho, jx, jy, jz):
     inverse = 1.0 / rho
-    a, c = difs[7] + difs[9], difs[7] - difs[9]
-    b, e = difs[11] + difs[13], difs[11] - difs[13]
-    d, g = difs[15] + difs[17], difs[15] - difs[17]
-    ab, cd, eg = a + b, c + d, e + g
-    jx, jy, jz = difs[1] + ab, difs[3] + cd, difs[5] + eg
     ux, uy, uz = jx * inverse, jy * inverse, jz * inverse
     xx, yy, zz = jx * ux, jy * uy, jz * uz
     yz_sum, yz_dif = yy + zz, yy - zz
     square = xx + yz_sum
-
-    even_e = RATE[1] * (8.0 * diag - 11.0 * axis - 30.0 * f[0] + 11.0 * rho - 19.0 * square)
-    even_s = RATE[2] * (12.0 * f[0] - 4.0 * axis + diag - 3.0 * rho + 5.5 * square)
-    axis_x, diag_x = 2.0 * sums[1] - s23, p12 - 2.0 * p3
     eq_x = 2.0 * xx - yz_sum
-    even_x = RATE[9] * (axis_x + diag_x - eq_x)
-    even_px = RATE[10] * (diag_x - 2.0 * axis_x + 0.5 * eq_x)
-    axis_w, diag_w = sums[3] - sums[5], p1 - p2
-    even_w = RATE[11] * (axis_w + diag_w - yz_dif)
-    even_pw = RATE[12] * (diag_w - 2.0 * axis_w + 0.5 * yz_dif)
-    moment_xy = d1 - jx * uy
-    even_xy = RATE[13] * moment_xy
-    even_yz = RATE[14] * (d3 - jy * uz)
-    even_xz = RATE[15] * (d2 - jx * uz)
-    flow_x = RATE[4] * (ab - 4.0 * difs[1] + (2.0 / 3.0) * jx)
-    flow_y = RATE[6] * (cd - 4.0 * difs[3] + (2.0 / 3.0) * jy)
-    flow_z = RATE[8] * (eg - 4.0 * difs[5] + (2.0 / 3.0) * jz)
-    twist_x = RATE[16] * (a - b)
-    twist_y = RATE[17] * (d - c)
-    twist_z = RATE[18] * (e - g)
-
-    base_axis = -11.0 * even_e - 4.0 * even_s
-    base_diag = 8.0 * even_e + even_s
-    lean = even_x - 2.0 * even_px
-    tilt = even_w - 2.0 * even_pw
-    side_x = even_x + even_px
-    side_w = even_w + even_pw
-    flat = base_diag + side_x
-    diag_xy, diag_xz = flat + side_w, flat - side_w
-    diag_yz = base_diag - 2.0 * side_x
-    low = base_axis - lean
+    third = -2.0 / 3.0
+    eq = [19.0 * square - 11.0 * rho, 3.0 * rho - 5.5 * square]
+    eq += [third * jx, third * jy, third * jz]
+    eq += [eq_x, -0.5 * eq_x, yz_dif, -0.5 * yz_dif, jx * uy, jy * uz, jx * uz]
+    return eq + [None] * 3
+
+
+def relax(moment):
+    scaled_by = [scaled(RATE[k], m) for k, m in zip(ORDER, moment)]
+    even_e, even_s, flow_x, flow_y, flow_z, even_x, even_px, even_w, even_pw = scaled_by[:9]
+    even_xy, even_yz, even_xz, twist_x, twist_y, twist_z = scaled_by[9:]
+    base_axis = minus(scaled(-11.0, even_e), scaled(4.0, even_s))
+    base_diag = plus(scaled(8.0, even_e), even_s)
+    lean = minus(even_x, scaled(2.0, even_px))
+    tilt = minus(even_w, scaled(2.0, even_pw))
+    side_x, side_w = plus(even_x, even_px), plus(even_w, even_pw)
+    flat = plus(base_diag, side_x)
+    diag_xy, diag_xz = plus(flat, side_w), minus(flat, side_w)
+    diag_yz = minus(base_diag, scaled(2.0, side_x))
+    low = minus(base_axis, lean)
     even = {
-        1: base_axis + 2.0 * lean,
-        3: low + tilt,
-        5: low - tilt,
-        7: diag_xy + even_xy,
-        9: diag_xy - even_xy,
-        11: diag_xz + even_xz,
-        13: diag_xz - even_xz,
-        15: diag_yz + even_yz,
-        17: diag_yz - even_yz,
+        1: plus(base_axis, scaled(2.0, lean)),
+        3: plus(low, tilt),
+        5: minus(low, tilt),
+        7: plus(diag_xy, even_xy),
+        9: minus(diag_xy, even_xy),
+        11: plus(diag_xz, even_xz),
+        13: minus(diag_xz, even_xz),
+        15: plus(diag_yz, even_yz),
+        17: minus(diag_yz, even_yz),
     }
-    x_up, x_down = flow_x + twist_x, flow_x - twist_x
-    y_up, y_down = flow_y + twist_y, flow_y - twist_y
-    z_up, z_down = flow_z + twist_z, flow_z - twist_z
+    x_up, x_down = plus(flow_x, twist_x), minus(flow_x, twist_x)
+    y_up, y_down = plus(flow_y, twist_y), minus(flow_y, twist_y)
+    z_up, z_down = plus(flow_z, twist_z), minus(flow_z, twist_z)
     odd = {
-        1: -4.0 * flow_x,
-        3: -4.0 * flow_y,
-        5: -4.0 * flow_z,
-        7: x_up + y_down,
-        9: x_up - y_down,
-        11: x_down + z_up,
-        13: x_down - z_up,
-        15: y_up + z_down,
-        17: y_up - z_down,
+        1: scaled(-4.0, flow_x),
+        3: scaled(-4.0, flow_y),
+        5: scaled(-4.0, flow_z),
+        7: plus(x_up, y_down),
+        9: minus(x_up, y_down),
+        11: plus(x_down, z_up),
+        13: minus(x_down, z_up),
+        15: plus(y_up, z_down),
+        17: minus(y_up, z_down),
     }
-    post = [None] * Q
-    post[0] = jnp.where(solid, f[0], f[0] + 30.0 * even_e - 12.0 * even_s)
+    out = [minus(scaled(12.0, even_s), scaled(30.0, even_e))]
     for i in range(1, Q, 2):
-        post[i] = jnp.where(solid, f[i + 1], f[i] - (even[i] + odd[i]))
-        post[i + 1] = jnp.where(solid, f[i], f[i + 1] - (even[i] - odd[i]))
-    return post, jx, moment_xy
+        out += [plus(even[i], odd[i]), minus(even[i], odd[i])]
+    return out
+
+
+def collide(f, solid):
+    kept, others = moments(f)
+    rest = [minus(m, e) for m, e in zip(others, equilibrium(*kept))]
+    change = relax(rest)
+    post = [jnp.where(solid, f[opposite[i]], f[i] - change[i]) for i in range(Q)]
+    return post, kept[1], rest[9]
 
 
 CHUNKS = 4
@@ -264,14 +305,12 @@
             send[slots] = extra
 
 
-def shift_xy(z, step, scalars, ref, gets, out, tops, bottoms, edges, finish=None):
+def fill_tables(z, ref, gets, tops, bottoms, edges):
     me = lax.axis_index("gx")
-    lanes = z.lanes()
-    last = z.width - 1
     for s in range(len(rising)):
         tops[me, s] = z.tile(ref, rising[s], z.planes - 1)
         bottoms[me, s] = z.tile(ref, falling[s], 0)
-    edges[me] = wall_columns(z, ref, lanes)
+    edges[me] = wall_columns(z, ref, z.lanes())
     for delta in range(1, z.count):
         get = gets[delta - 1]
         partner = jnp.bitwise_xor(me, delta)
@@ -280,35 +319,26 @@
             second = len(rising) + s if delta == z.count // 2 else s
             bottoms[partner, s] = get[second]
         edges[partner] = get[z.slots(delta) - 1]
-
     left = edges[lax.rem(me + z.count - 1, z.count)]
     right = edges[lax.rem(me + 1, z.count)]
-
-    def moved(i, y):
-        value = z.tile(ref, i, y)
-        if CX[i] == 1:
-            at = eastward.index(i) * z.planes + y
-            return jnp.where(lanes == 0, roll(left, -at), roll(value, 1))
-        if CX[i] == -1:
-            at = westward.index(i) * z.planes + y
-            return jnp.where(lanes == last, roll(right, last - at), roll(value, -1))
-        return value
-
-    def interior(start, stop):
-        for i in range(Q):
-            for y in range(start, stop):
-                if 0 <= y - CY[i] < z.planes:
-                    out[i, pl.ds(y * z.depth, z.depth), :] = moved(i, y - CY[i])
-
-    group = z.planes // CHUNKS
-    for k in range(1, CHUNKS - 1):
-        interior(k * group, (k + 1) * group)
-        if finish is not None:
-            finish(k)
-    interior(0, group)
-    interior(z.planes - group, z.planes)
-    whole_ref, part_ref = scalars()
-    whole, part = whole_ref[step], part_ref[step]
+    return left, right
+
+
+def moved_x(z, ref, i, y, left, right):
+    lanes, last = z.lanes(), z.width - 1
+    value = z.tile(ref, i, y)
+    if CX[i] == 1:
+        at = eastward.index(i) * z.planes + y
+        return jnp.where(lanes == 0, roll(left, -at), roll(value, 1))
+    if CX[i] == -1:
+        at = westward.index(i) * z.planes + y
+        return jnp.where(lanes == last, roll(right, last - at), roll(value, -1))
+    return value
+
+
+def sliding(z, whole, part, tops, bottoms, edges, put):
+    me = lax.axis_index("gx")
+    lanes, last = z.lanes(), z.width - 1
     weight = part.astype(jnp.float32) / fraction_unit
     far = lax.div(whole, z.width)
     rest = lax.rem(whole, z.width)
@@ -337,17 +367,17 @@
         near, next_one = window(i, tops, s, lax.rem(me + far, z.count), rest)
         fix = 6.0 * weights[i] * CX[i] * wall_speed
         value = (1.0 - weight) * near + weight * next_one
-        out[i, pl.ds(0, z.depth), :] = value - fix if CX[i] else value
-    if finish is not None:
-        finish(0)
+        put(i, value - fix if CX[i] else value)
     for s, i in enumerate(falling):
         block = lax.rem(me + 2 * z.count - far - 1, z.count)
         next_one, near = window(i, bottoms, s, block, last - rest)
         fix = 6.0 * weights[i] * CX[i] * wall_speed
         value = (1.0 - weight) * near + weight * next_one
-        out[i, pl.ds((z.planes - 1) * z.depth, z.depth), :] = value + fix if CX[i] else value
-    if finish is not None:
-        finish(CHUNKS - 1)
+        put(i, value + fix if CX[i] else value)
+
+
+def wall_slot(i):
+    return rising.index(i) if CY[i] == 1 else len(rising) + falling.index(i)
 
 
 def first_kernel(z, whole_hbm, pop_hbm, solid_hbm, post_ref, acc_ref, mask_ref, *refs):
@@ -400,30 +430,87 @@
 
 
 def second_kernel(z, whole_hbm, part_hbm, post_ref, mask_ref, *refs):
-    gets, (h_ref, inner_ref, outer_ref) = refs[: z.count - 1], refs[z.count - 1 : z.count + 2]
-    scratch = refs[z.count + 2 :]
-    scalars = fetch_scalars(whole_hbm, part_hbm, *scratch[3:])
-    shift_xy(z, 0, scalars, post_ref, gets, h_ref, *scratch[:3])
+    gets, outs = refs[: z.count - 1], refs[z.count - 1 : z.count + 3]
+    inner_ref, outer_ref, wall_ref, side_ref = outs
+    tops, bottoms, edges, whole_ref, part_ref, sems, rows_ref = refs[z.count + 3 :]
+    scalars = fetch_scalars(whole_hbm, part_hbm, whole_ref, part_ref, sems)
+    left, right = fill_tables(z, post_ref, gets, tops, bottoms, edges)
+    side_ref[0], side_ref[1] = left, right
+    columns = {1: left.T, -1: right.T}
+    shape = (z.planes, z.width)
+    lanes = lax.broadcasted_iota(jnp.int32, shape, 1)
+    heights = lax.broadcasted_iota(jnp.int32, shape, 0)
     even = lax.rem(lax.axis_index("gz"), 2) == 0
 
     def line(i, row):
-        return h_ref[i, pl.ds(row, z.planes, stride=z.depth), :]
-
-    def put(slot, up, down):
-        inner_ref[slot] = jnp.where(even, up, down)
-        outer_ref[slot] = jnp.where(even, down, up)
-
-    for i in near_list:
-        put(near_slot[i], line(i, z.depth - 1), line(mirror[i], 0))
-    for i in upward:
-        put(far_slot[i], line(i, z.depth - 2), line(mirror[i], 1))
+        value = post_ref[i, pl.ds(row, z.planes, stride=z.depth), :]
+        if CX[i]:
+            j = (eastward if CX[i] == 1 else westward).index(i)
+            column = columns[CX[i]][j * z.planes : (j + 1) * z.planes, row : row + 1]
+            edge = 0 if CX[i] == 1 else z.width - 1
+            value = jnp.where(lanes == edge, jnp.broadcast_to(column, shape), roll(value, CX[i]))
+        if CY[i]:
+            enter = 0 if CY[i] == 1 else z.planes - 1
+            wall = jnp.broadcast_to(wall_ref[wall_slot(i), row : row + 1, :], shape)
+            value = jnp.where(heights == enter, wall, roll(value, CY[i], 0))
+        return value
+
+    jobs = []
+    for side in range(2):
+        near, far = (z.depth - 1, z.depth - 2) if side == 0 else (0, 1)
+        for k in range(Q):
+            row = near if CZ[k] >= 0 else far
+            i = k if CZ[k] >= 0 else mirror[k]
+            jobs.append((side, k, i if side == 0 else mirror[i], row))
+    for still in (True, False):
+        for side, k, i, row in jobs:
+            if (CY[i] == 0) == still:
+                rows_ref[side, k] = line(i, row)
+        if still:
+            whole, part = (value[0] for value in scalars())
+
+            def put(i, value):
+                wall_ref[wall_slot(i)] = value
+
+            sliding(z, whole, part, tops, bottoms, edges, put)
+
+    chunk = min(8, z.planes)
+    for start in range(0, z.planes, chunk):
+        here = pl.ds(start, chunk)
+        found = []
+        for side in range(2):
+            f = [None] * Q
+            for i in level:
+                f[i] = rows_ref[side, i, here, :]
+            for i in upward:
+                f[i] = rows_ref[side, mirror[i], here, :]
+            kept, others = moments(f)
+            change = relax(others)
+            values = [rows_ref[side, i, here, :] for i in upward]
+            values += [f[i] - change[i] for i in upward]
+            found.append(values + kept)
+        for slot in range(MASK):
+            up, down = found[0][slot], found[1][slot]
+            inner_ref[slot, here, :] = jnp.where(even, up, down)
+            outer_ref[slot, here, :] = jnp.where(even, down, up)
     for k in range(z.planes // BLOCK):
         up = mask_ref[(k + 1) * z.deep - 1 : (k + 1) * z.deep, :]
         down = mask_ref[k * z.deep : k * z.deep + 1, :]
-        shape = (BLOCK, z.width)
         here = pl.ds(k * BLOCK, BLOCK)
-        inner_ref[MASK_SLOT, here, :] = jnp.broadcast_to(jnp.where(even, up, down), shape)
-        outer_ref[MASK_SLOT, here, :] = jnp.broadcast_to(jnp.where(even, down, up), shape)
+        block = (BLOCK, z.width)
+        inner_ref[MASK, here, :] = jnp.broadcast_to(jnp.where(even, up, down), block)
+        outer_ref[MASK, here, :] = jnp.broadcast_to(jnp.where(even, down, up), block)
+
+
+def bulk_kernel(z, post_ref, wall_ref, side_ref, h_ref):
+    left, right = side_ref[0], side_ref[1]
+    for i in range(Q):
+        for y in range(z.planes):
+            here = pl.ds(y * z.depth, z.depth)
+            if 0 <= y - CY[i] < z.planes:
+                h_ref[i, here, :] = moved_x(z, post_ref, i, y - CY[i], left, right)
+            else:
+                h_ref[i, here, :] = wall_ref[wall_slot(i)]
 
 
 def third_kernel(z, whole_hbm, h_ref, inner_ref, outer_ref, mask_ref, old_ref, *refs):
@@ -439,19 +526,18 @@
     for side in range(2):
         for start in range(0, z.planes, chunk):
             here = pl.ds(start, chunk)
+            row = start * z.depth + (0 if side == 0 else z.depth - 1)
             f = [None] * Q
-            for i in range(Q):
+            for i in downward:
                 k = i if side == 0 else mirror[i]
-                if CZ[k] == 0:
-                    f[i] = sides[side, near_slot[k], here, :]
-                elif CZ[k] == 1:
-                    f[i] = sides[side, far_slot[k], here, :]
-                else:
-                    row = start * z.depth + (0 if side == 0 else z.depth - 1)
-                    f[i] = h_ref[i, pl.ds(row, chunk, stride=z.depth), :]
-            post, _, _ = collide(f, sides[side, MASK_SLOT, here, :] > 0.5)
+                f[i] = h_ref[k, pl.ds(row, chunk, stride=z.depth), :]
+            kept, others = moments(f)
+            kept = [plus(kept[k], sides[side, SUMS + k, here, :]) for k in range(4)]
+            change = relax([minus(m, e) for m, e in zip(others, equilibrium(*kept))])
+            solid = sides[side, MASK, here, :] > 0.5
             for s, i in enumerate(upward):
-                extra[side, s, here, :] = post[i if side == 0 else mirror[i]]
+                value = sides[side, PART + s, here, :] - change[i]
+                extra[side, s, here, :] = jnp.where(solid, f[opposite[i]], value)
     rows, lanes = z.rows(), z.lanes()
 
     def moved(i, y, value, table, slot):
@@ -466,7 +552,7 @@
     sums = jnp.zeros((z.depth, z.width), jnp.float32)
     for y in range(z.planes):
         solid = z.solid_tile(mask_ref, y) > 0.5
-        f = [moved(i, y, z.tile(h_ref, i, y), sides, near_slot.get) for i in range(Q)]
+        f = [moved(i, y, z.tile(h_ref, i, y), sides, upward.index) for i in range(Q)]
         post, jx, moment_xy = collide(f, solid)
         here = pl.ds(y * z.depth, z.depth)
         for i in range(Q):
@@ -484,26 +570,68 @@
     acc_copy.wait()
 
 
+def direct_kernel(z, g_ref, out_hbm, sems):
+    inner = (z.planes - 1) * z.depth
+    copies = []
+    for k, i in enumerate(straight):
+        source, target = g_ref.at[i], out_hbm.at[i]
+        if CY[i] == 1:
+            source, target = source.at[pl.ds(0, inner), :], target.at[pl.ds(z.depth, inner), :]
+        elif CY[i] == -1:
+            source, target = source.at[pl.ds(z.depth, inner), :], target.at[pl.ds(0, inner), :]
+        copies.append(pltpu.make_async_copy(source, target, sems.at[k]))
+        copies[-1].start()
+    for copy in copies:
+        copy.wait()
+
+
 def fourth_kernel(z, whole_hbm, part_hbm, g_ref, own_ref, *refs):
-    gets, (out_hbm, profile_hbm) = refs[: z.count - 1], refs[z.count - 1 : z.count + 1]
-    scratch = refs[z.count + 1 :]
-    scalars = fetch_scalars(whole_hbm, part_hbm, *scratch[3:6])
-    out_ref, profile_ref, sems = scratch[6:]
+    gets, (_, out_hbm, profile_hbm) = refs[: z.count - 1], refs[z.count - 1 : z.count + 2]
+    tops, bottoms, edges, whole_ref, part_ref, pair_sems, out_ref, profile_ref, sems = refs[z.count + 2 :]
+    scalars = fetch_scalars(whole_hbm, part_hbm, whole_ref, part_ref, pair_sems)
     terms = [own_ref[...]] + [gets[d - 1][z.slots(d)] for d in range(1, z.count)]
     while len(terms) > 1:
         terms = [terms[k] + terms[k + 1] for k in range(0, len(terms), 2)]
     for k in range(2):
         profile_ref[k] = terms[0][:, k * z.planes : (k + 1) * z.planes]
-    copies = [pltpu.make_async_copy(profile_ref, profile_hbm, sems.at[CHUNKS])]
-    copies[0].start()
+    copies = []
+
+    def send(source, target):
+        copies.append(pltpu.make_async_copy(source, target, sems.at[len(copies)]))
+        copies[-1].start()
+
+    send(profile_ref, profile_hbm)
+    left, right = fill_tables(z, g_ref, gets, tops, bottoms, edges)
+    group = z.planes // CHUNKS
+
+    def interior(k):
+        for i in slanted:
+            for y in range(k * group, (k + 1) * group):
+                if 0 <= y - CY[i] < z.planes:
+                    here = pl.ds(y * z.depth, z.depth)
+                    out_ref[i, here, :] = moved_x(z, g_ref, i, y - CY[i], left, right)
 
     def finish(k):
-        group = z.planes // CHUNKS * z.depth
-        part = (slice(None), pl.ds(k * group, group), slice(None))
-        copies.append(pltpu.make_async_copy(out_ref.at[part], out_hbm.at[part], sems.at[k]))
-        copies[-1].start()
-
-    shift_xy(z, 1, scalars, g_ref, gets, out_ref, *scratch[:3], finish)
+        here = pl.ds(k * group * z.depth, group * z.depth)
+        for first, last in SPANS:
+            part = (pl.ds(first, last - first), here, slice(None))
+            send(out_ref.at[part], out_hbm.at[part])
+
+    for k in range(1, CHUNKS - 1):
+        interior(k)
+        finish(k)
+    whole, part = (value[1] for value in scalars())
+
+    def put(i, value):
+        here = pl.ds(0 if CY[i] == 1 else (z.planes - 1) * z.depth, z.depth)
+        out_ref[i, here, :] = value
+        if CX[i] == 0:
+            send(out_ref.at[i, here, :], out_hbm.at[i, here, :])
+
+    sliding(z, whole, part, tops, bottoms, edges, put)
+    for k in (0, CHUNKS - 1):
+        interior(k)
+        finish(k)
     for copy in copies:
         copy.wait()
 
@@ -519,7 +647,7 @@
     outside = pl.BlockSpec(memory_space=pl.ANY)
     cells = f32(Q, planes * depth, width)
     fields = f32(2, planes * depth, width)
-    halo = f32(Q + 1, planes, width)
+    halo = f32(SLOTS, planes, width)
     shifts = [pltpu.VMEM((count, len(rising), depth, width), jnp.float32)] * 2
     shifts.append(pltpu.VMEM((count, depth, width), jnp.float32))
     pair = pltpu.SMEM(shift_whole.shape, jnp.int32)
@@ -531,7 +659,7 @@
     def buffers(more):
         return [f32(z.slots(d) + more, depth, width) for d in range(1, count)]
 
-    def call(body, ins, outs, scratch=(), direct=()):
+    def call(body, ins, outs, scratch=(), direct=(), alias=None):
         specs = [outside if k in direct else vmem for k in range(len(outs))]
         return pl.pallas_call(
             functools.partial(body, z),
@@ -539,8 +667,8 @@
             in_specs=ins,
             out_specs=specs,
             scratch_shapes=list(scratch),
+            input_output_aliases=alias or {},
             compiler_params=pltpu.CompilerParams(vmem_limit_bytes=8 << 20),
-            name=body.__name__,
         )
 
     def swap_x(values):
@@ -560,17 +688,22 @@
         [pair, cells, pltpu.VMEM(solid_blocks.shape, jnp.int32), sems(CHUNKS + 2)],
     )(shift_whole, pop, solid_blocks)
     gets = swap_x(sends)
-    h, inner, outer = call(
-        second_kernel, [outside] * 2 + [vmem] * (1 + count), [cells, halo, halo], shifts
+    walls, both = f32(2 * len(rising), depth, width), f32(2, depth, width)
+    inner, outer, wall, side = call(
+        second_kernel,
+        [outside] * 2 + [vmem] * (1 + count),
+        [halo, halo, walls, both],
+        shifts + [f32(2, Q, planes, width)],
     )(shift_whole, shift_frac, *keep(post, mask, *gets))
     outer = lax.ppermute(outer, "gz", across)
     inner = lax.ppermute(inner, "gz", pairs)
+    (h,) = call(bulk_kernel, [vmem] * 3, [cells])(*keep(post, wall, side))
     g, acc, own, *sends = call(
         third_kernel,
         [outside] + [vmem] * 5,
         [cells, hbm(fields), f32(depth, width)] + buffers(1),
         [
-            pltpu.VMEM((2, Q + 1, planes, width), jnp.float32),
+            pltpu.VMEM((2, SLOTS, planes, width), jnp.float32),
             pltpu.VMEM((2, len(upward), planes, width), jnp.float32),
             fields,
             pair,
@@ -579,13 +712,16 @@
         [1],
     )(shift_whole, *keep(h, inner, outer, mask, old))
     gets = swap_x(sends)
+    (out,) = call(direct_kernel, [vmem], [hbm(cells)], [sems(len(straight))], [0])(*keep(g))
+    moves = 1 + len(SPANS) * CHUNKS + sum(CX[i] == 0 for i in rising + falling)
     out, profile = call(
         fourth_kernel,
-        [outside] * 2 + [vmem] * (1 + count),
+        [outside] * 2 + [vmem] * (1 + count) + [outside],
         [hbm(cells), hbm(f32(2, depth, planes))],
-        shifts + [cells, f32(2, depth, planes), sems(CHUNKS + 1)],
+        shifts + [cells, f32(2, depth, planes), sems(moves)],
         [0, 1],
-    )(shift_whole, shift_frac, *keep(g, own, *gets))
+        {3 + count: 0},
+    )(shift_whole, shift_frac, *keep(g, own, *gets), out)
     return (
         out.reshape(pop_ratio.shape),
         acc.reshape(2, planes, depth, width),

time: 30 us -> 29 us (0.967)
  waiting for transfers between devices: 11 us -> 8.86 us
  Pallas kernels: 6.2 us -> 7.33 us
    ppermute x1, waiting for transfers between devices: 4.01 us -> 2.73 us  [local(): outer = lax.ppermute(outer, 'gz', across)]
    pallas_call x2 -> x4, Pallas kernels: 3.21 us -> 4.27 us  [the longest x1 2.01 us: local(): call(fourth_kernel, [outside] * 2 + [vmem] * (1 + count) + [outside], [hb...]
    ppermute x6, waiting for transfers between devices: 7 us -> 6.13 us  [swap_x(): lax.ppermute(values[d - 1], 'gx', [(i, i ^ d) for i in range(count)])]
  transfers between devices with their start and end apart: 8 -> 8, of which waited for: 5 -> 4; matrix products, arithmetic and copies ran while one was open for 0% -> 0% of each run, Pallas kernels for 0% -> 4%
where the time goes in v3:
time: 29 us; the launch traced here: 28.8 us
  starting transfers between devices  11.9 us (41%)
  waiting for transfers between devices  8.86 us (31%)
  Pallas kernels  7.33 us (25%)
  between operations  0.69 us (2%)
    ppermute x6, starting transfers between devices, swap_x(): lax.ppermute(values[d - 1], 'gx', [(i, i ^ d) for i in range(count)])  8.15 us
    ppermute x6, waiting for transfers between devices, swap_x(): lax.ppermute(values[d - 1], 'gx', [(i, i ^ d) for i in range(count)])  6.13 us
    ppermute x1, starting transfers between devices, local(): outer = lax.ppermute(outer, 'gz', across)  3.7 us
    ppermute x1, waiting for transfers between devices, local(): outer = lax.ppermute(outer, 'gz', across)  2.73 us
    pallas_call x1, Pallas kernels, local(): call(fourth_kernel, [outside] * 2 + [vmem] * (1 + count) + [outside], [hb...  2.01 us
    pallas_call x1, Pallas kernels, local(): call(first_kernel, [outside] * 3, [cells, fields, f32(planes // BLOCK * z...  1.91 us
    pallas_call x1, Pallas kernels, local(): call(third_kernel, [outside] + [vmem] * 5, [cells, hbm(fields), f32(depth...  1.15 us
    pallas_call x1, Pallas kernels, local(): call(second_kernel, [outside] * 2 + [vmem] * (1 + count), [halo, halo, wa...  1 us
  transfers between devices with their start and end apart: 8, of which 4 were waited for; matrix products, arithmetic and copies ran while one was open for 0% of the time, Pallas kernels for 4%

profile of v3, /device:TPU:0, one launch (start us, length us, event | category | flops | bytes accessed | tf_op | source)
XLA Modules:
  0.0 28.8 jit_solution(4991614585577558832)
XLA Ops:
  0.6 1.9 %shard_map.67 = (f32[19,128,128]{2,1,0:T(8,128)S(1)}, f32[2,128,128]{2,1,0:T(8,128)S(1)}, f32[8,128]{1,0:T(8,128)S(1)}, f32[6,8,128]{2,1,0:T(8,128)S(1)}, f32[11...) custom-call(s32[2]{0:T(128)} %whole_hbm.7, f32[19,128,128]{2,1,0:T(8,128)} %bitcast.5, s32[4,2,32]{2,1,0:T(2,128)} %solid_hbm.1), custom_call_target="tpu_custom_call" | custom-call | tf_op jit(solution)/shard_map/pallas_call | solution.py:684
  2.5 3.1 %collective-permute-start.1 = (f32[11,8,128]{2,1,0:T(8,128)S(1)}, f32[11,8,128]{2,1,0:T(8,128)S(1)}, u32[]{:S(2)}, u32[]{:S(2)}) collective-permute-start(f32[11,8,128]{2,1,0:T(8,128)S(1)} %get-tuple-element.24), channel_id=1, source_target_pairs={{0,16},{8,24},{16,0},{24,8},{1,17},{9,25},{17,1},{25,9},{2,18},{10... | collective-permute-start | bytes 135176 | tf_op jit(solution)/shard_map/ppermute | solution.py:676
  5.6 1.5 %collective-permute-start = (f32[6,8,128]{2,1,0:T(8,128)S(1)}, f32[6,8,128]{2,1,0:T(8,128)S(1)}, u32[]{:S(2)}, u32[]{:S(2)}) collective-permute-start(f32[6,8,128]{2,1,0:T(8,128)S(1)} %get-tuple-element.23), channel_id=1, source_target_pairs={{0,8},{8,0},{16,24},{24,16},{1,9},{9,1},{17,25},{25,17},{2,10},{10... | collective-permute-start | bytes 73736 | tf_op jit(solution)/shard_map/ppermute | solution.py:676
  7.1 0.0 collective-permute-start.2
  7.2 2.3 %collective-permute-done.refs_0_ = f32[6,8,128]{2,1,0:T(8,128)S(1)} collective-permute-done((f32[6,8,128]{2,1,0:T(8,128)S(1)}, f32[6,8,128]{2,1,0:T(8,128)S(1)}, u32[]{:S(2)}, u32[]{:S(2)}) %collective-permute-start) | collective-permute-done | bytes 24608 | tf_op jit(solution)/shard_map/ppermute | solution.py:676
  9.4 2.4 %collective-permute-done.2.refs_2_ = f32[6,8,128]{2,1,0:T(8,128)S(1)} collective-permute-done((f32[6,8,128]{2,1,0:T(8,128)S(1)}, f32[6,8,128]{2,1,0:T(8,128)S(1)}, u32[]{:S(2)}, u32[]{:S(2)}) %collective-permute-start.2) | collective-permute-done | bytes 24608 | tf_op jit(solution)/shard_map/ppermute | solution.py:676
  11.8 0.0 collective-permute-done.1.refs_1_
  11.8 1.0 %shard_map.68 = (f32[15,16,128]{2,1,0:T(8,128)S(1)}, f32[15,16,128]{2,1,0:T(8,128)S(1)}, f32[10,8,128]{2,1,0:T(8,128)S(1)}, f32[2,8,128]{2,1,0:T(8,128)S(1)}) custom-call(s32[2]{0:T(128)} %whole_hbm.7, s32[2]{0:T(128)} %part_hbm.3, f32[19,128,128]{2,1,0:T(8,128)S(1)} %get-tuple-element.21.post_ref, f32[8,128]{1,0:T(8,128)S(1)} %get-tuple-element.22.mask_ref, ...), custom_call_target="tpu_custom_call" | custom-call | tf_op jit(solution)/shard_map/pallas_call | solution.py:692
  12.8 0.1 collective-permute-start.3
  12.9 3.7 %collective-permute-start.4 = (f32[15,16,128]{2,1,0:T(8,128)S(1)}, f32[15,16,128]{2,1,0:T(8,128)S(1)}, u32[]{:S(2)}, u32[]{:S(2)}) collective-permute-start(f32[15,16,128]{2,1,0:T(8,128)S(1)} %get-tuple-element.29), channel_id=1, source_target_pairs={{0,7},{1,2},{2,1},{3,4},{4,3},{5,6},{6,5},{7,0},{8,15},{9,10},{10,... | collective-permute-start | bytes 368648 | tf_op jit(solution)/shard_map/ppermute | solution.py:698
  16.6 0.4 %shard_map.69.h_ref = f32[19,128,128]{2,1,0:T(8,128)S(1)} custom-call(f32[19,128,128]{2,1,0:T(8,128)S(1)} %get-tuple-element.21.post_ref, f32[10,8,128]{2,1,0:T(8,128)S(1)} %get-tuple-element.26.wall_ref, f32[2,8,128]{2,1,0:T(8,128)S(1)} %get-tuple-element.27.side_ref), custom_call_target="tpu_custom_call" | custom-call | tf_op jit(solution)/shard_map/pallas_call | solution.py:700
  17.0 0.0 collective-permute-done.3.inner_ref
  17.0 2.7 %collective-permute-done.4.outer_ref = f32[15,16,128]{2,1,0:T(8,128)S(1)} collective-permute-done((f32[15,16,128]{2,1,0:T(8,128)S(1)}, f32[15,16,128]{2,1,0:T(8,128)S(1)}, u32[]{:S(2)}, u32[]{:S(2)}) %collective-permute-start.4) | collective-permute-done | bytes 122912 | tf_op jit(solution)/shard_map/ppermute | solution.py:698
  19.8 1.2 %shard_map.70 = (f32[19,128,128]{2,1,0:T(8,128)S(1)}, f32[2,128,128]{2,1,0:T(8,128)}, f32[8,128]{1,0:T(8,128)S(1)}, f32[7,8,128]{2,1,0:T(8,128)S(1)}, f32[12,8,1...) custom-call(s32[2]{0:T(128)} %whole_hbm.7, f32[19,128,128]{2,1,0:T(8,128)S(1)} %shard_map.69.h_ref, ...), custom_call_target="tpu_custom_call" | custom-call | tf_op jit(solution)/shard_map/pallas_call | solution.py:701
  20.9 0.6 %collective-permute-start.6 = (f32[12,8,128]{2,1,0:T(8,128)S(1)}, f32[12,8,128]{2,1,0:T(8,128)S(1)}, u32[]{:S(2)}, u32[]{:S(2)}) collective-permute-start(f32[12,8,128]{2,1,0:T(8,128)S(1)} %get-tuple-element.34), channel_id=1, source_target_pairs={{0,16},{8,24},{16,0},{24,8},{1,17},{9,25},{17,1},{25,9},{2,18},{10... | collective-permute-start | bytes 147464 | tf_op jit(solution)/shard_map/ppermute | solution.py:676
  21.5 0.5 %collective-permute-start.5 = (f32[7,8,128]{2,1,0:T(8,128)S(1)}, f32[7,8,128]{2,1,0:T(8,128)S(1)}, u32[]{:S(2)}, u32[]{:S(2)}) collective-permute-start(f32[7,8,128]{2,1,0:T(8,128)S(1)} %get-tuple-element.33), channel_id=1, source_target_pairs={{0,8},{8,0},{16,24},{24,16},{1,9},{9,1},{17,25},{25,17},{2,10},{10... | collective-permute-start | bytes 86024 | tf_op jit(solution)/shard_map/ppermute | solution.py:676
  22.0 2.4 %collective-permute-start.7 = (f32[7,8,128]{2,1,0:T(8,128)S(1)}, f32[7,8,128]{2,1,0:T(8,128)S(1)}, u32[]{:S(2)}, u32[]{:S(2)}) collective-permute-start(f32[7,8,128]{2,1,0:T(8,128)S(1)} %get-tuple-element.35), channel_id=1, source_target_pairs={{0,24},{8,16},{16,8},{24,0},{1,25},{9,17},{17,9},{25,1},{2,26},{10... | collective-permute-start | bytes 86024 | tf_op jit(solution)/shard_map/ppermute | solution.py:676
  24.5 0.9 %shard_map.71.refs_3_ = f32[19,128,128]{2,1,0:T(8,128)} custom-call(f32[19,128,128]{2,1,0:T(8,128)S(1)} %get-tuple-element.31.g_ref), custom_call_target="tpu_custom_call" | custom-call | tf_op jit(solution)/shard_map/pallas_call | solution.py:715
  25.3 0.0 collective-permute-done.5.refs_0_
  25.4 1.4 %collective-permute-done.7.refs_2_ = f32[7,8,128]{2,1,0:T(8,128)S(1)} collective-permute-done((f32[7,8,128]{2,1,0:T(8,128)S(1)}, f32[7,8,128]{2,1,0:T(8,128)S(1)}, u32[]{:S(2)}, u32[]{:S(2)}) %collective-permute-start.7) | collective-permute-done | bytes 28704 | tf_op jit(solution)/shard_map/ppermute | solution.py:676
  26.8 0.0 collective-permute-done.6.refs_1_
  26.8 2.0 %shard_map.72 = (f32[19,128,128]{2,1,0:T(8,128)}, f32[2,8,16]{2,1,0:T(8,128)}) custom-call(s32[2]{0:T(128)} %whole_hbm.7, s32[2]{0:T(128)} %part_hbm.3, f32[19,128,128]{2,1,0:T(8,128)S(1)} %get-tuple-element.31.g_ref, f32[8,128]{1,0:T(8,128)S(1)} %get-tuple-element.32.own_ref, ...), custom_call_target="tpu_custom_call", output_to_operand_aliasing={{0}: (7, {})} | custom-call | tf_op jit(solution)/shard_map/pallas_call | solution.py:717
Async XLA Ops:
  2.5 9.3 %collective-permute-start.1 = (f32[11,8,128]{2,1,0:T(8,128)S(1)}, f32[11,8,128]{2,1,0:T(8,128)S(1)}, u32[]{:S(2)}, u32[]{:S(2)}) collective-permute-start(f32[11,8,128]{2,1,0:T(8,128)S(1)} %get-tuple-element.24), channel_id=1, source_target_pairs={{0,16},{8,24},{16,0},{24,8},{1,17},{9,25},{17,1},{25,9},{2,18},{10... | collective-permute-start | bytes 135176 | tf_op jit(solution)/shard_map/ppermute | solution.py:676
  5.6 3.8 %collective-permute-start = (f32[6,8,128]{2,1,0:T(8,128)S(1)}, f32[6,8,128]{2,1,0:T(8,128)S(1)}, u32[]{:S(2)}, u32[]{:S(2)}) collective-permute-start(f32[6,8,128]{2,1,0:T(8,128)S(1)} %get-tuple-element.23), channel_id=1, source_target_pairs={{0,8},{8,0},{16,24},{24,16},{1,9},{9,1},{17,25},{25,17},{2,10},{10... | collective-permute-start | bytes 73736 | tf_op jit(solution)/shard_map/ppermute | solution.py:676
  7.1 4.7 %collective-permute-start.2 = (f32[6,8,128]{2,1,0:T(8,128)S(1)}, f32[6,8,128]{2,1,0:T(8,128)S(1)}, u32[]{:S(2)}, u32[]{:S(2)}) collective-permute-start(f32[6,8,128]{2,1,0:T(8,128)S(1)} %get-tuple-element.25), channel_id=1, source_target_pairs={{0,24},{8,16},{16,8},{24,0},{1,25},{9,17},{17,9},{25,1},{2,26},{10... | collective-permute-start | bytes 73736 | tf_op jit(solution)/shard_map/ppermute | solution.py:676
  12.8 4.2 %collective-permute-start.3 = (f32[15,16,128]{2,1,0:T(8,128)S(1)}, f32[15,16,128]{2,1,0:T(8,128)S(1)}, u32[]{:S(2)}, u32[]{:S(2)}) collective-permute-start(f32[15,16,128]{2,1,0:T(8,128)S(1)} %get-tuple-element.28), channel_id=1, source_target_pairs={{0,1},{1,0},{2,3},{3,2},{4,5},{5,4},{6,7},{7,6},{8,9},{9,8},{10,11... | collective-permute-start | bytes 368648 | tf_op jit(solution)/shard_map/ppermute | solution.py:699
  12.9 6.8 %collective-permute-start.4 = (f32[15,16,128]{2,1,0:T(8,128)S(1)}, f32[15,16,128]{2,1,0:T(8,128)S(1)}, u32[]{:S(2)}, u32[]{:S(2)}) collective-permute-start(f32[15,16,128]{2,1,0:T(8,128)S(1)} %get-tuple-element.29), channel_id=1, source_target_pairs={{0,7},{1,2},{2,1},{3,4},{4,3},{5,6},{6,5},{7,0},{8,15},{9,10},{10,... | collective-permute-start | bytes 368648 | tf_op jit(solution)/shard_map/ppermute | solution.py:698
  20.9 5.9 %collective-permute-start.6 = (f32[12,8,128]{2,1,0:T(8,128)S(1)}, f32[12,8,128]{2,1,0:T(8,128)S(1)}, u32[]{:S(2)}, u32[]{:S(2)}) collective-permute-start(f32[12,8,128]{2,1,0:T(8,128)S(1)} %get-tuple-element.34), channel_id=1, source_target_pairs={{0,16},{8,24},{16,0},{24,8},{1,17},{9,25},{17,1},{25,9},{2,18},{10... | collective-permute-start | bytes 147464 | tf_op jit(solution)/shard_map/ppermute | solution.py:676
  21.5 3.9 %collective-permute-start.5 = (f32[7,8,128]{2,1,0:T(8,128)S(1)}, f32[7,8,128]{2,1,0:T(8,128)S(1)}, u32[]{:S(2)}, u32[]{:S(2)}) collective-permute-start(f32[7,8,128]{2,1,0:T(8,128)S(1)} %get-tuple-element.33), channel_id=1, source_target_pairs={{0,8},{8,0},{16,24},{24,16},{1,9},{9,1},{17,25},{25,17},{2,10},{10... | collective-permute-start | bytes 86024 | tf_op jit(solution)/shard_map/ppermute | solution.py:676
  22.0 4.8 %collective-permute-start.7 = (f32[7,8,128]{2,1,0:T(8,128)S(1)}, f32[7,8,128]{2,1,0:T(8,128)S(1)}, u32[]{:S(2)}, u32[]{:S(2)}) collective-permute-start(f32[7,8,128]{2,1,0:T(8,128)S(1)} %get-tuple-element.35), channel_id=1, source_target_pairs={{0,24},{8,16},{16,8},{24,0},{1,25},{9,17},{17,9},{25,1},{2,26},{10... | collective-permute-start | bytes 86024 | tf_op jit(solution)/shard_map/ppermute | solution.py:676

commit v4 on v3

--- a/solution.py
+++ b/solution.py
@@ -380,14 +380,15 @@
     return rising.index(i) if CY[i] == 1 else len(rising) + falling.index(i)
 
 
-def first_kernel(z, whole_hbm, pop_hbm, solid_hbm, post_ref, acc_ref, mask_ref, *refs):
-    sends, (whole_ref, pop_ref, solid_ref, sems) = refs[: z.count - 1], refs[z.count - 1 :]
+def first_kernel(z, whole_hbm, part_hbm, pop_hbm, solid_hbm, post_ref, acc_ref, mask_ref, info_ref, *refs):
+    sends, (whole_ref, part_ref, pop_ref, solid_ref, sems) = refs[: z.count - 1], refs[z.count - 1 :]
     group = z.planes // CHUNKS * z.depth
     copies = [pltpu.make_async_copy(solid_hbm, solid_ref, sems.at[CHUNKS])]
     for k in range(CHUNKS):
         part = (slice(None), pl.ds(k * group, group), slice(None))
         copies.append(pltpu.make_async_copy(pop_hbm.at[part], pop_ref.at[part], sems.at[k]))
     copies.append(pltpu.make_async_copy(whole_hbm, whole_ref, sems.at[CHUNKS + 1]))
+    copies.append(pltpu.make_async_copy(part_hbm, part_ref, sems.at[CHUNKS + 2]))
     for copy in copies:
         copy.start()
     copies[0].wait()
@@ -409,31 +410,25 @@
             post_ref[i, here, :] = post[i]
         acc_ref[0, here, :] = jnp.where(solid, 0.0, jx)
         acc_ref[1, here, :] = jnp.where(solid, 0.0, -(1.0 - 0.5 * visc_rate) * moment_xy)
+    copies[-2].wait()
     copies[-1].wait()
+    for step in range(whole_ref.shape[0]):
+        for k, ref in enumerate((whole_ref, part_ref)):
+            value = ref[step].astype(jnp.float32)
+            info_ref[pl.ds(2 * step + k, 1), :] = jnp.full((1, z.width), value, jnp.float32)
     pack_x(z, whole_ref[0], post_ref, sends)
 
 
-def fetch_scalars(whole_hbm, part_hbm, whole_ref, part_ref, sems):
-    copies = [
-        pltpu.make_async_copy(whole_hbm, whole_ref, sems.at[0]),
-        pltpu.make_async_copy(part_hbm, part_ref, sems.at[1]),
-    ]
-    for copy in copies:
-        copy.start()
-
-    def scalars():
-        for copy in copies:
-            copy.wait()
-        return whole_ref, part_ref
-
-    return scalars
-
-
-def second_kernel(z, whole_hbm, part_hbm, post_ref, mask_ref, *refs):
+def shift_of(info_ref, step):
+    values = [jnp.max(info_ref[2 * step + k : 2 * step + k + 1, :]) for k in range(2)]
+    return [value.astype(jnp.int32) for value in values]
+
+
+def second_kernel(z, info_ref, post_ref, mask_ref, *refs):
     gets, outs = refs[: z.count - 1], refs[z.count - 1 : z.count + 3]
     inner_ref, outer_ref, wall_ref, side_ref = outs
-    tops, bottoms, edges, whole_ref, part_ref, sems, rows_ref = refs[z.count + 3 :]
-    scalars = fetch_scalars(whole_hbm, part_hbm, whole_ref, part_ref, sems)
+    tops, bottoms, edges, rows_ref = refs[z.count + 3 :]
+    whole, part = shift_of(info_ref, 0)
     left, right = fill_tables(z, post_ref, gets, tops, bottoms, edges)
     side_ref[0], side_ref[1] = left, right
     columns = {1: left.T, -1: right.T}
@@ -467,7 +462,6 @@
             if (CY[i] == 0) == still:
                 rows_ref[side, k] = line(i, row)
         if still:
-            whole, part = (value[0] for value in scalars())
 
             def put(i, value):
                 wall_ref[wall_slot(i)] = value
@@ -513,12 +507,10 @@
                 h_ref[i, here, :] = wall_ref[wall_slot(i)]
 
 
-def third_kernel(z, whole_hbm, h_ref, inner_ref, outer_ref, mask_ref, old_ref, *refs):
-    (g_ref, acc_hbm, part_ref), sends = refs[:3], refs[3 : 2 + z.count]
-    sides, extra, acc_ref, whole_ref, sems = refs[2 + z.count :]
-    whole_copy = pltpu.make_async_copy(whole_hbm, whole_ref, sems.at[0])
-    whole_copy.start()
-    acc_copy = pltpu.make_async_copy(acc_ref, acc_hbm, sems.at[1])
+def third_kernel(z, info_ref, h_ref, inner_ref, outer_ref, mask_ref, old_ref, *refs):
+    (g_ref, acc_ref, part_ref), sends = refs[:3], refs[3 : 2 + z.count]
+    sides, extra = refs[2 + z.count :]
+    whole, _ = shift_of(info_ref, 1)
     even = lax.rem(lax.axis_index("gz"), 2) == 0
     sides[jnp.where(even, 1, 0)] = inner_ref[...]
     sides[jnp.where(even, 0, 1)] = outer_ref[...]
@@ -563,16 +555,14 @@
             acc_ref[k, here, :] = value
             total = z.spread(jnp.sum(value, axis=1, keepdims=True))
             sums = jnp.where(lanes == k * z.planes + y, total, sums)
-    acc_copy.start()
     part_ref[...] = sums
-    whole_copy.wait()
-    pack_x(z, whole_ref[1], g_ref, sends, sums)
-    acc_copy.wait()
-
-
-def direct_kernel(z, g_ref, out_hbm, sems):
+    pack_x(z, whole, g_ref, sends, sums)
+
+
+def direct_kernel(z, g_ref, acc_ref, out_hbm, acc_hbm, sems):
     inner = (z.planes - 1) * z.depth
-    copies = []
+    copies = [pltpu.make_async_copy(acc_ref, acc_hbm, sems.at[len(straight)])]
+    copies[0].start()
     for k, i in enumerate(straight):
         source, target = g_ref.at[i], out_hbm.at[i]
         if CY[i] == 1:
@@ -585,10 +575,10 @@
         copy.wait()
 
 
-def fourth_kernel(z, whole_hbm, part_hbm, g_ref, own_ref, *refs):
+def fourth_kernel(z, info_ref, g_ref, own_ref, *refs):
     gets, (_, out_hbm, profile_hbm) = refs[: z.count - 1], refs[z.count - 1 : z.count + 2]
-    tops, bottoms, edges, whole_ref, part_ref, pair_sems, out_ref, profile_ref, sems = refs[z.count + 2 :]
-    scalars = fetch_scalars(whole_hbm, part_hbm, whole_ref, part_ref, pair_sems)
+    tops, bottoms, edges, out_ref, profile_ref, sems = refs[z.count + 2 :]
+    whole, part = shift_of(info_ref, 1)
     terms = [own_ref[...]] + [gets[d - 1][z.slots(d)] for d in range(1, z.count)]
     while len(terms) > 1:
         terms = [terms[k] + terms[k + 1] for k in range(0, len(terms), 2)]
@@ -620,7 +610,6 @@
     for k in range(1, CHUNKS - 1):
         interior(k)
         finish(k)
-    whole, part = (value[1] for value in scalars())
 
     def put(i, value):
         here = pl.ds(0 if CY[i] == 1 else (z.planes - 1) * z.depth, z.depth)
@@ -652,7 +641,6 @@
     shifts.append(pltpu.VMEM((count, depth, width), jnp.float32))
     pair = pltpu.SMEM(shift_whole.shape, jnp.int32)
     sems = lambda number: pltpu.SemaphoreType.DMA((number,))
-    shifts += [pair, pair, sems(2)]
     outer_keep = lambda *values: [pltpu.with_memory_space_constraint(v, pltpu.HBM) for v in values]
     shift_whole, shift_frac, solid_blocks = outer_keep(shift_whole, shift_frac, solid_blocks)
 
@@ -681,47 +669,45 @@
     across = [(i, (i - 1 if i % 2 == 0 else i + 1) % ranks) for i in range(ranks)]
 
     (pop,) = outer_keep(pop_ratio.reshape(cells.shape))
-    post, old, mask, *sends = call(
+    post, old, mask, info, *sends = call(
         first_kernel,
-        [outside] * 3,
-        [cells, fields, f32(planes // BLOCK * z.deep, width)] + buffers(0),
-        [pair, cells, pltpu.VMEM(solid_blocks.shape, jnp.int32), sems(CHUNKS + 2)],
-    )(shift_whole, pop, solid_blocks)
+        [outside] * 4,
+        [cells, fields, f32(planes // BLOCK * z.deep, width), f32(2 * shift_whole.shape[0], width)] + buffers(0),
+        [pair, pair, cells, pltpu.VMEM(solid_blocks.shape, jnp.int32), sems(CHUNKS + 3)],
+    )(shift_whole, shift_frac, pop, solid_blocks)
     gets = swap_x(sends)
     walls, both = f32(2 * len(rising), depth, width), f32(2, depth, width)
     inner, outer, wall, side = call(
         second_kernel,
-        [outside] * 2 + [vmem] * (1 + count),
+        [vmem] * (2 + count),
         [halo, halo, walls, both],
         shifts + [f32(2, Q, planes, width)],
-    )(shift_whole, shift_frac, *keep(post, mask, *gets))
+    )(*keep(info, post, mask, *gets))
     outer = lax.ppermute(outer, "gz", across)
     inner = lax.ppermute(inner, "gz", pairs)
     (h,) = call(bulk_kernel, [vmem] * 3, [cells])(*keep(post, wall, side))
     g, acc, own, *sends = call(
         third_kernel,
-        [outside] + [vmem] * 5,
-        [cells, hbm(fields), f32(depth, width)] + buffers(1),
+        [vmem] * 6,
+        [cells, fields, f32(depth, width)] + buffers(1),
         [
             pltpu.VMEM((2, SLOTS, planes, width), jnp.float32),
             pltpu.VMEM((2, len(upward), planes, width), jnp.float32),
-            fields,
-            pair,
-            sems(2),
         ],
-        [1],
-    )(shift_whole, *keep(h, inner, outer, mask, old))
+    )(*keep(info, h, inner, outer, mask, old))
     gets = swap_x(sends)
-    (out,) = call(direct_kernel, [vmem], [hbm(cells)], [sems(len(straight))], [0])(*keep(g))
+    out, acc = call(
+        direct_kernel, [vmem] * 2, [hbm(cells), hbm(fields)], [sems(len(straight) + 1)], [0, 1]
+    )(*keep(g, acc))
     moves = 1 + len(SPANS) * CHUNKS + sum(CX[i] == 0 for i in rising + falling)
     out, profile = call(
         fourth_kernel,
-        [outside] * 2 + [vmem] * (1 + count) + [outside],
+        [vmem] * (2 + count) + [outside],
         [hbm(cells), hbm(f32(2, depth, planes))],
         shifts + [cells, f32(2, depth, planes), sems(moves)],
         [0, 1],
-        {3 + count: 0},
-    )(shift_whole, shift_frac, *keep(g, own, *gets), out)
+        {2 + count: 0},
+    )(*keep(info, g, own, *gets), out)
     return (
         out.reshape(pop_ratio.shape),
         acc.reshape(2, planes, depth, width),

time: 29 us -> 27.8 us (0.959)
  Pallas kernels: 7.33 us -> 6.16 us
    pallas_call x5, Pallas kernels: 6.94 us -> 5.77 us  [the longest x1 1.93 us: local(): call(first_kernel, [outside] * 4, [cells, fields, f32(planes // BLOCK * z...]
  transfers between devices with their start and end apart: 8 -> 8, of which waited for: 4 -> 4; matrix products, arithmetic and copies ran while one was open for 0% -> 0% of each run, Pallas kernels for 4% -> 5%
where the time goes in v4:
time: 27.8 us; the launch traced here: 27.6 us
  starting transfers between devices  11.9 us (43%)
  waiting for transfers between devices  8.8 us (32%)
  Pallas kernels  6.16 us (22%)
  between operations  0.7 us (3%)
    ppermute x6, starting transfers between devices, swap_x(): lax.ppermute(values[d - 1], 'gx', [(i, i ^ d) for i in range(count)])  8.15 us
    ppermute x6, waiting for transfers between devices, swap_x(): lax.ppermute(values[d - 1], 'gx', [(i, i ^ d) for i in range(count)])  6.07 us
    ppermute x1, starting transfers between devices, local(): outer = lax.ppermute(outer, 'gz', across)  3.7 us
    ppermute x1, waiting for transfers between devices, local(): outer = lax.ppermute(outer, 'gz', across)  2.73 us
    pallas_call x1, Pallas kernels, local(): call(first_kernel, [outside] * 4, [cells, fields, f32(planes // BLOCK * z...  1.93 us
    pallas_call x1, Pallas kernels, local(): call(fourth_kernel, [vmem] * (2 + count) + [outside], [hbm(cells), hbm(f3...  1.52 us
    pallas_call x1, Pallas kernels, local(): call(third_kernel, [vmem] * 6, [cells, fields, f32(depth, width)] + buffe...  1 us
    pallas_call x1, Pallas kernels, local(): call(direct_kernel, [vmem] * 2, [hbm(cells), hbm(fields)], [sems(len(stra...  0.92 us
  transfers between devices with their start and end apart: 8, of which 4 were waited for; matrix products, arithmetic and copies ran while one was open for 0% of the time, Pallas kernels for 5%

profile of v4, /device:TPU:0, one launch (start us, length us, event | category | flops | bytes accessed | tf_op | source)
XLA Modules:
  0.0 27.6 jit_solution(9080675064659907915)
XLA Ops:
  0.6 1.9 %shard_map.67 = (f32[19,128,128]{2,1,0:T(8,128)S(1)}, f32[2,128,128]{2,1,0:T(8,128)S(1)}, f32[8,128]{1,0:T(8,128)S(1)}, f32[4,128]{1,0:T(4,128)S(1)}, f32[6,8,12...) custom-call(s32[2]{0:T(128)} %whole_hbm.1, s32[2]{0:T(128)} %part_hbm.1, ...), custom_call_target="tpu_custom_call" | custom-call | tf_op jit(solution)/shard_map/pallas_call | solution.py:672
  2.6 3.1 %collective-permute-start.1 = (f32[11,8,128]{2,1,0:T(8,128)S(1)}, f32[11,8,128]{2,1,0:T(8,128)S(1)}, u32[]{:S(2)}, u32[]{:S(2)}) collective-permute-start(f32[11,8,128]{2,1,0:T(8,128)S(1)} %get-tuple-element.28), channel_id=1, source_target_pairs={{0,16},{8,24},{16,0},{24,8},{1,17},{9,25},{17,1},{25,9},{2,18},{10... | collective-permute-start | bytes 135176 | tf_op jit(solution)/shard_map/ppermute | solution.py:664
  5.6 1.5 %collective-permute-start = (f32[6,8,128]{2,1,0:T(8,128)S(1)}, f32[6,8,128]{2,1,0:T(8,128)S(1)}, u32[]{:S(2)}, u32[]{:S(2)}) collective-permute-start(f32[6,8,128]{2,1,0:T(8,128)S(1)} %get-tuple-element.27), channel_id=1, source_target_pairs={{0,8},{8,0},{16,24},{24,16},{1,9},{9,1},{17,25},{25,17},{2,10},{10... | collective-permute-start | bytes 73736 | tf_op jit(solution)/shard_map/ppermute | solution.py:664
  7.1 0.0 collective-permute-start.2
  7.2 2.3 %collective-permute-done.refs_0_ = f32[6,8,128]{2,1,0:T(8,128)S(1)} collective-permute-done((f32[6,8,128]{2,1,0:T(8,128)S(1)}, f32[6,8,128]{2,1,0:T(8,128)S(1)}, u32[]{:S(2)}, u32[]{:S(2)}) %collective-permute-start) | collective-permute-done | bytes 24608 | tf_op jit(solution)/shard_map/ppermute | solution.py:664
  9.5 2.4 %collective-permute-done.2.refs_2_ = f32[6,8,128]{2,1,0:T(8,128)S(1)} collective-permute-done((f32[6,8,128]{2,1,0:T(8,128)S(1)}, f32[6,8,128]{2,1,0:T(8,128)S(1)}, u32[]{:S(2)}, u32[]{:S(2)}) %collective-permute-start.2) | collective-permute-done | bytes 24608 | tf_op jit(solution)/shard_map/ppermute | solution.py:664
  11.8 0.0 collective-permute-done.1.refs_1_
  11.8 0.4 %shard_map.68 = (f32[15,16,128]{2,1,0:T(8,128)S(1)}, f32[15,16,128]{2,1,0:T(8,128)S(1)}, f32[10,8,128]{2,1,0:T(8,128)S(1)}, f32[2,8,128]{2,1,0:T(8,128)S(1)}) custom-call(f32[4,128]{1,0:T(4,128)S(1)} %get-tuple-element.24.info_ref, f32[19,128,128]{2,1,0:T(8,128)S(1)} %get-tuple-element.25.post_ref, f32[8,128]{1,0:T(8,128)S(1)} %get-tuple-element.26.mask_ref, ...), custom_call_target="tpu_custom_call" | custom-call | tf_op jit(solution)/shard_map/pallas_call | solution.py:680
  12.3 0.1 collective-permute-start.3
  12.3 3.7 %collective-permute-start.4 = (f32[15,16,128]{2,1,0:T(8,128)S(1)}, f32[15,16,128]{2,1,0:T(8,128)S(1)}, u32[]{:S(2)}, u32[]{:S(2)}) collective-permute-start(f32[15,16,128]{2,1,0:T(8,128)S(1)} %get-tuple-element.33), channel_id=1, source_target_pairs={{0,7},{1,2},{2,1},{3,4},{4,3},{5,6},{6,5},{7,0},{8,15},{9,10},{10,... | collective-permute-start | bytes 368648 | tf_op jit(solution)/shard_map/ppermute | solution.py:686
  16.0 0.4 %shard_map.69.h_ref = f32[19,128,128]{2,1,0:T(8,128)S(1)} custom-call(f32[19,128,128]{2,1,0:T(8,128)S(1)} %get-tuple-element.25.post_ref, f32[10,8,128]{2,1,0:T(8,128)S(1)} %get-tuple-element.30.wall_ref, f32[2,8,128]{2,1,0:T(8,128)S(1)} %get-tuple-element.31.side_ref), custom_call_target="tpu_custom_call" | custom-call | tf_op jit(solution)/shard_map/pallas_call | solution.py:688
  16.4 0.0 collective-permute-done.3.inner_ref
  16.5 2.7 %collective-permute-done.4.outer_ref = f32[15,16,128]{2,1,0:T(8,128)S(1)} collective-permute-done((f32[15,16,128]{2,1,0:T(8,128)S(1)}, f32[15,16,128]{2,1,0:T(8,128)S(1)}, u32[]{:S(2)}, u32[]{:S(2)}) %collective-permute-start.4) | collective-permute-done | bytes 122912 | tf_op jit(solution)/shard_map/ppermute | solution.py:686
  19.2 1.0 %shard_map.70 = (f32[19,128,128]{2,1,0:T(8,128)S(1)}, f32[2,128,128]{2,1,0:T(8,128)S(1)}, f32[8,128]{1,0:T(8,128)S(1)}, f32[7,8,128]{2,1,0:T(8,128)S(1)}, f32[12...) custom-call(f32[4,128]{1,0:T(4,128)S(1)} %get-tuple-element.24.info_ref, f32[19,128,128]{2,1,0:T(8,128)S(1)} %shard_map.69.h_ref, ...), custom_call_target="tpu_custom_call" | custom-call | tf_op jit(solution)/shard_map/pallas_call | solution.py:689
  20.2 0.6 %collective-permute-start.6 = (f32[12,8,128]{2,1,0:T(8,128)S(1)}, f32[12,8,128]{2,1,0:T(8,128)S(1)}, u32[]{:S(2)}, u32[]{:S(2)}) collective-permute-start(f32[12,8,128]{2,1,0:T(8,128)S(1)} %get-tuple-element.38), channel_id=1, source_target_pairs={{0,16},{8,24},{16,0},{24,8},{1,17},{9,25},{17,1},{25,9},{2,18},{10... | collective-permute-start | bytes 147464 | tf_op jit(solution)/shard_map/ppermute | solution.py:664
  20.8 0.5 %collective-permute-start.5 = (f32[7,8,128]{2,1,0:T(8,128)S(1)}, f32[7,8,128]{2,1,0:T(8,128)S(1)}, u32[]{:S(2)}, u32[]{:S(2)}) collective-permute-start(f32[7,8,128]{2,1,0:T(8,128)S(1)} %get-tuple-element.37), channel_id=1, source_target_pairs={{0,8},{8,0},{16,24},{24,16},{1,9},{9,1},{17,25},{25,17},{2,10},{10... | collective-permute-start | bytes 86024 | tf_op jit(solution)/shard_map/ppermute | solution.py:664
  21.3 2.4 %collective-permute-start.7 = (f32[7,8,128]{2,1,0:T(8,128)S(1)}, f32[7,8,128]{2,1,0:T(8,128)S(1)}, u32[]{:S(2)}, u32[]{:S(2)}) collective-permute-start(f32[7,8,128]{2,1,0:T(8,128)S(1)} %get-tuple-element.39), channel_id=1, source_target_pairs={{0,24},{8,16},{16,8},{24,0},{1,25},{9,17},{17,9},{25,1},{2,26},{10... | collective-permute-start | bytes 86024 | tf_op jit(solution)/shard_map/ppermute | solution.py:664
  23.7 0.9 %shard_map.71 = (f32[19,128,128]{2,1,0:T(8,128)}, f32[2,128,128]{2,1,0:T(8,128)}) custom-call(f32[19,128,128]{2,1,0:T(8,128)S(1)} %get-tuple-element.35.g_ref, f32[2,128,128]{2,1,0:T(8,128)S(1)} %get-tuple-element.40.acc_ref), custom_call_target="tpu_custom_call" | custom-call | tf_op jit(solution)/shard_map/pallas_call | solution.py:699
  24.7 0.0 collective-permute-done.5.refs_0_
  24.7 1.4 %collective-permute-done.7.refs_2_ = f32[7,8,128]{2,1,0:T(8,128)S(1)} collective-permute-done((f32[7,8,128]{2,1,0:T(8,128)S(1)}, f32[7,8,128]{2,1,0:T(8,128)S(1)}, u32[]{:S(2)}, u32[]{:S(2)}) %collective-permute-start.7) | collective-permute-done | bytes 28704 | tf_op jit(solution)/shard_map/ppermute | solution.py:664
  26.1 0.0 collective-permute-done.6.refs_1_
  26.1 1.5 %shard_map.72 = (f32[19,128,128]{2,1,0:T(8,128)}, f32[2,8,16]{2,1,0:T(8,128)}) custom-call(f32[4,128]{1,0:T(4,128)S(1)} %get-tuple-element.24.info_ref, f32[19,128,128]{2,1,0:T(8,128)S(1)} %get-tuple-element.35.g_ref, f32[8,128]{1,0:T(8,128)S(1)} %get-tuple-element.36.own_ref, ...), custom_call_target="tpu_custom_call", output_to_operand_aliasing={{0}: (6, {})} | custom-call | tf_op jit(solution)/shard_map/pallas_call | solution.py:703
Async XLA Ops:
  2.6 9.3 %collective-permute-start.1 = (f32[11,8,128]{2,1,0:T(8,128)S(1)}, f32[11,8,128]{2,1,0:T(8,128)S(1)}, u32[]{:S(2)}, u32[]{:S(2)}) collective-permute-start(f32[11,8,128]{2,1,0:T(8,128)S(1)} %get-tuple-element.28), channel_id=1, source_target_pairs={{0,16},{8,24},{16,0},{24,8},{1,17},{9,25},{17,1},{25,9},{2,18},{10... | collective-permute-start | bytes 135176 | tf_op jit(solution)/shard_map/ppermute | solution.py:664
  5.6 3.8 %collective-permute-start = (f32[6,8,128]{2,1,0:T(8,128)S(1)}, f32[6,8,128]{2,1,0:T(8,128)S(1)}, u32[]{:S(2)}, u32[]{:S(2)}) collective-permute-start(f32[6,8,128]{2,1,0:T(8,128)S(1)} %get-tuple-element.27), channel_id=1, source_target_pairs={{0,8},{8,0},{16,24},{24,16},{1,9},{9,1},{17,25},{25,17},{2,10},{10... | collective-permute-start | bytes 73736 | tf_op jit(solution)/shard_map/ppermute | solution.py:664
  7.1 4.7 %collective-permute-start.2 = (f32[6,8,128]{2,1,0:T(8,128)S(1)}, f32[6,8,128]{2,1,0:T(8,128)S(1)}, u32[]{:S(2)}, u32[]{:S(2)}) collective-permute-start(f32[6,8,128]{2,1,0:T(8,128)S(1)} %get-tuple-element.29), channel_id=1, source_target_pairs={{0,24},{8,16},{16,8},{24,0},{1,25},{9,17},{17,9},{25,1},{2,26},{10... | collective-permute-start | bytes 73736 | tf_op jit(solution)/shard_map/ppermute | solution.py:664
  12.3 4.2 %collective-permute-start.3 = (f32[15,16,128]{2,1,0:T(8,128)S(1)}, f32[15,16,128]{2,1,0:T(8,128)S(1)}, u32[]{:S(2)}, u32[]{:S(2)}) collective-permute-start(f32[15,16,128]{2,1,0:T(8,128)S(1)} %get-tuple-element.32), channel_id=1, source_target_pairs={{0,1},{1,0},{2,3},{3,2},{4,5},{5,4},{6,7},{7,6},{8,9},{9,8},{10,11... | collective-permute-start | bytes 368648 | tf_op jit(solution)/shard_map/ppermute | solution.py:687
  12.3 6.8 %collective-permute-start.4 = (f32[15,16,128]{2,1,0:T(8,128)S(1)}, f32[15,16,128]{2,1,0:T(8,128)S(1)}, u32[]{:S(2)}, u32[]{:S(2)}) collective-permute-start(f32[15,16,128]{2,1,0:T(8,128)S(1)} %get-tuple-element.33), channel_id=1, source_target_pairs={{0,7},{1,2},{2,1},{3,4},{4,3},{5,6},{6,5},{7,0},{8,15},{9,10},{10,... | collective-permute-start | bytes 368648 | tf_op jit(solution)/shard_map/ppermute | solution.py:686
  20.2 5.9 %collective-permute-start.6 = (f32[12,8,128]{2,1,0:T(8,128)S(1)}, f32[12,8,128]{2,1,0:T(8,128)S(1)}, u32[]{:S(2)}, u32[]{:S(2)}) collective-permute-start(f32[12,8,128]{2,1,0:T(8,128)S(1)} %get-tuple-element.38), channel_id=1, source_target_pairs={{0,16},{8,24},{16,0},{24,8},{1,17},{9,25},{17,1},{25,9},{2,18},{10... | collective-permute-start | bytes 147464 | tf_op jit(solution)/shard_map/ppermute | solution.py:664
  20.8 3.9 %collective-permute-start.5 = (f32[7,8,128]{2,1,0:T(8,128)S(1)}, f32[7,8,128]{2,1,0:T(8,128)S(1)}, u32[]{:S(2)}, u32[]{:S(2)}) collective-permute-start(f32[7,8,128]{2,1,0:T(8,128)S(1)} %get-tuple-element.37), channel_id=1, source_target_pairs={{0,8},{8,0},{16,24},{24,16},{1,9},{9,1},{17,25},{25,17},{2,10},{10... | collective-permute-start | bytes 86024 | tf_op jit(solution)/shard_map/ppermute | solution.py:664
  21.3 4.8 %collective-permute-start.7 = (f32[7,8,128]{2,1,0:T(8,128)S(1)}, f32[7,8,128]{2,1,0:T(8,128)S(1)}, u32[]{:S(2)}, u32[]{:S(2)}) collective-permute-start(f32[7,8,128]{2,1,0:T(8,128)S(1)} %get-tuple-element.39), channel_id=1, source_target_pairs={{0,24},{8,16},{16,8},{24,0},{1,25},{9,17},{17,9},{25,1},{2,26},{10... | collective-permute-start | bytes 86024 | tf_op jit(solution)/shard_map/ppermute | solution.py:664

commit v5 on v4

--- a/solution.py
+++ b/solution.py
@@ -124,11 +124,11 @@
         plus(difs[5], eg),
     ]
     others = [
-        minus(minus(scaled(8.0, diag), scaled(11.0, axis)), scaled(30.0, f[0])),
-        plus(scaled(12.0, f[0]), minus(diag, scaled(4.0, axis))),
-        minus(ab, scaled(4.0, difs[1])),
-        minus(cd, scaled(4.0, difs[3])),
-        minus(eg, scaled(4.0, difs[5])),
+        minus(diag, f[0]),
+        minus(plus(f[0], diag), scaled(2.0, axis)),
+        minus(ab, scaled(2.0, difs[1])),
+        minus(cd, scaled(2.0, difs[3])),
+        minus(eg, scaled(2.0, difs[5])),
         plus(axis_x, diag_x),
         minus(diag_x, scaled(2.0, axis_x)),
         plus(axis_w, diag_w),
@@ -143,9 +143,6 @@
     return kept, others
 
 
-ORDER = [1, 2, 4, 6, 8, 9, 10, 11, 12, 13, 14, 15, 16, 17, 18]
-
-
 def equilibrium(rho, jx, jy, jz):
     inverse = 1.0 / rho
     ux, uy, uz = jx * inverse, jy * inverse, jz * inverse
@@ -153,19 +150,28 @@
     yz_sum, yz_dif = yy + zz, yy - zz
     square = xx + yz_sum
     eq_x = 2.0 * xx - yz_sum
-    third = -2.0 / 3.0
-    eq = [19.0 * square - 11.0 * rho, 3.0 * rho - 5.5 * square]
-    eq += [third * jx, third * jy, third * jz]
+    eq = [square, None, None, None, None]
     eq += [eq_x, -0.5 * eq_x, yz_dif, -0.5 * yz_dif, jx * uy, jy * uz, jx * uz]
     return eq + [None] * 3
 
 
+ORDER = [4, 6, 8, 9, 10, 11, 12, 13, 14, 15, 16, 17, 18]
+FLOW = 5.0 / 3.0
+
+
 def relax(moment):
-    scaled_by = [scaled(RATE[k], m) for k, m in zip(ORDER, moment)]
-    even_e, even_s, flow_x, flow_y, flow_z, even_x, even_px, even_w, even_pw = scaled_by[:9]
-    even_xy, even_yz, even_xz, twist_x, twist_y, twist_z = scaled_by[9:]
-    base_axis = minus(scaled(-11.0, even_e), scaled(4.0, even_s))
-    base_diag = plus(scaled(8.0, even_e), even_s)
+    level_a, level_c = moment[:2]
+    factors = [RATE[k] * (FLOW if k in (4, 6, 8) else 1.0) for k in ORDER]
+    scaled_by = [scaled(k, m) for k, m in zip(factors, moment[2:])]
+    flow_x, flow_y, flow_z, even_x, even_px, even_w, even_pw = scaled_by[:7]
+    even_xy, even_yz, even_xz, twist_x, twist_y, twist_z = scaled_by[7:]
+
+    def blend(by_e, by_s):
+        rate_e, rate_s = by_e * RATE[1], by_s * RATE[2]
+        return plus(scaled(19.0 * rate_e - 5.5 * rate_s, level_a), scaled(3.5 * rate_s, level_c))
+
+    base_axis = blend(-11.0, -4.0)
+    base_diag = blend(8.0, 1.0)
     lean = minus(even_x, scaled(2.0, even_px))
     tilt = minus(even_w, scaled(2.0, even_pw))
     side_x, side_w = plus(even_x, even_px), plus(even_w, even_pw)
@@ -198,7 +204,7 @@
         15: plus(y_up, z_down),
         17: minus(y_up, z_down),
     }
-    out = [minus(scaled(12.0, even_s), scaled(30.0, even_e))]
+    out = [blend(-30.0, 12.0)]
     for i in range(1, Q, 2):
         out += [plus(even[i], odd[i]), minus(even[i], odd[i])]
     return out
@@ -324,16 +330,19 @@
     return left, right
 
 
-def moved_x(z, ref, i, y, left, right):
+def mended(z, value, i, y, left, right):
     lanes, last = z.lanes(), z.width - 1
-    value = z.tile(ref, i, y)
     if CX[i] == 1:
         at = eastward.index(i) * z.planes + y
-        return jnp.where(lanes == 0, roll(left, -at), roll(value, 1))
+        return jnp.where(lanes == 0, roll(left, -at), value)
     if CX[i] == -1:
         at = westward.index(i) * z.planes + y
-        return jnp.where(lanes == last, roll(right, last - at), roll(value, -1))
+        return jnp.where(lanes == last, roll(right, last - at), value)
     return value
+
+
+def moved_x(z, ref, i, y, left, right):
+    return mended(z, roll(z.tile(ref, i, y), CX[i]), i, y, left, right)
 
 
 def sliding(z, whole, part, tops, bottoms, edges, put):
@@ -559,7 +568,7 @@
     pack_x(z, whole, g_ref, sends, sums)
 
 
-def direct_kernel(z, g_ref, acc_ref, out_hbm, acc_hbm, sems):
+def direct_kernel(z, g_ref, acc_ref, out_hbm, acc_hbm, turned_ref, sems):
     inner = (z.planes - 1) * z.depth
     copies = [pltpu.make_async_copy(acc_ref, acc_hbm, sems.at[len(straight)])]
     copies[0].start()
@@ -571,11 +580,16 @@
             source, target = source.at[pl.ds(z.depth, inner), :], target.at[pl.ds(0, inner), :]
         copies.append(pltpu.make_async_copy(source, target, sems.at[k]))
         copies[-1].start()
+    for k, i in enumerate(slanted):
+        for y in range(z.planes):
+            if 0 <= y - CY[i] < z.planes:
+                here = pl.ds(y * z.depth, z.depth)
+                turned_ref[k, here, :] = roll(z.tile(g_ref, i, y - CY[i]), CX[i])
     for copy in copies:
         copy.wait()
 
 
-def fourth_kernel(z, info_ref, g_ref, own_ref, *refs):
+def fourth_kernel(z, info_ref, g_ref, turned_ref, own_ref, *refs):
     gets, (_, out_hbm, profile_hbm) = refs[: z.count - 1], refs[z.count - 1 : z.count + 2]
     tops, bottoms, edges, out_ref, profile_ref, sems = refs[z.count + 2 :]
     whole, part = shift_of(info_ref, 1)
@@ -599,7 +613,8 @@
             for y in range(k * group, (k + 1) * group):
                 if 0 <= y - CY[i] < z.planes:
                     here = pl.ds(y * z.depth, z.depth)
-                    out_ref[i, here, :] = moved_x(z, g_ref, i, y - CY[i], left, right)
+                    value = turned_ref[slanted.index(i), here, :]
+                    out_ref[i, here, :] = mended(z, value, i, y - CY[i], left, right)
 
     def finish(k):
         here = pl.ds(k * group * z.depth, group * z.depth)
@@ -607,10 +622,6 @@
             part = (pl.ds(first, last - first), here, slice(None))
             send(out_ref.at[part], out_hbm.at[part])
 
-    for k in range(1, CHUNKS - 1):
-        interior(k)
-        finish(k)
-
     def put(i, value):
         here = pl.ds(0 if CY[i] == 1 else (z.planes - 1) * z.depth, z.depth)
         out_ref[i, here, :] = value
@@ -618,7 +629,7 @@
             send(out_ref.at[i, here, :], out_hbm.at[i, here, :])
 
     sliding(z, whole, part, tops, bottoms, edges, put)
-    for k in (0, CHUNKS - 1):
+    for k in range(CHUNKS):
         interior(k)
         finish(k)
     for copy in copies:
@@ -696,18 +707,23 @@
         ],
     )(*keep(info, h, inner, outer, mask, old))
     gets = swap_x(sends)
-    out, acc = call(
-        direct_kernel, [vmem] * 2, [hbm(cells), hbm(fields)], [sems(len(straight) + 1)], [0, 1]
+    turned = f32(len(slanted), planes * depth, width)
+    out, acc, turned = call(
+        direct_kernel,
+        [vmem] * 2,
+        [hbm(cells), hbm(fields), turned],
+        [sems(len(straight) + 1)],
+        [0, 1],
     )(*keep(g, acc))
     moves = 1 + len(SPANS) * CHUNKS + sum(CX[i] == 0 for i in rising + falling)
     out, profile = call(
         fourth_kernel,
-        [vmem] * (2 + count) + [outside],
+        [vmem] * (3 + count) + [outside],
         [hbm(cells), hbm(f32(2, depth, planes))],
         shifts + [cells, f32(2, depth, planes), sems(moves)],
         [0, 1],
-        {2 + count: 0},
-    )(*keep(info, g, own, *gets), out)
+        {3 + count: 0},
+    )(*keep(info, g, turned, own, *gets), out)
     return (
         out.reshape(pop_ratio.shape),
         acc.reshape(2, planes, depth, width),

time: 27.8 us -> 27.5 us (0.989)
  no operation moved by 1% of the time
where the time goes in v5:
time: 27.5 us; the launch traced here: 27.4 us
  starting transfers between devices  11.9 us (43%)
  waiting for transfers between devices  8.8 us (32%)
  Pallas kernels  5.95 us (22%)
  between operations  0.69 us (3%)
    ppermute x6, starting transfers between devices, swap_x(): lax.ppermute(values[d - 1], 'gx', [(i, i ^ d) for i in range(count)])  8.15 us
    ppermute x6, waiting for transfers between devices, swap_x(): lax.ppermute(values[d - 1], 'gx', [(i, i ^ d) for i in range(count)])  6.07 us
    ppermute x1, starting transfers between devices, local(): outer = lax.ppermute(outer, 'gz', across)  3.7 us
    ppermute x1, waiting for transfers between devices, local(): outer = lax.ppermute(outer, 'gz', across)  2.73 us
    pallas_call x1, Pallas kernels, local(): call(first_kernel, [outside] * 4, [cells, fields, f32(planes // BLOCK * z...  1.91 us
    pallas_call x1, Pallas kernels, local(): call(fourth_kernel, [vmem] * (3 + count) + [outside], [hbm(cells), hbm(f3...  1.36 us
    pallas_call x1, Pallas kernels, local(): call(third_kernel, [vmem] * 6, [cells, fields, f32(depth, width)] + buffe...  0.96 us
    pallas_call x1, Pallas kernels, local(): call(direct_kernel, [vmem] * 2, [hbm(cells), hbm(fields), turned], [sems(...  0.92 us
  transfers between devices with their start and end apart: 8, of which 4 were waited for; matrix products, arithmetic and copies ran while one was open for 0% of the time, Pallas kernels for 5%

profile of v5, /device:TPU:0, one launch (start us, length us, event | category | flops | bytes accessed | tf_op | source)
XLA Modules:
  0.0 27.4 jit_solution(5818016244526082569)
XLA Ops:
  0.6 1.9 %shard_map.67 = (f32[19,128,128]{2,1,0:T(8,128)S(1)}, f32[2,128,128]{2,1,0:T(8,128)S(1)}, f32[8,128]{1,0:T(8,128)S(1)}, f32[4,128]{1,0:T(4,128)S(1)}, f32[6,8,12...) custom-call(s32[2]{0:T(128)} %whole_hbm.1, s32[2]{0:T(128)} %part_hbm.1, ...), custom_call_target="tpu_custom_call" | custom-call | tf_op jit(solution)/shard_map/pallas_call | solution.py:683
  2.6 3.1 %collective-permute-start.1 = (f32[11,8,128]{2,1,0:T(8,128)S(1)}, f32[11,8,128]{2,1,0:T(8,128)S(1)}, u32[]{:S(2)}, u32[]{:S(2)}) collective-permute-start(f32[11,8,128]{2,1,0:T(8,128)S(1)} %get-tuple-element.29), channel_id=1, source_target_pairs={{0,16},{8,24},{16,0},{24,8},{1,17},{9,25},{17,1},{25,9},{2,18},{10... | collective-permute-start | bytes 135176 | tf_op jit(solution)/shard_map/ppermute | solution.py:675
  5.6 1.5 %collective-permute-start = (f32[6,8,128]{2,1,0:T(8,128)S(1)}, f32[6,8,128]{2,1,0:T(8,128)S(1)}, u32[]{:S(2)}, u32[]{:S(2)}) collective-permute-start(f32[6,8,128]{2,1,0:T(8,128)S(1)} %get-tuple-element.28), channel_id=1, source_target_pairs={{0,8},{8,0},{16,24},{24,16},{1,9},{9,1},{17,25},{25,17},{2,10},{10... | collective-permute-start | bytes 73736 | tf_op jit(solution)/shard_map/ppermute | solution.py:675
  7.1 0.0 collective-permute-start.2
  7.2 2.3 %collective-permute-done.refs_0_ = f32[6,8,128]{2,1,0:T(8,128)S(1)} collective-permute-done((f32[6,8,128]{2,1,0:T(8,128)S(1)}, f32[6,8,128]{2,1,0:T(8,128)S(1)}, u32[]{:S(2)}, u32[]{:S(2)}) %collective-permute-start) | collective-permute-done | bytes 24608 | tf_op jit(solution)/shard_map/ppermute | solution.py:675
  9.4 2.4 %collective-permute-done.2.refs_2_ = f32[6,8,128]{2,1,0:T(8,128)S(1)} collective-permute-done((f32[6,8,128]{2,1,0:T(8,128)S(1)}, f32[6,8,128]{2,1,0:T(8,128)S(1)}, u32[]{:S(2)}, u32[]{:S(2)}) %collective-permute-start.2) | collective-permute-done | bytes 24608 | tf_op jit(solution)/shard_map/ppermute | solution.py:675
  11.8 0.0 collective-permute-done.1.refs_1_
  11.8 0.4 %shard_map.68 = (f32[15,16,128]{2,1,0:T(8,128)S(1)}, f32[15,16,128]{2,1,0:T(8,128)S(1)}, f32[10,8,128]{2,1,0:T(8,128)S(1)}, f32[2,8,128]{2,1,0:T(8,128)S(1)}) custom-call(f32[4,128]{1,0:T(4,128)S(1)} %get-tuple-element.25.info_ref, f32[19,128,128]{2,1,0:T(8,128)S(1)} %get-tuple-element.26.post_ref, f32[8,128]{1,0:T(8,128)S(1)} %get-tuple-element.27.mask_ref, ...), custom_call_target="tpu_custom_call" | custom-call | tf_op jit(solution)/shard_map/pallas_call | solution.py:691
  12.2 0.1 collective-permute-start.3
  12.3 3.7 %collective-permute-start.4 = (f32[15,16,128]{2,1,0:T(8,128)S(1)}, f32[15,16,128]{2,1,0:T(8,128)S(1)}, u32[]{:S(2)}, u32[]{:S(2)}) collective-permute-start(f32[15,16,128]{2,1,0:T(8,128)S(1)} %get-tuple-element.34), channel_id=1, source_target_pairs={{0,7},{1,2},{2,1},{3,4},{4,3},{5,6},{6,5},{7,0},{8,15},{9,10},{10,... | collective-permute-start | bytes 368648 | tf_op jit(solution)/shard_map/ppermute | solution.py:697
  16.0 0.4 %shard_map.69.h_ref = f32[19,128,128]{2,1,0:T(8,128)S(1)} custom-call(f32[19,128,128]{2,1,0:T(8,128)S(1)} %get-tuple-element.26.post_ref, f32[10,8,128]{2,1,0:T(8,128)S(1)} %get-tuple-element.31.wall_ref, f32[2,8,128]{2,1,0:T(8,128)S(1)} %get-tuple-element.32.side_ref), custom_call_target="tpu_custom_call" | custom-call | tf_op jit(solution)/shard_map/pallas_call | solution.py:699
  16.4 0.0 collective-permute-done.3.inner_ref
  16.4 2.7 %collective-permute-done.4.outer_ref = f32[15,16,128]{2,1,0:T(8,128)S(1)} collective-permute-done((f32[15,16,128]{2,1,0:T(8,128)S(1)}, f32[15,16,128]{2,1,0:T(8,128)S(1)}, u32[]{:S(2)}, u32[]{:S(2)}) %collective-permute-start.4) | collective-permute-done | bytes 122912 | tf_op jit(solution)/shard_map/ppermute | solution.py:697
  19.2 1.0 %shard_map.70 = (f32[19,128,128]{2,1,0:T(8,128)S(1)}, f32[2,128,128]{2,1,0:T(8,128)S(1)}, f32[8,128]{1,0:T(8,128)S(1)}, f32[7,8,128]{2,1,0:T(8,128)S(1)}, f32[12...) custom-call(f32[4,128]{1,0:T(4,128)S(1)} %get-tuple-element.25.info_ref, f32[19,128,128]{2,1,0:T(8,128)S(1)} %shard_map.69.h_ref, ...), custom_call_target="tpu_custom_call" | custom-call | tf_op jit(solution)/shard_map/pallas_call | solution.py:700
  20.1 0.6 %collective-permute-start.6 = (f32[12,8,128]{2,1,0:T(8,128)S(1)}, f32[12,8,128]{2,1,0:T(8,128)S(1)}, u32[]{:S(2)}, u32[]{:S(2)}) collective-permute-start(f32[12,8,128]{2,1,0:T(8,128)S(1)} %get-tuple-element.41), channel_id=1, source_target_pairs={{0,16},{8,24},{16,0},{24,8},{1,17},{9,25},{17,1},{25,9},{2,18},{10... | collective-permute-start | bytes 147464 | tf_op jit(solution)/shard_map/ppermute | solution.py:675
  20.7 0.5 %collective-permute-start.5 = (f32[7,8,128]{2,1,0:T(8,128)S(1)}, f32[7,8,128]{2,1,0:T(8,128)S(1)}, u32[]{:S(2)}, u32[]{:S(2)}) collective-permute-start(f32[7,8,128]{2,1,0:T(8,128)S(1)} %get-tuple-element.40), channel_id=1, source_target_pairs={{0,8},{8,0},{16,24},{24,16},{1,9},{9,1},{17,25},{25,17},{2,10},{10... | collective-permute-start | bytes 86024 | tf_op jit(solution)/shard_map/ppermute | solution.py:675
  21.2 2.4 %collective-permute-start.7 = (f32[7,8,128]{2,1,0:T(8,128)S(1)}, f32[7,8,128]{2,1,0:T(8,128)S(1)}, u32[]{:S(2)}, u32[]{:S(2)}) collective-permute-start(f32[7,8,128]{2,1,0:T(8,128)S(1)} %get-tuple-element.42), channel_id=1, source_target_pairs={{0,24},{8,16},{16,8},{24,0},{1,25},{9,17},{17,9},{25,1},{2,26},{10... | collective-permute-start | bytes 86024 | tf_op jit(solution)/shard_map/ppermute | solution.py:675
  23.7 0.9 %shard_map.71 = (f32[19,128,128]{2,1,0:T(8,128)}, f32[2,128,128]{2,1,0:T(8,128)}, f32[10,128,128]{2,1,0:T(8,128)S(1)}) custom-call(f32[19,128,128]{2,1,0:T(8,128)S(1)} %get-tuple-element.36.g_ref, f32[2,128,128]{2,1,0:T(8,128)S(1)} %get-tuple-element.37.acc_ref), custom_call_target="tpu_custom_call" | custom-call | tf_op jit(solution)/shard_map/pallas_call | solution.py:711
  24.6 0.0 collective-permute-done.5.refs_0_
  24.6 1.4 %collective-permute-done.7.refs_2_ = f32[7,8,128]{2,1,0:T(8,128)S(1)} collective-permute-done((f32[7,8,128]{2,1,0:T(8,128)S(1)}, f32[7,8,128]{2,1,0:T(8,128)S(1)}, u32[]{:S(2)}, u32[]{:S(2)}) %collective-permute-start.7) | collective-permute-done | bytes 28704 | tf_op jit(solution)/shard_map/ppermute | solution.py:675
  26.0 0.0 collective-permute-done.6.refs_1_
  26.0 1.4 %shard_map.72 = (f32[19,128,128]{2,1,0:T(8,128)}, f32[2,8,16]{2,1,0:T(8,128)}) custom-call(f32[4,128]{1,0:T(4,128)S(1)} %get-tuple-element.25.info_ref, f32[19,128,128]{2,1,0:T(8,128)S(1)} %get-tuple-element.36.g_ref, f32[10,128,128]{2,1,0:T(8,128)S(1)} %get-tuple-element.38.turned_ref, ...), custom_call_target="tpu_custom_call", output_to_operand_aliasing={{0}: (7, {})} | custom-call | tf_op jit(solution)/shard_map/pallas_call | solution.py:719
Async XLA Ops:
  2.6 9.3 %collective-permute-start.1 = (f32[11,8,128]{2,1,0:T(8,128)S(1)}, f32[11,8,128]{2,1,0:T(8,128)S(1)}, u32[]{:S(2)}, u32[]{:S(2)}) collective-permute-start(f32[11,8,128]{2,1,0:T(8,128)S(1)} %get-tuple-element.29), channel_id=1, source_target_pairs={{0,16},{8,24},{16,0},{24,8},{1,17},{9,25},{17,1},{25,9},{2,18},{10... | collective-permute-start | bytes 135176 | tf_op jit(solution)/shard_map/ppermute | solution.py:675
  5.6 3.8 %collective-permute-start = (f32[6,8,128]{2,1,0:T(8,128)S(1)}, f32[6,8,128]{2,1,0:T(8,128)S(1)}, u32[]{:S(2)}, u32[]{:S(2)}) collective-permute-start(f32[6,8,128]{2,1,0:T(8,128)S(1)} %get-tuple-element.28), channel_id=1, source_target_pairs={{0,8},{8,0},{16,24},{24,16},{1,9},{9,1},{17,25},{25,17},{2,10},{10... | collective-permute-start | bytes 73736 | tf_op jit(solution)/shard_map/ppermute | solution.py:675
  7.1 4.7 %collective-permute-start.2 = (f32[6,8,128]{2,1,0:T(8,128)S(1)}, f32[6,8,128]{2,1,0:T(8,128)S(1)}, u32[]{:S(2)}, u32[]{:S(2)}) collective-permute-start(f32[6,8,128]{2,1,0:T(8,128)S(1)} %get-tuple-element.30), channel_id=1, source_target_pairs={{0,24},{8,16},{16,8},{24,0},{1,25},{9,17},{17,9},{25,1},{2,26},{10... | collective-permute-start | bytes 73736 | tf_op jit(solution)/shard_map/ppermute | solution.py:675
  12.2 4.2 %collective-permute-start.3 = (f32[15,16,128]{2,1,0:T(8,128)S(1)}, f32[15,16,128]{2,1,0:T(8,128)S(1)}, u32[]{:S(2)}, u32[]{:S(2)}) collective-permute-start(f32[15,16,128]{2,1,0:T(8,128)S(1)} %get-tuple-element.33), channel_id=1, source_target_pairs={{0,1},{1,0},{2,3},{3,2},{4,5},{5,4},{6,7},{7,6},{8,9},{9,8},{10,11... | collective-permute-start | bytes 368648 | tf_op jit(solution)/shard_map/ppermute | solution.py:698
  12.3 6.8 %collective-permute-start.4 = (f32[15,16,128]{2,1,0:T(8,128)S(1)}, f32[15,16,128]{2,1,0:T(8,128)S(1)}, u32[]{:S(2)}, u32[]{:S(2)}) collective-permute-start(f32[15,16,128]{2,1,0:T(8,128)S(1)} %get-tuple-element.34), channel_id=1, source_target_pairs={{0,7},{1,2},{2,1},{3,4},{4,3},{5,6},{6,5},{7,0},{8,15},{9,10},{10,... | collective-permute-start | bytes 368648 | tf_op jit(solution)/shard_map/ppermute | solution.py:697
  20.1 5.9 %collective-permute-start.6 = (f32[12,8,128]{2,1,0:T(8,128)S(1)}, f32[12,8,128]{2,1,0:T(8,128)S(1)}, u32[]{:S(2)}, u32[]{:S(2)}) collective-permute-start(f32[12,8,128]{2,1,0:T(8,128)S(1)} %get-tuple-element.41), channel_id=1, source_target_pairs={{0,16},{8,24},{16,0},{24,8},{1,17},{9,25},{17,1},{25,9},{2,18},{10... | collective-permute-start | bytes 147464 | tf_op jit(solution)/shard_map/ppermute | solution.py:675
  20.7 3.9 %collective-permute-start.5 = (f32[7,8,128]{2,1,0:T(8,128)S(1)}, f32[7,8,128]{2,1,0:T(8,128)S(1)}, u32[]{:S(2)}, u32[]{:S(2)}) collective-permute-start(f32[7,8,128]{2,1,0:T(8,128)S(1)} %get-tuple-element.40), channel_id=1, source_target_pairs={{0,8},{8,0},{16,24},{24,16},{1,9},{9,1},{17,25},{25,17},{2,10},{10... | collective-permute-start | bytes 86024 | tf_op jit(solution)/shard_map/ppermute | solution.py:675
  21.2 4.8 %collective-permute-start.7 = (f32[7,8,128]{2,1,0:T(8,128)S(1)}, f32[7,8,128]{2,1,0:T(8,128)S(1)}, u32[]{:S(2)}, u32[]{:S(2)}) collective-permute-start(f32[7,8,128]{2,1,0:T(8,128)S(1)} %get-tuple-element.42), channel_id=1, source_target_pairs={{0,24},{8,16},{16,8},{24,0},{1,25},{9,17},{17,9},{25,1},{2,26},{10... | collective-permute-start | bytes 86024 | tf_op jit(solution)/shard_map/ppermute | solution.py:675

commit v6 on v5

--- a/solution.py
+++ b/solution.py
@@ -48,7 +48,7 @@
 straight = [i for i in range(Q) if CX[i] == 0]
 slanted = [i for i in range(Q) if CX[i] != 0]
 SPANS = [(i, next(k for k in range(i, Q + 1) if k == Q or CX[k] == 0)) for i in slanted if CX[i - 1] == 0]
-PART, SUMS = len(upward), 2 * len(upward)
+NEAR, PART, SUMS = 0, len(upward), 2 * len(upward)
 MASK = SUMS + 4
 SLOTS = MASK + 1
 wall_speed = 0.08
@@ -516,53 +516,76 @@
                 h_ref[i, here, :] = wall_ref[wall_slot(i)]
 
 
+def middle_kernel(z, h_ref, mask_ref, old_ref, g_ref, acc_ref):
+    for y in range(z.planes):
+        solid = z.solid_tile(mask_ref, y) > 0.5
+        f = [roll(z.tile(h_ref, i, y), CZ[i], 0) for i in range(Q)]
+        post, jx, moment_xy = collide(f, solid)
+        here = pl.ds(y * z.depth, z.depth)
+        for i in range(Q):
+            g_ref[i, here, :] = roll(post[i], CZ[i], 0)
+        fields = [jx, -(1.0 - 0.5 * visc_rate) * moment_xy]
+        for k in range(2):
+            acc_ref[k, here, :] = old_ref[k, here, :] + jnp.where(solid, 0.0, fields[k])
+
+
 def third_kernel(z, info_ref, h_ref, inner_ref, outer_ref, mask_ref, old_ref, *refs):
-    (g_ref, acc_ref, part_ref), sends = refs[:3], refs[3 : 2 + z.count]
-    sides, extra = refs[2 + z.count :]
+    (g_ref, acc_ref, part_ref), sends = refs[2:5], refs[5 : 4 + z.count]
+    (sides,) = refs[4 + z.count :]
     whole, _ = shift_of(info_ref, 1)
     even = lax.rem(lax.axis_index("gz"), 2) == 0
     sides[jnp.where(even, 1, 0)] = inner_ref[...]
     sides[jnp.where(even, 0, 1)] = outer_ref[...]
-    chunk = min(8, z.planes)
+    chunk = min(2 * BLOCK, z.planes)
+    shape = (chunk, z.width)
+    heights = lax.broadcasted_iota(jnp.int32, shape, 0)
     for side in range(2):
+        edge, next_row = (0, 1) if side == 0 else (z.depth - 1, z.depth - 2)
+        actual = list(range(Q)) if side == 0 else mirror
         for start in range(0, z.planes, chunk):
             here = pl.ds(start, chunk)
-            row = start * z.depth + (0 if side == 0 else z.depth - 1)
+
+            def rows(row):
+                return pl.ds(start * z.depth + row, chunk, stride=z.depth)
+
+            own = {i: h_ref[actual[i], rows(edge), :] for i in level + downward}
             f = [None] * Q
             for i in downward:
-                k = i if side == 0 else mirror[i]
-                f[i] = h_ref[k, pl.ds(row, chunk, stride=z.depth), :]
+                f[i] = own[i]
             kept, others = moments(f)
             kept = [plus(kept[k], sides[side, SUMS + k, here, :]) for k in range(4)]
             change = relax([minus(m, e) for m, e in zip(others, equilibrium(*kept))])
             solid = sides[side, MASK, here, :] > 0.5
             for s, i in enumerate(upward):
                 value = sides[side, PART + s, here, :] - change[i]
-                extra[side, s, here, :] = jnp.where(solid, f[opposite[i]], value)
-    rows, lanes = z.rows(), z.lanes()
-
-    def moved(i, y, value, table, slot):
-        if CZ[i] == 1:
-            line = z.spread(table[0, slot(i), pl.ds(y, 1), :])
-            return jnp.where(rows == 0, line, roll(value, 1, 0))
-        if CZ[i] == -1:
-            line = z.spread(table[1, slot(mirror[i]), pl.ds(y, 1), :])
-            return jnp.where(rows == z.depth - 1, line, roll(value, -1, 0))
-        return value
-
+                g_ref[actual[i], rows(edge), :] = jnp.where(solid, f[opposite[i]], value)
+
+            for i in level:
+                f[i] = own[i]
+            for s, i in enumerate(upward):
+                f[i] = sides[side, NEAR + s, here, :]
+            for i in downward:
+                f[i] = h_ref[actual[i], rows(next_row), :]
+            solid = jnp.zeros(shape, jnp.float32)
+            for k in range(chunk // BLOCK):
+                at = (start // BLOCK + k) * z.deep + (0 if side == 0 else z.deep - 1)
+                line = jnp.broadcast_to(mask_ref[at : at + 1, :], shape)
+                solid = jnp.where(heights >= k * BLOCK, line, solid)
+            solid = solid > 0.5
+            post, jx, moment_xy = collide(f, solid)
+            for i in level:
+                g_ref[actual[i], rows(edge), :] = post[i]
+            for i in upward:
+                g_ref[actual[i], rows(next_row), :] = post[i]
+            fields = [jx, -(1.0 - 0.5 * visc_rate) * moment_xy]
+            for k in range(2):
+                value = old_ref[k, rows(edge), :] + jnp.where(solid, 0.0, fields[k])
+                acc_ref[k, rows(edge), :] = value
+    lanes = z.lanes()
     sums = jnp.zeros((z.depth, z.width), jnp.float32)
     for y in range(z.planes):
-        solid = z.solid_tile(mask_ref, y) > 0.5
-        f = [moved(i, y, z.tile(h_ref, i, y), sides, upward.index) for i in range(Q)]
-        post, jx, moment_xy = collide(f, solid)
-        here = pl.ds(y * z.depth, z.depth)
-        for i in range(Q):
-            g_ref[i, here, :] = moved(i, y, post[i], extra, upward.index)
-        fields = [jx, -(1.0 - 0.5 * visc_rate) * moment_xy]
         for k in range(2):
-            value = old_ref[k, here, :] + jnp.where(solid, 0.0, fields[k])
-            acc_ref[k, here, :] = value
-            total = z.spread(jnp.sum(value, axis=1, keepdims=True))
+            total = z.spread(jnp.sum(z.tile(acc_ref, k, y), axis=1, keepdims=True))
             sums = jnp.where(lanes == k * z.planes + y, total, sums)
     part_ref[...] = sums
     pack_x(z, whole, g_ref, sends, sums)
@@ -697,15 +720,14 @@
     outer = lax.ppermute(outer, "gz", across)
     inner = lax.ppermute(inner, "gz", pairs)
     (h,) = call(bulk_kernel, [vmem] * 3, [cells])(*keep(post, wall, side))
+    g, acc = call(middle_kernel, [vmem] * 3, [cells, fields])(*keep(h, mask, old))
     g, acc, own, *sends = call(
         third_kernel,
-        [vmem] * 6,
+        [vmem] * 8,
         [cells, fields, f32(depth, width)] + buffers(1),
-        [
-            pltpu.VMEM((2, SLOTS, planes, width), jnp.float32),
-            pltpu.VMEM((2, len(upward), planes, width), jnp.float32),
-        ],
-    )(*keep(info, h, inner, outer, mask, old))
+        [pltpu.VMEM((2, SLOTS, planes, width), jnp.float32)],
+        alias={6: 0, 7: 1},
+    )(*keep(info, h, inner, outer, mask, old, g, acc))
     gets = swap_x(sends)
     turned = f32(len(slanted), planes * depth, width)
     out, acc, turned = call(

time: 27.5 us -> 27 us (0.982)
  waiting for transfers between devices: 8.8 us -> 8.24 us
    ppermute x1, waiting for transfers between devices: 2.73 us -> 2.17 us  [local(): outer = lax.ppermute(outer, 'gz', across)]
    pallas_call x1 -> x2, Pallas kernels: 0.96 us -> 1 us  [the longest x1 0.55 us: local(): call(middle_kernel, [vmem] * 3, [cells, fields])(*keep(h, mask, old))]
  transfers between devices with their start and end apart: 8 -> 8, of which waited for: 4 -> 4; matrix products, arithmetic and copies ran while one was open for 0% -> 0% of each run, Pallas kernels for 5% -> 7%
where the time goes in v6:
time: 27 us; the launch traced here: 26.9 us
  starting transfers between devices  11.9 us (44%)
  waiting for transfers between devices  8.24 us (31%)
  Pallas kernels  5.98 us (22%)
  between operations  0.7 us (3%)
    ppermute x6, starting transfers between devices, swap_x(): lax.ppermute(values[d - 1], 'gx', [(i, i ^ d) for i in range(count)])  8.15 us
    ppermute x6, waiting for transfers between devices, swap_x(): lax.ppermute(values[d - 1], 'gx', [(i, i ^ d) for i in range(count)])  6.07 us
    ppermute x1, starting transfers between devices, local(): outer = lax.ppermute(outer, 'gz', across)  3.7 us
    ppermute x1, waiting for transfers between devices, local(): outer = lax.ppermute(outer, 'gz', across)  2.17 us
    pallas_call x1, Pallas kernels, local(): call(first_kernel, [outside] * 4, [cells, fields, f32(planes // BLOCK * z...  1.91 us
    pallas_call x1, Pallas kernels, local(): call(fourth_kernel, [vmem] * (3 + count) + [outside], [hbm(cells), hbm(f3...  1.36 us
    pallas_call x1, Pallas kernels, local(): call(direct_kernel, [vmem] * 2, [hbm(cells), hbm(fields), turned], [sems(...  0.92 us
    pallas_call x1, Pallas kernels, local(): call(middle_kernel, [vmem] * 3, [cells, fields])(*keep(h, mask, old))  0.55 us
  transfers between devices with their start and end apart: 8, of which 4 were waited for; matrix products, arithmetic and copies ran while one was open for 0% of the time, Pallas kernels for 7%

profile of v6, /device:TPU:0, one launch (start us, length us, event | category | flops | bytes accessed | tf_op | source)
XLA Modules:
  0.0 26.9 jit_solution(9519853892153568094)
XLA Ops:
  0.6 1.9 %shard_map.67 = (f32[19,128,128]{2,1,0:T(8,128)S(1)}, f32[2,128,128]{2,1,0:T(8,128)S(1)}, f32[8,128]{1,0:T(8,128)S(1)}, f32[4,128]{1,0:T(4,128)S(1)}, f32[6,8,12...) custom-call(s32[2]{0:T(128)} %whole_hbm.1, s32[2]{0:T(128)} %part_hbm.1, ...), custom_call_target="tpu_custom_call" | custom-call | tf_op jit(solution)/shard_map/pallas_call | solution.py:706
  2.6 3.1 %collective-permute-start.1 = (f32[11,8,128]{2,1,0:T(8,128)S(1)}, f32[11,8,128]{2,1,0:T(8,128)S(1)}, u32[]{:S(2)}, u32[]{:S(2)}) collective-permute-start(f32[11,8,128]{2,1,0:T(8,128)S(1)} %get-tuple-element.31), channel_id=1, source_target_pairs={{0,16},{8,24},{16,0},{24,8},{1,17},{9,25},{17,1},{25,9},{2,18},{10... | collective-permute-start | bytes 135176 | tf_op jit(solution)/shard_map/ppermute | solution.py:698
  5.6 1.5 %collective-permute-start = (f32[6,8,128]{2,1,0:T(8,128)S(1)}, f32[6,8,128]{2,1,0:T(8,128)S(1)}, u32[]{:S(2)}, u32[]{:S(2)}) collective-permute-start(f32[6,8,128]{2,1,0:T(8,128)S(1)} %get-tuple-element.30), channel_id=1, source_target_pairs={{0,8},{8,0},{16,24},{24,16},{1,9},{9,1},{17,25},{25,17},{2,10},{10... | collective-permute-start | bytes 73736 | tf_op jit(solution)/shard_map/ppermute | solution.py:698
  7.1 0.0 collective-permute-start.2
  7.2 2.3 %collective-permute-done.refs_0_ = f32[6,8,128]{2,1,0:T(8,128)S(1)} collective-permute-done((f32[6,8,128]{2,1,0:T(8,128)S(1)}, f32[6,8,128]{2,1,0:T(8,128)S(1)}, u32[]{:S(2)}, u32[]{:S(2)}) %collective-permute-start) | collective-permute-done | bytes 24608 | tf_op jit(solution)/shard_map/ppermute | solution.py:698
  9.4 2.4 %collective-permute-done.2.refs_2_ = f32[6,8,128]{2,1,0:T(8,128)S(1)} collective-permute-done((f32[6,8,128]{2,1,0:T(8,128)S(1)}, f32[6,8,128]{2,1,0:T(8,128)S(1)}, u32[]{:S(2)}, u32[]{:S(2)}) %collective-permute-start.2) | collective-permute-done | bytes 24608 | tf_op jit(solution)/shard_map/ppermute | solution.py:698
  11.8 0.0 collective-permute-done.1.refs_1_
  11.8 0.4 %shard_map.68 = (f32[15,16,128]{2,1,0:T(8,128)S(1)}, f32[15,16,128]{2,1,0:T(8,128)S(1)}, f32[10,8,128]{2,1,0:T(8,128)S(1)}, f32[2,8,128]{2,1,0:T(8,128)S(1)}) custom-call(f32[4,128]{1,0:T(4,128)S(1)} %get-tuple-element.27.info_ref, f32[19,128,128]{2,1,0:T(8,128)S(1)} %get-tuple-element.28.post_ref, f32[8,128]{1,0:T(8,128)S(1)} %get-tuple-element.29.mask_ref, ...), custom_call_target="tpu_custom_call" | custom-call | tf_op jit(solution)/shard_map/pallas_call | solution.py:714
  12.2 0.1 collective-permute-start.3
  12.3 3.7 %collective-permute-start.4 = (f32[15,16,128]{2,1,0:T(8,128)S(1)}, f32[15,16,128]{2,1,0:T(8,128)S(1)}, u32[]{:S(2)}, u32[]{:S(2)}) collective-permute-start(f32[15,16,128]{2,1,0:T(8,128)S(1)} %get-tuple-element.36), channel_id=1, source_target_pairs={{0,7},{1,2},{2,1},{3,4},{4,3},{5,6},{6,5},{7,0},{8,15},{9,10},{10,... | collective-permute-start | bytes 368648 | tf_op jit(solution)/shard_map/ppermute | solution.py:720
  16.0 0.4 %shard_map.69.h_ref = f32[19,128,128]{2,1,0:T(8,128)S(1)} custom-call(f32[19,128,128]{2,1,0:T(8,128)S(1)} %get-tuple-element.28.post_ref, f32[10,8,128]{2,1,0:T(8,128)S(1)} %get-tuple-element.33.wall_ref, f32[2,8,128]{2,1,0:T(8,128)S(1)} %get-tuple-element.34.side_ref), custom_call_target="tpu_custom_call" | custom-call | tf_op jit(solution)/shard_map/pallas_call | solution.py:722
  16.4 0.6 %shard_map.70 = (f32[19,128,128]{2,1,0:T(8,128)S(1)}, f32[2,128,128]{2,1,0:T(8,128)S(1)}) custom-call(f32[19,128,128]{2,1,0:T(8,128)S(1)} %shard_map.69.h_ref, f32[8,128]{1,0:T(8,128)S(1)} %get-tuple-element.29.mask_ref, f32[2,128,128]{2,1,0:T(8,128)S(1)} %get-tuple-element.37.old_ref), custom_call_target="tpu_custom_call" | custom-call | tf_op jit(solution)/shard_map/pallas_call | solution.py:723
  17.0 0.0 collective-permute-done.3.inner_ref
  17.0 2.2 %collective-permute-done.4.outer_ref = f32[15,16,128]{2,1,0:T(8,128)S(1)} collective-permute-done((f32[15,16,128]{2,1,0:T(8,128)S(1)}, f32[15,16,128]{2,1,0:T(8,128)S(1)}, u32[]{:S(2)}, u32[]{:S(2)}) %collective-permute-start.4) | collective-permute-done | bytes 122912 | tf_op jit(solution)/shard_map/ppermute | solution.py:720
  19.2 0.4 %shard_map.71 = (f32[19,128,128]{2,1,0:T(8,128)S(1)}, f32[2,128,128]{2,1,0:T(8,128)S(1)}, f32[8,128]{1,0:T(8,128)S(1)}, f32[7,8,128]{2,1,0:T(8,128)S(1)}, f32[12...) custom-call(f32[4,128]{1,0:T(4,128)S(1)} %get-tuple-element.27.info_ref, ...), custom_call_target="tpu_custom_call", output_to_operand_aliasing={{0}: (6, {}), {1}: (7, {})} | custom-call | tf_op jit(solution)/shard_map/pallas_call | solution.py:724
  19.6 0.6 %collective-permute-start.6 = (f32[12,8,128]{2,1,0:T(8,128)S(1)}, f32[12,8,128]{2,1,0:T(8,128)S(1)}, u32[]{:S(2)}, u32[]{:S(2)}) collective-permute-start(f32[12,8,128]{2,1,0:T(8,128)S(1)} %get-tuple-element.45), channel_id=1, source_target_pairs={{0,16},{8,24},{16,0},{24,8},{1,17},{9,25},{17,1},{25,9},{2,18},{10... | collective-permute-start | bytes 147464 | tf_op jit(solution)/shard_map/ppermute | solution.py:698
  20.2 0.5 %collective-permute-start.5 = (f32[7,8,128]{2,1,0:T(8,128)S(1)}, f32[7,8,128]{2,1,0:T(8,128)S(1)}, u32[]{:S(2)}, u32[]{:S(2)}) collective-permute-start(f32[7,8,128]{2,1,0:T(8,128)S(1)} %get-tuple-element.44), channel_id=1, source_target_pairs={{0,8},{8,0},{16,24},{24,16},{1,9},{9,1},{17,25},{25,17},{2,10},{10... | collective-permute-start | bytes 86024 | tf_op jit(solution)/shard_map/ppermute | solution.py:698
  20.7 2.4 %collective-permute-start.7 = (f32[7,8,128]{2,1,0:T(8,128)S(1)}, f32[7,8,128]{2,1,0:T(8,128)S(1)}, u32[]{:S(2)}, u32[]{:S(2)}) collective-permute-start(f32[7,8,128]{2,1,0:T(8,128)S(1)} %get-tuple-element.46), channel_id=1, source_target_pairs={{0,24},{8,16},{16,8},{24,0},{1,25},{9,17},{17,9},{25,1},{2,26},{10... | collective-permute-start | bytes 86024 | tf_op jit(solution)/shard_map/ppermute | solution.py:698
  23.2 0.9 %shard_map.72 = (f32[19,128,128]{2,1,0:T(8,128)}, f32[2,128,128]{2,1,0:T(8,128)}, f32[10,128,128]{2,1,0:T(8,128)S(1)}) custom-call(f32[19,128,128]{2,1,0:T(8,128)S(1)} %get-tuple-element.40.g_ref, f32[2,128,128]{2,1,0:T(8,128)S(1)} %get-tuple-element.41.acc_ref), custom_call_target="tpu_custom_call" | custom-call | tf_op jit(solution)/shard_map/pallas_call | solution.py:733
  24.1 0.0 collective-permute-done.5.refs_0_
  24.1 1.4 %collective-permute-done.7.refs_2_ = f32[7,8,128]{2,1,0:T(8,128)S(1)} collective-permute-done((f32[7,8,128]{2,1,0:T(8,128)S(1)}, f32[7,8,128]{2,1,0:T(8,128)S(1)}, u32[]{:S(2)}, u32[]{:S(2)}) %collective-permute-start.7) | collective-permute-done | bytes 28704 | tf_op jit(solution)/shard_map/ppermute | solution.py:698
  25.5 0.0 collective-permute-done.6.refs_1_
  25.5 1.4 %shard_map.73 = (f32[19,128,128]{2,1,0:T(8,128)}, f32[2,8,16]{2,1,0:T(8,128)}) custom-call(f32[4,128]{1,0:T(4,128)S(1)} %get-tuple-element.27.info_ref, f32[19,128,128]{2,1,0:T(8,128)S(1)} %get-tuple-element.40.g_ref, f32[10,128,128]{2,1,0:T(8,128)S(1)} %get-tuple-element.42.turned_ref, ...), custom_call_target="tpu_custom_call", output_to_operand_aliasing={{0}: (7, {})} | custom-call | tf_op jit(solution)/shard_map/pallas_call | solution.py:741
Async XLA Ops:
  2.6 9.3 %collective-permute-start.1 = (f32[11,8,128]{2,1,0:T(8,128)S(1)}, f32[11,8,128]{2,1,0:T(8,128)S(1)}, u32[]{:S(2)}, u32[]{:S(2)}) collective-permute-start(f32[11,8,128]{2,1,0:T(8,128)S(1)} %get-tuple-element.31), channel_id=1, source_target_pairs={{0,16},{8,24},{16,0},{24,8},{1,17},{9,25},{17,1},{25,9},{2,18},{10... | collective-permute-start | bytes 135176 | tf_op jit(solution)/shard_map/ppermute | solution.py:698
  5.6 3.8 %collective-permute-start = (f32[6,8,128]{2,1,0:T(8,128)S(1)}, f32[6,8,128]{2,1,0:T(8,128)S(1)}, u32[]{:S(2)}, u32[]{:S(2)}) collective-permute-start(f32[6,8,128]{2,1,0:T(8,128)S(1)} %get-tuple-element.30), channel_id=1, source_target_pairs={{0,8},{8,0},{16,24},{24,16},{1,9},{9,1},{17,25},{25,17},{2,10},{10... | collective-permute-start | bytes 73736 | tf_op jit(solution)/shard_map/ppermute | solution.py:698
  7.1 4.7 %collective-permute-start.2 = (f32[6,8,128]{2,1,0:T(8,128)S(1)}, f32[6,8,128]{2,1,0:T(8,128)S(1)}, u32[]{:S(2)}, u32[]{:S(2)}) collective-permute-start(f32[6,8,128]{2,1,0:T(8,128)S(1)} %get-tuple-element.32), channel_id=1, source_target_pairs={{0,24},{8,16},{16,8},{24,0},{1,25},{9,17},{17,9},{25,1},{2,26},{10... | collective-permute-start | bytes 73736 | tf_op jit(solution)/shard_map/ppermute | solution.py:698
  12.2 4.7 %collective-permute-start.3 = (f32[15,16,128]{2,1,0:T(8,128)S(1)}, f32[15,16,128]{2,1,0:T(8,128)S(1)}, u32[]{:S(2)}, u32[]{:S(2)}) collective-permute-start(f32[15,16,128]{2,1,0:T(8,128)S(1)} %get-tuple-element.35), channel_id=1, source_target_pairs={{0,1},{1,0},{2,3},{3,2},{4,5},{5,4},{6,7},{7,6},{8,9},{9,8},{10,11... | collective-permute-start | bytes 368648 | tf_op jit(solution)/shard_map/ppermute | solution.py:721
  12.3 6.8 %collective-permute-start.4 = (f32[15,16,128]{2,1,0:T(8,128)S(1)}, f32[15,16,128]{2,1,0:T(8,128)S(1)}, u32[]{:S(2)}, u32[]{:S(2)}) collective-permute-start(f32[15,16,128]{2,1,0:T(8,128)S(1)} %get-tuple-element.36), channel_id=1, source_target_pairs={{0,7},{1,2},{2,1},{3,4},{4,3},{5,6},{6,5},{7,0},{8,15},{9,10},{10,... | collective-permute-start | bytes 368648 | tf_op jit(solution)/shard_map/ppermute | solution.py:720
  19.6 5.9 %collective-permute-start.6 = (f32[12,8,128]{2,1,0:T(8,128)S(1)}, f32[12,8,128]{2,1,0:T(8,128)S(1)}, u32[]{:S(2)}, u32[]{:S(2)}) collective-permute-start(f32[12,8,128]{2,1,0:T(8,128)S(1)} %get-tuple-element.45), channel_id=1, source_target_pairs={{0,16},{8,24},{16,0},{24,8},{1,17},{9,25},{17,1},{25,9},{2,18},{10... | collective-permute-start | bytes 147464 | tf_op jit(solution)/shard_map/ppermute | solution.py:698
  20.2 3.9 %collective-permute-start.5 = (f32[7,8,128]{2,1,0:T(8,128)S(1)}, f32[7,8,128]{2,1,0:T(8,128)S(1)}, u32[]{:S(2)}, u32[]{:S(2)}) collective-permute-start(f32[7,8,128]{2,1,0:T(8,128)S(1)} %get-tuple-element.44), channel_id=1, source_target_pairs={{0,8},{8,0},{16,24},{24,16},{1,9},{9,1},{17,25},{25,17},{2,10},{10... | collective-permute-start | bytes 86024 | tf_op jit(solution)/shard_map/ppermute | solution.py:698
  20.7 4.8 %collective-permute-start.7 = (f32[7,8,128]{2,1,0:T(8,128)S(1)}, f32[7,8,128]{2,1,0:T(8,128)S(1)}, u32[]{:S(2)}, u32[]{:S(2)}) collective-permute-start(f32[7,8,128]{2,1,0:T(8,128)S(1)} %get-tuple-element.46), channel_id=1, source_target_pairs={{0,24},{8,16},{16,8},{24,0},{1,25},{9,17},{17,9},{25,1},{2,26},{10... | collective-permute-start | bytes 86024 | tf_op jit(solution)/shard_map/ppermute | solution.py:698

commit v7 on v6

--- a/solution.py
+++ b/solution.py
@@ -226,10 +226,14 @@
         self.planes, self.depth, self.width, self.count = planes, depth, width, count
         self.deep, self.wide = depth // BLOCK, width // BLOCK
         assert count >= 4 and count & (count - 1) == 0
-        assert len(eastward) * planes + 4 <= width and 2 * planes <= width
+        self.walls = 2 * planes * (len(eastward) + 1) // 2
+        assert len(eastward) % 2 == 1 and self.walls + 4 <= width
 
     def slots(self, delta):
         return (2 if delta == self.count // 2 else 1) * len(rising) + 1
+
+    def at(self, j, y):
+        return 2 * self.planes * (j // 2) + 2 * y + j % 2
 
     def tile(self, ref, i, y):
         return ref[i, pl.ds(y * self.depth, self.depth), :]
@@ -267,29 +271,32 @@
     ]
 
 
-def wall_columns(z, ref, lanes):
+def wall_columns(z, get, lanes):
     out = jnp.zeros((z.depth, z.width), jnp.float32)
-    start = len(eastward) * z.planes
     for k, (i, y, right) in enumerate(edge_columns(z)):
-        at = start + k
-        moved = roll(z.tile(ref, i, y), at - (z.width - 1 if right else 0))
+        at = z.walls + k
+        moved = roll(get(i, y), at - (z.width - 1 if right else 0))
         out = jnp.where(lanes == at, moved, out)
     return out
 
 
-def pack_x(z, whole, ref, sends, extra=None):
-    me = lax.axis_index("gx")
+def edge_tiles(z, ref):
     lanes = z.lanes()
-    right_edge = wall_columns(z, ref, lanes)
+    right_edge = wall_columns(z, functools.partial(z.tile, ref), lanes)
     left_edge = right_edge
     for j in range(len(eastward)):
         for y in range(z.planes):
-            at = j * z.planes + y
+            at = z.at(j, y)
             hit = lanes == at
             moved = roll(z.tile(ref, eastward[j], y), at - (z.width - 1))
             right_edge = jnp.where(hit, moved, right_edge)
             moved = roll(z.tile(ref, westward[j], y), at)
             left_edge = jnp.where(hit, moved, left_edge)
+    return right_edge, left_edge
+
+
+def pack_x(z, whole, get, right_edge, left_edge, sends, extra=None):
+    me = lax.axis_index("gx")
     far = lax.div(whole, z.width)
     for delta in range(1, z.count):
         send = sends[delta - 1]
@@ -297,8 +304,8 @@
         ahead = lax.rem(me - partner + z.count, z.count)
         at_top = (ahead == far) | (ahead == lax.rem(far + 1, z.count))
         for s in range(len(rising)):
-            top = z.tile(ref, rising[s], z.planes - 1)
-            bottom = z.tile(ref, falling[s], 0)
+            top = get(rising[s], z.planes - 1)
+            bottom = get(falling[s], 0)
             if delta == z.count // 2:
                 send[s] = top
                 send[len(rising) + s] = bottom
@@ -316,7 +323,7 @@
     for s in range(len(rising)):
         tops[me, s] = z.tile(ref, rising[s], z.planes - 1)
         bottoms[me, s] = z.tile(ref, falling[s], 0)
-    edges[me] = wall_columns(z, ref, z.lanes())
+    edges[me] = wall_columns(z, functools.partial(z.tile, ref), z.lanes())
     for delta in range(1, z.count):
         get = gets[delta - 1]
         partner = jnp.bitwise_xor(me, delta)
@@ -333,10 +340,10 @@
 def mended(z, value, i, y, left, right):
     lanes, last = z.lanes(), z.width - 1
     if CX[i] == 1:
-        at = eastward.index(i) * z.planes + y
+        at = z.at(eastward.index(i), y)
         return jnp.where(lanes == 0, roll(left, -at), value)
     if CX[i] == -1:
-        at = westward.index(i) * z.planes + y
+        at = z.at(westward.index(i), y)
         return jnp.where(lanes == last, roll(right, last - at), value)
     return value
 
@@ -351,8 +358,7 @@
     weight = part.astype(jnp.float32) / fraction_unit
     far = lax.div(whole, z.width)
     rest = lax.rem(whole, z.width)
-    start = len(eastward) * z.planes
-    columns = {i: start + k for k, (i, _, _) in enumerate(edge_columns(z))}
+    columns = {i: z.walls + k for k, (i, _, _) in enumerate(edge_columns(z))}
 
     def window(i, planes, s, block, offset):
         pair = []
@@ -389,8 +395,8 @@
     return rising.index(i) if CY[i] == 1 else len(rising) + falling.index(i)
 
 
-def first_kernel(z, whole_hbm, part_hbm, pop_hbm, solid_hbm, post_ref, acc_ref, mask_ref, info_ref, *refs):
-    sends, (whole_ref, part_ref, pop_ref, solid_ref, sems) = refs[: z.count - 1], refs[z.count - 1 :]
+def first_kernel(z, whole_hbm, part_hbm, pop_hbm, solid_hbm, pop_ref, mask_ref, info_ref, *refs):
+    sends, (whole_ref, part_ref, solid_ref, sems) = refs[: z.count - 1], refs[z.count - 1 :]
     group = z.planes // CHUNKS * z.depth
     copies = [pltpu.make_async_copy(solid_hbm, solid_ref, sems.at[CHUNKS])]
     for k in range(CHUNKS):
@@ -408,9 +414,45 @@
         flags = jnp.where(solid_ref[k] > 0, 1.0, 0.0)
         line = jnp.dot(flags, grow, preferred_element_type=jnp.float32)
         mask_ref[pl.ds(k * z.deep, z.deep), :] = line
+
+    lanes = z.lanes()
+    couple = lanes // 2
+    post, edge, solid_edge = {}, [None] * Q, None
     for y in range(z.planes):
         if y % (z.planes // CHUNKS) == 0:
             copies[1 + y // (z.planes // CHUNKS)].wait()
+        flags = z.solid_tile(mask_ref, y)
+        if y in (0, z.planes - 1):
+            f = [z.tile(pop_ref, i, y) * np.float32(weights[i]) for i in range(Q)]
+            values, _, _ = collide(f, flags > 0.5)
+            for i in falling if y == 0 else rising:
+                post[i, y] = values[i]
+
+        def joined(value, old):
+            value = roll(value, 2 * y + 1)
+            return value if old is None else jnp.where(couple == y, value, old)
+
+        edge = [joined(z.tile(pop_ref, i, y), edge[i]) for i in range(Q)]
+        solid_edge = joined(flags, solid_edge)
+    f = [edge[i] * np.float32(weights[i]) for i in range(Q)]
+    values, _, _ = collide(f, solid_edge > 0.5)
+    get = lambda i, y: post[i, y]
+    right_edge = left_edge = wall_columns(z, get, lanes)
+    for j in range(len(eastward)):
+        hit = (lanes // (2 * z.planes) == j // 2) & (lanes % 2 == j % 2)
+        right_edge = jnp.where(hit, roll(values[eastward[j]], z.at(j, 0)), right_edge)
+        left_edge = jnp.where(hit, roll(values[westward[j]], z.at(j, 0) - 1), left_edge)
+    copies[-2].wait()
+    copies[-1].wait()
+    for step in range(whole_ref.shape[0]):
+        for k, ref in enumerate((whole_ref, part_ref)):
+            value = ref[step].astype(jnp.float32)
+            info_ref[pl.ds(2 * step + k, 1), :] = jnp.full((1, z.width), value, jnp.float32)
+    pack_x(z, whole_ref[0], get, right_edge, left_edge, sends)
+
+
+def collide_kernel(z, pop_ref, mask_ref, post_ref, acc_ref):
+    for y in range(z.planes):
         solid = z.solid_tile(mask_ref, y) > 0.5
         f = [z.tile(pop_ref, i, y) * np.float32(weights[i]) for i in range(Q)]
         post, jx, moment_xy = collide(f, solid)
@@ -419,13 +461,6 @@
             post_ref[i, here, :] = post[i]
         acc_ref[0, here, :] = jnp.where(solid, 0.0, jx)
         acc_ref[1, here, :] = jnp.where(solid, 0.0, -(1.0 - 0.5 * visc_rate) * moment_xy)
-    copies[-2].wait()
-    copies[-1].wait()
-    for step in range(whole_ref.shape[0]):
-        for k, ref in enumerate((whole_ref, part_ref)):
-            value = ref[step].astype(jnp.float32)
-            info_ref[pl.ds(2 * step + k, 1), :] = jnp.full((1, z.width), value, jnp.float32)
-    pack_x(z, whole_ref[0], post_ref, sends)
 
 
 def shift_of(info_ref, step):
@@ -436,11 +471,11 @@
 def second_kernel(z, info_ref, post_ref, mask_ref, *refs):
     gets, outs = refs[: z.count - 1], refs[z.count - 1 : z.count + 3]
     inner_ref, outer_ref, wall_ref, side_ref = outs
-    tops, bottoms, edges, rows_ref = refs[z.count + 3 :]
+    tops, bottoms, edges, rows_ref, columns_ref = refs[z.count + 3 :]
     whole, part = shift_of(info_ref, 0)
     left, right = fill_tables(z, post_ref, gets, tops, bottoms, edges)
     side_ref[0], side_ref[1] = left, right
-    columns = {1: left.T, -1: right.T}
+    columns_ref[0], columns_ref[1] = left.T, right.T
     shape = (z.planes, z.width)
     lanes = lax.broadcasted_iota(jnp.int32, shape, 1)
     heights = lax.broadcasted_iota(jnp.int32, shape, 0)
@@ -450,7 +485,8 @@
         value = post_ref[i, pl.ds(row, z.planes, stride=z.depth), :]
         if CX[i]:
             j = (eastward if CX[i] == 1 else westward).index(i)
-            column = columns[CX[i]][j * z.planes : (j + 1) * z.planes, row : row + 1]
+            here = pl.ds(z.at(j, 0), z.planes, stride=2)
+            column = columns_ref[0 if CX[i] == 1 else 1, here, :][:, row : row + 1]
             edge = 0 if CX[i] == 1 else z.width - 1
             value = jnp.where(lanes == edge, jnp.broadcast_to(column, shape), roll(value, CX[i]))
         if CY[i]:
@@ -588,7 +624,7 @@
             total = z.spread(jnp.sum(z.tile(acc_ref, k, y), axis=1, keepdims=True))
             sums = jnp.where(lanes == k * z.planes + y, total, sums)
     part_ref[...] = sums
-    pack_x(z, whole, g_ref, sends, sums)
+    pack_x(z, whole, functools.partial(z.tile, g_ref), *edge_tiles(z, g_ref), sends, sums)
 
 
 def direct_kernel(z, g_ref, acc_ref, out_hbm, acc_hbm, turned_ref, sems):
@@ -651,9 +687,13 @@
         if CX[i] == 0:
             send(out_ref.at[i, here, :], out_hbm.at[i, here, :])
 
+    for k in range(1, CHUNKS - 1):
+        interior(k)
+        finish(k)
+    for k in (0, CHUNKS - 1):
+        interior(k)
     sliding(z, whole, part, tops, bottoms, edges, put)
-    for k in range(CHUNKS):
-        interior(k)
+    for k in (0, CHUNKS - 1):
         finish(k)
     for copy in copies:
         copy.wait()
@@ -703,19 +743,21 @@
     across = [(i, (i - 1 if i % 2 == 0 else i + 1) % ranks) for i in range(ranks)]
 
     (pop,) = outer_keep(pop_ratio.reshape(cells.shape))
-    post, old, mask, info, *sends = call(
+    mask_shape = f32(planes // BLOCK * z.deep, width)
+    loaded, mask, info, *sends = call(
         first_kernel,
         [outside] * 4,
-        [cells, fields, f32(planes // BLOCK * z.deep, width), f32(2 * shift_whole.shape[0], width)] + buffers(0),
-        [pair, pair, cells, pltpu.VMEM(solid_blocks.shape, jnp.int32), sems(CHUNKS + 3)],
+        [cells, mask_shape, f32(2 * shift_whole.shape[0], width)] + buffers(0),
+        [pair, pair, pltpu.VMEM(solid_blocks.shape, jnp.int32), sems(CHUNKS + 3)],
     )(shift_whole, shift_frac, pop, solid_blocks)
+    post, old = call(collide_kernel, [vmem] * 2, [cells, fields])(*keep(loaded, mask))
     gets = swap_x(sends)
     walls, both = f32(2 * len(rising), depth, width), f32(2, depth, width)
     inner, outer, wall, side = call(
         second_kernel,
         [vmem] * (2 + count),
         [halo, halo, walls, both],
-        shifts + [f32(2, Q, planes, width)],
+        shifts + [f32(2, Q, planes, width), f32(2, width, depth)],
     )(*keep(info, post, mask, *gets))
     outer = lax.ppermute(outer, "gz", across)
     inner = lax.ppermute(inner, "gz", pairs)

time: 27 us -> 26.8 us (level)
  waiting for transfers between devices: 8.24 us -> 7.55 us
  Pallas kernels: 5.98 us -> 6.45 us
    ppermute x6, waiting for transfers between devices: 6.07 us -> 5.38 us  [swap_x(): lax.ppermute(values[d - 1], 'gx', [(i, i ^ d) for i in range(count)])]
    pallas_call x1 -> x2, Pallas kernels: 1.91 us -> 2.48 us  [the longest x1 1.79 us: local(): call(first_kernel, [outside] * 4, [cells, mask_shape, f32(2 * shift_whole...]
  transfers between devices with their start and end apart: 8 -> 8, of which waited for: 4 -> 4; matrix products, arithmetic and copies ran while one was open for 0% -> 0% of each run, Pallas kernels for 7% -> 10%
where the time goes in v7:
time: 26.8 us; the launch traced here: 26.6 us
  starting transfers between devices  11.9 us (44%)
  waiting for transfers between devices  7.55 us (28%)
  Pallas kernels  6.45 us (24%)
  between operations  0.71 us (3%)
    ppermute x6, starting transfers between devices, swap_x(): lax.ppermute(values[d - 1], 'gx', [(i, i ^ d) for i in range(count)])  8.15 us
    ppermute x6, waiting for transfers between devices, swap_x(): lax.ppermute(values[d - 1], 'gx', [(i, i ^ d) for i in range(count)])  5.38 us
    ppermute x1, starting transfers between devices, local(): outer = lax.ppermute(outer, 'gz', across)  3.7 us
    ppermute x1, waiting for transfers between devices, local(): outer = lax.ppermute(outer, 'gz', across)  2.17 us
    pallas_call x1, Pallas kernels, local(): call(first_kernel, [outside] * 4, [cells, mask_shape, f32(2 * shift_whole...  1.79 us
    pallas_call x1, Pallas kernels, local(): call(fourth_kernel, [vmem] * (3 + count) + [outside], [hbm(cells), hbm(f3...  1.25 us
    pallas_call x1, Pallas kernels, local(): call(direct_kernel, [vmem] * 2, [hbm(cells), hbm(fields), turned], [sems(...  0.92 us
    pallas_call x1, Pallas kernels, local(): call(collide_kernel, [vmem] * 2, [cells, fields])(*keep(loaded, mask))  0.68 us
  transfers between devices with their start and end apart: 8, of which 4 were waited for; matrix products, arithmetic and copies ran while one was open for 0% of the time, Pallas kernels for 10%

profile of v7, /device:TPU:0, one launch (start us, length us, event | category | flops | bytes accessed | tf_op | source)
XLA Modules:
  0.0 26.6 jit_solution(12786614583459752627)
XLA Ops:
  0.6 1.8 %shard_map.67 = (f32[19,128,128]{2,1,0:T(8,128)S(1)}, f32[8,128]{1,0:T(8,128)S(1)}, f32[4,128]{1,0:T(4,128)S(1)}, f32[6,8,128]{2,1,0:T(8,128)S(1)}, f32[11,8,128]{2,1,0:T(8,128)S(1)}, /*index=5*/f32[6,8,128]{2,1,0:T(8,128)S(1)}) custom-call(s32[2]{0:T(128)} %whole_hbm.1, s32[2]{0:T(128)} %part_hbm.1, f32[19,128,128]{2,1,0:T(8,128)} %bitcast.4, ...), custom_call_target="tpu_custom_call" | custom-call | tf_op jit(solution)/shard_map/pallas_call | solution.py:747
  2.4 3.1 %collective-permute-start.1 = (f32[11,8,128]{2,1,0:T(8,128)S(1)}, f32[11,8,128]{2,1,0:T(8,128)S(1)}, u32[]{:S(2)}, u32[]{:S(2)}) collective-permute-start(f32[11,8,128]{2,1,0:T(8,128)S(1)} %get-tuple-element.33), channel_id=1, source_target_pairs={{0,16},{8,24},{16,0},{24,8},{1,17},{9,25},{17,1},{25,9},{2,18},{10... | collective-permute-start | bytes 135176 | tf_op jit(solution)/shard_map/ppermute | solution.py:738
  5.5 1.5 %collective-permute-start = (f32[6,8,128]{2,1,0:T(8,128)S(1)}, f32[6,8,128]{2,1,0:T(8,128)S(1)}, u32[]{:S(2)}, u32[]{:S(2)}) collective-permute-start(f32[6,8,128]{2,1,0:T(8,128)S(1)} %get-tuple-element.32), channel_id=1, source_target_pairs={{0,8},{8,0},{16,24},{24,16},{1,9},{9,1},{17,25},{25,17},{2,10},{10... | collective-permute-start | bytes 73736 | tf_op jit(solution)/shard_map/ppermute | solution.py:738
  7.0 0.0 collective-permute-start.2
  7.0 0.7 %shard_map.68 = (f32[19,128,128]{2,1,0:T(8,128)S(1)}, f32[2,128,128]{2,1,0:T(8,128)S(1)}) custom-call(f32[19,128,128]{2,1,0:T(8,128)S(1)} %get-tuple-element.29.pop_ref, f32[8,128]{1,0:T(8,128)S(1)} %get-tuple-element.30.mask_ref), custom_call_target="tpu_custom_call" | custom-call | tf_op jit(solution)/shard_map/pallas_call | solution.py:753
  7.7 1.6 %collective-permute-done.refs_0_ = f32[6,8,128]{2,1,0:T(8,128)S(1)} collective-permute-done((f32[6,8,128]{2,1,0:T(8,128)S(1)}, f32[6,8,128]{2,1,0:T(8,128)S(1)}, u32[]{:S(2)}, u32[]{:S(2)}) %collective-permute-start) | collective-permute-done | bytes 24608 | tf_op jit(solution)/shard_map/ppermute | solution.py:738
  9.3 2.4 %collective-permute-done.2.refs_2_ = f32[6,8,128]{2,1,0:T(8,128)S(1)} collective-permute-done((f32[6,8,128]{2,1,0:T(8,128)S(1)}, f32[6,8,128]{2,1,0:T(8,128)S(1)}, u32[]{:S(2)}, u32[]{:S(2)}) %collective-permute-start.2) | collective-permute-done | bytes 24608 | tf_op jit(solution)/shard_map/ppermute | solution.py:738
  11.7 0.0 collective-permute-done.1.refs_1_
  11.7 0.4 %shard_map.69 = (f32[15,16,128]{2,1,0:T(8,128)S(1)}, f32[15,16,128]{2,1,0:T(8,128)S(1)}, f32[10,8,128]{2,1,0:T(8,128)S(1)}, f32[2,8,128]{2,1,0:T(8,128)S(1)}) custom-call(f32[4,128]{1,0:T(4,128)S(1)} %get-tuple-element.28.info_ref, f32[19,128,128]{2,1,0:T(8,128)S(1)} %get-tuple-element.31.post_ref, f32[8,128]{1,0:T(8,128)S(1)} %get-tuple-element.30.mask_ref, ...), custom_call_target="tpu_custom_call" | custom-call | tf_op jit(solution)/shard_map/pallas_call | solution.py:756
  12.1 0.1 collective-permute-start.3
  12.2 3.7 %collective-permute-start.4 = (f32[15,16,128]{2,1,0:T(8,128)S(1)}, f32[15,16,128]{2,1,0:T(8,128)S(1)}, u32[]{:S(2)}, u32[]{:S(2)}) collective-permute-start(f32[15,16,128]{2,1,0:T(8,128)S(1)} %get-tuple-element.38), channel_id=1, source_target_pairs={{0,7},{1,2},{2,1},{3,4},{4,3},{5,6},{6,5},{7,0},{8,15},{9,10},{10,... | collective-permute-start | bytes 368648 | tf_op jit(solution)/shard_map/ppermute | solution.py:762
  15.9 0.4 %shard_map.70.h_ref = f32[19,128,128]{2,1,0:T(8,128)S(1)} custom-call(f32[19,128,128]{2,1,0:T(8,128)S(1)} %get-tuple-element.31.post_ref, f32[10,8,128]{2,1,0:T(8,128)S(1)} %get-tuple-element.35.wall_ref, f32[2,8,128]{2,1,0:T(8,128)S(1)} %get-tuple-element.36.side_ref), custom_call_target="tpu_custom_call" | custom-call | tf_op jit(solution)/shard_map/pallas_call | solution.py:764
  16.3 0.5 %shard_map.71 = (f32[19,128,128]{2,1,0:T(8,128)S(1)}, f32[2,128,128]{2,1,0:T(8,128)S(1)}) custom-call(f32[19,128,128]{2,1,0:T(8,128)S(1)} %shard_map.70.h_ref, f32[8,128]{1,0:T(8,128)S(1)} %get-tuple-element.30.mask_ref, f32[2,128,128]{2,1,0:T(8,128)S(1)} %get-tuple-element.39.old_ref), custom_call_target="tpu_custom_call" | custom-call | tf_op jit(solution)/shard_map/pallas_call | solution.py:765
  16.9 0.0 collective-permute-done.3.inner_ref
  16.9 2.2 %collective-permute-done.4.outer_ref = f32[15,16,128]{2,1,0:T(8,128)S(1)} collective-permute-done((f32[15,16,128]{2,1,0:T(8,128)S(1)}, f32[15,16,128]{2,1,0:T(8,128)S(1)}, u32[]{:S(2)}, u32[]{:S(2)}) %collective-permute-start.4) | collective-permute-done | bytes 122912 | tf_op jit(solution)/shard_map/ppermute | solution.py:762
  19.1 0.4 %shard_map.72 = (f32[19,128,128]{2,1,0:T(8,128)S(1)}, f32[2,128,128]{2,1,0:T(8,128)S(1)}, f32[8,128]{1,0:T(8,128)S(1)}, f32[7,8,128]{2,1,0:T(8,128)S(1)}, f32[12...) custom-call(f32[4,128]{1,0:T(4,128)S(1)} %get-tuple-element.28.info_ref, ...), custom_call_target="tpu_custom_call", output_to_operand_aliasing={{0}: (6, {}), {1}: (7, {})} | custom-call | tf_op jit(solution)/shard_map/pallas_call | solution.py:766
  19.5 0.6 %collective-permute-start.6 = (f32[12,8,128]{2,1,0:T(8,128)S(1)}, f32[12,8,128]{2,1,0:T(8,128)S(1)}, u32[]{:S(2)}, u32[]{:S(2)}) collective-permute-start(f32[12,8,128]{2,1,0:T(8,128)S(1)} %get-tuple-element.47), channel_id=1, source_target_pairs={{0,16},{8,24},{16,0},{24,8},{1,17},{9,25},{17,1},{25,9},{2,18},{10... | collective-permute-start | bytes 147464 | tf_op jit(solution)/shard_map/ppermute | solution.py:738
  20.1 0.5 %collective-permute-start.5 = (f32[7,8,128]{2,1,0:T(8,128)S(1)}, f32[7,8,128]{2,1,0:T(8,128)S(1)}, u32[]{:S(2)}, u32[]{:S(2)}) collective-permute-start(f32[7,8,128]{2,1,0:T(8,128)S(1)} %get-tuple-element.46), channel_id=1, source_target_pairs={{0,8},{8,0},{16,24},{24,16},{1,9},{9,1},{17,25},{25,17},{2,10},{10... | collective-permute-start | bytes 86024 | tf_op jit(solution)/shard_map/ppermute | solution.py:738
  20.6 2.4 %collective-permute-start.7 = (f32[7,8,128]{2,1,0:T(8,128)S(1)}, f32[7,8,128]{2,1,0:T(8,128)S(1)}, u32[]{:S(2)}, u32[]{:S(2)}) collective-permute-start(f32[7,8,128]{2,1,0:T(8,128)S(1)} %get-tuple-element.48), channel_id=1, source_target_pairs={{0,24},{8,16},{16,8},{24,0},{1,25},{9,17},{17,9},{25,1},{2,26},{10... | collective-permute-start | bytes 86024 | tf_op jit(solution)/shard_map/ppermute | solution.py:738
  23.1 0.9 %shard_map.73 = (f32[19,128,128]{2,1,0:T(8,128)}, f32[2,128,128]{2,1,0:T(8,128)}, f32[10,128,128]{2,1,0:T(8,128)S(1)}) custom-call(f32[19,128,128]{2,1,0:T(8,128)S(1)} %get-tuple-element.42.g_ref, f32[2,128,128]{2,1,0:T(8,128)S(1)} %get-tuple-element.43.acc_ref), custom_call_target="tpu_custom_call" | custom-call | tf_op jit(solution)/shard_map/pallas_call | solution.py:775
  24.0 0.0 collective-permute-done.5.refs_0_
  24.0 1.4 %collective-permute-done.7.refs_2_ = f32[7,8,128]{2,1,0:T(8,128)S(1)} collective-permute-done((f32[7,8,128]{2,1,0:T(8,128)S(1)}, f32[7,8,128]{2,1,0:T(8,128)S(1)}, u32[]{:S(2)}, u32[]{:S(2)}) %collective-permute-start.7) | collective-permute-done | bytes 28704 | tf_op jit(solution)/shard_map/ppermute | solution.py:738
  25.4 0.0 collective-permute-done.6.refs_1_
  25.4 1.2 %shard_map.74 = (f32[19,128,128]{2,1,0:T(8,128)}, f32[2,8,16]{2,1,0:T(8,128)}) custom-call(f32[4,128]{1,0:T(4,128)S(1)} %get-tuple-element.28.info_ref, f32[19,128,128]{2,1,0:T(8,128)S(1)} %get-tuple-element.42.g_ref, f32[10,128,128]{2,1,0:T(8,128)S(1)} %get-tuple-element.44.turned_ref, ...), custom_call_target="tpu_custom_call", output_to_operand_aliasing={{0}: (7, {})} | custom-call | tf_op jit(solution)/shard_map/pallas_call | solution.py:783
Async XLA Ops:
  2.4 9.3 %collective-permute-start.1 = (f32[11,8,128]{2,1,0:T(8,128)S(1)}, f32[11,8,128]{2,1,0:T(8,128)S(1)}, u32[]{:S(2)}, u32[]{:S(2)}) collective-permute-start(f32[11,8,128]{2,1,0:T(8,128)S(1)} %get-tuple-element.33), channel_id=1, source_target_pairs={{0,16},{8,24},{16,0},{24,8},{1,17},{9,25},{17,1},{25,9},{2,18},{10... | collective-permute-start | bytes 135176 | tf_op jit(solution)/shard_map/ppermute | solution.py:738
  5.5 3.8 %collective-permute-start = (f32[6,8,128]{2,1,0:T(8,128)S(1)}, f32[6,8,128]{2,1,0:T(8,128)S(1)}, u32[]{:S(2)}, u32[]{:S(2)}) collective-permute-start(f32[6,8,128]{2,1,0:T(8,128)S(1)} %get-tuple-element.32), channel_id=1, source_target_pairs={{0,8},{8,0},{16,24},{24,16},{1,9},{9,1},{17,25},{25,17},{2,10},{10... | collective-permute-start | bytes 73736 | tf_op jit(solution)/shard_map/ppermute | solution.py:738
  7.0 4.7 %collective-permute-start.2 = (f32[6,8,128]{2,1,0:T(8,128)S(1)}, f32[6,8,128]{2,1,0:T(8,128)S(1)}, u32[]{:S(2)}, u32[]{:S(2)}) collective-permute-start(f32[6,8,128]{2,1,0:T(8,128)S(1)} %get-tuple-element.34), channel_id=1, source_target_pairs={{0,24},{8,16},{16,8},{24,0},{1,25},{9,17},{17,9},{25,1},{2,26},{10... | collective-permute-start | bytes 73736 | tf_op jit(solution)/shard_map/ppermute | solution.py:738
  12.1 4.7 %collective-permute-start.3 = (f32[15,16,128]{2,1,0:T(8,128)S(1)}, f32[15,16,128]{2,1,0:T(8,128)S(1)}, u32[]{:S(2)}, u32[]{:S(2)}) collective-permute-start(f32[15,16,128]{2,1,0:T(8,128)S(1)} %get-tuple-element.37), channel_id=1, source_target_pairs={{0,1},{1,0},{2,3},{3,2},{4,5},{5,4},{6,7},{7,6},{8,9},{9,8},{10,11... | collective-permute-start | bytes 368648 | tf_op jit(solution)/shard_map/ppermute | solution.py:763
  12.2 6.8 %collective-permute-start.4 = (f32[15,16,128]{2,1,0:T(8,128)S(1)}, f32[15,16,128]{2,1,0:T(8,128)S(1)}, u32[]{:S(2)}, u32[]{:S(2)}) collective-permute-start(f32[15,16,128]{2,1,0:T(8,128)S(1)} %get-tuple-element.38), channel_id=1, source_target_pairs={{0,7},{1,2},{2,1},{3,4},{4,3},{5,6},{6,5},{7,0},{8,15},{9,10},{10,... | collective-permute-start | bytes 368648 | tf_op jit(solution)/shard_map/ppermute | solution.py:762
  19.5 5.9 %collective-permute-start.6 = (f32[12,8,128]{2,1,0:T(8,128)S(1)}, f32[12,8,128]{2,1,0:T(8,128)S(1)}, u32[]{:S(2)}, u32[]{:S(2)}) collective-permute-start(f32[12,8,128]{2,1,0:T(8,128)S(1)} %get-tuple-element.47), channel_id=1, source_target_pairs={{0,16},{8,24},{16,0},{24,8},{1,17},{9,25},{17,1},{25,9},{2,18},{10... | collective-permute-start | bytes 147464 | tf_op jit(solution)/shard_map/ppermute | solution.py:738
  20.1 3.9 %collective-permute-start.5 = (f32[7,8,128]{2,1,0:T(8,128)S(1)}, f32[7,8,128]{2,1,0:T(8,128)S(1)}, u32[]{:S(2)}, u32[]{:S(2)}) collective-permute-start(f32[7,8,128]{2,1,0:T(8,128)S(1)} %get-tuple-element.46), channel_id=1, source_target_pairs={{0,8},{8,0},{16,24},{24,16},{1,9},{9,1},{17,25},{25,17},{2,10},{10... | collective-permute-start | bytes 86024 | tf_op jit(solution)/shard_map/ppermute | solution.py:738
  20.6 4.8 %collective-permute-start.7 = (f32[7,8,128]{2,1,0:T(8,128)S(1)}, f32[7,8,128]{2,1,0:T(8,128)S(1)}, u32[]{:S(2)}, u32[]{:S(2)}) collective-permute-start(f32[7,8,128]{2,1,0:T(8,128)S(1)} %get-tuple-element.48), channel_id=1, source_target_pairs={{0,24},{8,16},{16,8},{24,0},{1,25},{9,17},{17,9},{25,1},{2,26},{10... | collective-permute-start | bytes 86024 | tf_op jit(solution)/shard_map/ppermute | solution.py:738

commit v8 on v7

--- a/solution.py
+++ b/solution.py
@@ -219,6 +219,7 @@
 
 
 CHUNKS = 4
+LOADS = 2
 
 
 class Sizes:
@@ -397,13 +398,13 @@
 
 def first_kernel(z, whole_hbm, part_hbm, pop_hbm, solid_hbm, pop_ref, mask_ref, info_ref, *refs):
     sends, (whole_ref, part_ref, solid_ref, sems) = refs[: z.count - 1], refs[z.count - 1 :]
-    group = z.planes // CHUNKS * z.depth
-    copies = [pltpu.make_async_copy(solid_hbm, solid_ref, sems.at[CHUNKS])]
-    for k in range(CHUNKS):
+    group = z.planes // LOADS * z.depth
+    copies = [pltpu.make_async_copy(solid_hbm, solid_ref, sems.at[LOADS])]
+    for k in range(LOADS):
         part = (slice(None), pl.ds(k * group, group), slice(None))
         copies.append(pltpu.make_async_copy(pop_hbm.at[part], pop_ref.at[part], sems.at[k]))
-    copies.append(pltpu.make_async_copy(whole_hbm, whole_ref, sems.at[CHUNKS + 1]))
-    copies.append(pltpu.make_async_copy(part_hbm, part_ref, sems.at[CHUNKS + 2]))
+    copies.append(pltpu.make_async_copy(whole_hbm, whole_ref, sems.at[LOADS + 1]))
+    copies.append(pltpu.make_async_copy(part_hbm, part_ref, sems.at[LOADS + 2]))
     for copy in copies:
         copy.start()
     copies[0].wait()
@@ -419,8 +420,8 @@
     couple = lanes // 2
     post, edge, solid_edge = {}, [None] * Q, None
     for y in range(z.planes):
-        if y % (z.planes // CHUNKS) == 0:
-            copies[1 + y // (z.planes // CHUNKS)].wait()
+        if y % (z.planes // LOADS) == 0:
+            copies[1 + y // (z.planes // LOADS)].wait()
         flags = z.solid_tile(mask_ref, y)
         if y in (0, z.planes - 1):
             f = [z.tile(pop_ref, i, y) * np.float32(weights[i]) for i in range(Q)]
@@ -464,7 +465,7 @@
 
 
 def shift_of(info_ref, step):
-    values = [jnp.max(info_ref[2 * step + k : 2 * step + k + 1, :]) for k in range(2)]
+    values = [info_ref[2 * step + k : 2 * step + k + 1, :][0, 0] for k in range(2)]
     return [value.astype(jnp.int32) for value in values]
 
 
@@ -748,7 +749,7 @@
         first_kernel,
         [outside] * 4,
         [cells, mask_shape, f32(2 * shift_whole.shape[0], width)] + buffers(0),
-        [pair, pair, pltpu.VMEM(solid_blocks.shape, jnp.int32), sems(CHUNKS + 3)],
+        [pair, pair, pltpu.VMEM(solid_blocks.shape, jnp.int32), sems(LOADS + 3)],
     )(shift_whole, shift_frac, pop, solid_blocks)
     post, old = call(collide_kernel, [vmem] * 2, [cells, fields])(*keep(loaded, mask))
     gets = swap_x(sends)

time: 26.8 us -> 26.8 us (level)
  no operation moved by 1% of the time
where the time goes in v8:
time: 26.8 us; the launch traced here: 26.6 us
  starting transfers between devices  11.9 us (44%)
  waiting for transfers between devices  7.55 us (28%)
  Pallas kernels  6.4 us (24%)
  between operations  0.71 us (3%)
    ppermute x6, starting transfers between devices, swap_x(): lax.ppermute(values[d - 1], 'gx', [(i, i ^ d) for i in range(count)])  8.15 us
    ppermute x6, waiting for transfers between devices, swap_x(): lax.ppermute(values[d - 1], 'gx', [(i, i ^ d) for i in range(count)])  5.38 us
    ppermute x1, starting transfers between devices, local(): outer = lax.ppermute(outer, 'gz', across)  3.7 us
    ppermute x1, waiting for transfers between devices, local(): outer = lax.ppermute(outer, 'gz', across)  2.17 us
    pallas_call x1, Pallas kernels, local(): call(first_kernel, [outside] * 4, [cells, mask_shape, f32(2 * shift_whole...  1.75 us
    pallas_call x1, Pallas kernels, local(): call(fourth_kernel, [vmem] * (3 + count) + [outside], [hbm(cells), hbm(f3...  1.25 us
    pallas_call x1, Pallas kernels, local(): call(direct_kernel, [vmem] * 2, [hbm(cells), hbm(fields), turned], [sems(...  0.92 us
    pallas_call x1, Pallas kernels, local(): call(collide_kernel, [vmem] * 2, [cells, fields])(*keep(loaded, mask))  0.68 us
  transfers between devices with their start and end apart: 8, of which 4 were waited for; matrix products, arithmetic and copies ran while one was open for 0% of the time, Pallas kernels for 10%

profile of v8, /device:TPU:0, one launch (start us, length us, event | category | flops | bytes accessed | tf_op | source)
XLA Modules:
  0.0 26.6 jit_solution(13171902115164442530)
XLA Ops:
  0.6 1.7 %shard_map.67 = (f32[19,128,128]{2,1,0:T(8,128)S(1)}, f32[8,128]{1,0:T(8,128)S(1)}, f32[4,128]{1,0:T(4,128)S(1)}, f32[6,8,128]{2,1,0:T(8,128)S(1)}, f32[11,8,128]{2,1,0:T(8,128)S(1)}, /*index=5*/f32[6,8,128]{2,1,0:T(8,128)S(1)}) custom-call(s32[2]{0:T(128)} %whole_hbm.1, s32[2]{0:T(128)} %part_hbm.1, f32[19,128,128]{2,1,0:T(8,128)} %bitcast.4, ...), custom_call_target="tpu_custom_call" | custom-call | tf_op jit(solution)/shard_map/pallas_call | solution.py:748
  2.4 3.1 %collective-permute-start.1 = (f32[11,8,128]{2,1,0:T(8,128)S(1)}, f32[11,8,128]{2,1,0:T(8,128)S(1)}, u32[]{:S(2)}, u32[]{:S(2)}) collective-permute-start(f32[11,8,128]{2,1,0:T(8,128)S(1)} %get-tuple-element.33), channel_id=1, source_target_pairs={{0,16},{8,24},{16,0},{24,8},{1,17},{9,25},{17,1},{25,9},{2,18},{10... | collective-permute-start | bytes 135176 | tf_op jit(solution)/shard_map/ppermute | solution.py:739
  5.4 1.5 %collective-permute-start = (f32[6,8,128]{2,1,0:T(8,128)S(1)}, f32[6,8,128]{2,1,0:T(8,128)S(1)}, u32[]{:S(2)}, u32[]{:S(2)}) collective-permute-start(f32[6,8,128]{2,1,0:T(8,128)S(1)} %get-tuple-element.32), channel_id=1, source_target_pairs={{0,8},{8,0},{16,24},{24,16},{1,9},{9,1},{17,25},{25,17},{2,10},{10... | collective-permute-start | bytes 73736 | tf_op jit(solution)/shard_map/ppermute | solution.py:739
  6.9 0.0 collective-permute-start.2
  7.0 0.7 %shard_map.68 = (f32[19,128,128]{2,1,0:T(8,128)S(1)}, f32[2,128,128]{2,1,0:T(8,128)S(1)}) custom-call(f32[19,128,128]{2,1,0:T(8,128)S(1)} %get-tuple-element.29.pop_ref, f32[8,128]{1,0:T(8,128)S(1)} %get-tuple-element.30.mask_ref), custom_call_target="tpu_custom_call" | custom-call | tf_op jit(solution)/shard_map/pallas_call | solution.py:754
  7.7 1.6 %collective-permute-done.refs_0_ = f32[6,8,128]{2,1,0:T(8,128)S(1)} collective-permute-done((f32[6,8,128]{2,1,0:T(8,128)S(1)}, f32[6,8,128]{2,1,0:T(8,128)S(1)}, u32[]{:S(2)}, u32[]{:S(2)}) %collective-permute-start) | collective-permute-done | bytes 24608 | tf_op jit(solution)/shard_map/ppermute | solution.py:739
  9.3 2.4 %collective-permute-done.2.refs_2_ = f32[6,8,128]{2,1,0:T(8,128)S(1)} collective-permute-done((f32[6,8,128]{2,1,0:T(8,128)S(1)}, f32[6,8,128]{2,1,0:T(8,128)S(1)}, u32[]{:S(2)}, u32[]{:S(2)}) %collective-permute-start.2) | collective-permute-done | bytes 24608 | tf_op jit(solution)/shard_map/ppermute | solution.py:739
  11.7 0.0 collective-permute-done.1.refs_1_
  11.7 0.4 %shard_map.69 = (f32[15,16,128]{2,1,0:T(8,128)S(1)}, f32[15,16,128]{2,1,0:T(8,128)S(1)}, f32[10,8,128]{2,1,0:T(8,128)S(1)}, f32[2,8,128]{2,1,0:T(8,128)S(1)}) custom-call(f32[4,128]{1,0:T(4,128)S(1)} %get-tuple-element.28.info_ref, f32[19,128,128]{2,1,0:T(8,128)S(1)} %get-tuple-element.31.post_ref, f32[8,128]{1,0:T(8,128)S(1)} %get-tuple-element.30.mask_ref, ...), custom_call_target="tpu_custom_call" | custom-call | tf_op jit(solution)/shard_map/pallas_call | solution.py:757
  12.1 0.1 collective-permute-start.3
  12.2 3.7 %collective-permute-start.4 = (f32[15,16,128]{2,1,0:T(8,128)S(1)}, f32[15,16,128]{2,1,0:T(8,128)S(1)}, u32[]{:S(2)}, u32[]{:S(2)}) collective-permute-start(f32[15,16,128]{2,1,0:T(8,128)S(1)} %get-tuple-element.38), channel_id=1, source_target_pairs={{0,7},{1,2},{2,1},{3,4},{4,3},{5,6},{6,5},{7,0},{8,15},{9,10},{10,... | collective-permute-start | bytes 368648 | tf_op jit(solution)/shard_map/ppermute | solution.py:763
  15.9 0.4 %shard_map.70.h_ref = f32[19,128,128]{2,1,0:T(8,128)S(1)} custom-call(f32[19,128,128]{2,1,0:T(8,128)S(1)} %get-tuple-element.31.post_ref, f32[10,8,128]{2,1,0:T(8,128)S(1)} %get-tuple-element.35.wall_ref, f32[2,8,128]{2,1,0:T(8,128)S(1)} %get-tuple-element.36.side_ref), custom_call_target="tpu_custom_call" | custom-call | tf_op jit(solution)/shard_map/pallas_call | solution.py:765
  16.3 0.5 %shard_map.71 = (f32[19,128,128]{2,1,0:T(8,128)S(1)}, f32[2,128,128]{2,1,0:T(8,128)S(1)}) custom-call(f32[19,128,128]{2,1,0:T(8,128)S(1)} %shard_map.70.h_ref, f32[8,128]{1,0:T(8,128)S(1)} %get-tuple-element.30.mask_ref, f32[2,128,128]{2,1,0:T(8,128)S(1)} %get-tuple-element.39.old_ref), custom_call_target="tpu_custom_call" | custom-call | tf_op jit(solution)/shard_map/pallas_call | solution.py:766
  16.8 0.0 collective-permute-done.3.inner_ref
  16.8 2.2 %collective-permute-done.4.outer_ref = f32[15,16,128]{2,1,0:T(8,128)S(1)} collective-permute-done((f32[15,16,128]{2,1,0:T(8,128)S(1)}, f32[15,16,128]{2,1,0:T(8,128)S(1)}, u32[]{:S(2)}, u32[]{:S(2)}) %collective-permute-start.4) | collective-permute-done | bytes 122912 | tf_op jit(solution)/shard_map/ppermute | solution.py:763
  19.0 0.4 %shard_map.72 = (f32[19,128,128]{2,1,0:T(8,128)S(1)}, f32[2,128,128]{2,1,0:T(8,128)S(1)}, f32[8,128]{1,0:T(8,128)S(1)}, f32[7,8,128]{2,1,0:T(8,128)S(1)}, f32[12...) custom-call(f32[4,128]{1,0:T(4,128)S(1)} %get-tuple-element.28.info_ref, ...), custom_call_target="tpu_custom_call", output_to_operand_aliasing={{0}: (6, {}), {1}: (7, {})} | custom-call | tf_op jit(solution)/shard_map/pallas_call | solution.py:767
  19.5 0.6 %collective-permute-start.6 = (f32[12,8,128]{2,1,0:T(8,128)S(1)}, f32[12,8,128]{2,1,0:T(8,128)S(1)}, u32[]{:S(2)}, u32[]{:S(2)}) collective-permute-start(f32[12,8,128]{2,1,0:T(8,128)S(1)} %get-tuple-element.47), channel_id=1, source_target_pairs={{0,16},{8,24},{16,0},{24,8},{1,17},{9,25},{17,1},{25,9},{2,18},{10... | collective-permute-start | bytes 147464 | tf_op jit(solution)/shard_map/ppermute | solution.py:739
  20.0 0.5 %collective-permute-start.5 = (f32[7,8,128]{2,1,0:T(8,128)S(1)}, f32[7,8,128]{2,1,0:T(8,128)S(1)}, u32[]{:S(2)}, u32[]{:S(2)}) collective-permute-start(f32[7,8,128]{2,1,0:T(8,128)S(1)} %get-tuple-element.46), channel_id=1, source_target_pairs={{0,8},{8,0},{16,24},{24,16},{1,9},{9,1},{17,25},{25,17},{2,10},{10... | collective-permute-start | bytes 86024 | tf_op jit(solution)/shard_map/ppermute | solution.py:739
  20.6 2.4 %collective-permute-start.7 = (f32[7,8,128]{2,1,0:T(8,128)S(1)}, f32[7,8,128]{2,1,0:T(8,128)S(1)}, u32[]{:S(2)}, u32[]{:S(2)}) collective-permute-start(f32[7,8,128]{2,1,0:T(8,128)S(1)} %get-tuple-element.48), channel_id=1, source_target_pairs={{0,24},{8,16},{16,8},{24,0},{1,25},{9,17},{17,9},{25,1},{2,26},{10... | collective-permute-start | bytes 86024 | tf_op jit(solution)/shard_map/ppermute | solution.py:739
  23.0 0.9 %shard_map.73 = (f32[19,128,128]{2,1,0:T(8,128)}, f32[2,128,128]{2,1,0:T(8,128)}, f32[10,128,128]{2,1,0:T(8,128)S(1)}) custom-call(f32[19,128,128]{2,1,0:T(8,128)S(1)} %get-tuple-element.42.g_ref, f32[2,128,128]{2,1,0:T(8,128)S(1)} %get-tuple-element.43.acc_ref), custom_call_target="tpu_custom_call" | custom-call | tf_op jit(solution)/shard_map/pallas_call | solution.py:776
  23.9 0.0 collective-permute-done.5.refs_0_
  23.9 1.4 %collective-permute-done.7.refs_2_ = f32[7,8,128]{2,1,0:T(8,128)S(1)} collective-permute-done((f32[7,8,128]{2,1,0:T(8,128)S(1)}, f32[7,8,128]{2,1,0:T(8,128)S(1)}, u32[]{:S(2)}, u32[]{:S(2)}) %collective-permute-start.7) | collective-permute-done | bytes 28704 | tf_op jit(solution)/shard_map/ppermute | solution.py:739
  25.3 0.0 collective-permute-done.6.refs_1_
  25.3 1.3 %shard_map.74 = (f32[19,128,128]{2,1,0:T(8,128)}, f32[2,8,16]{2,1,0:T(8,128)}) custom-call(f32[4,128]{1,0:T(4,128)S(1)} %get-tuple-element.28.info_ref, f32[19,128,128]{2,1,0:T(8,128)S(1)} %get-tuple-element.42.g_ref, f32[10,128,128]{2,1,0:T(8,128)S(1)} %get-tuple-element.44.turned_ref, ...), custom_call_target="tpu_custom_call", output_to_operand_aliasing={{0}: (7, {})} | custom-call | tf_op jit(solution)/shard_map/pallas_call | solution.py:784
Async XLA Ops:
  2.4 9.3 %collective-permute-start.1 = (f32[11,8,128]{2,1,0:T(8,128)S(1)}, f32[11,8,128]{2,1,0:T(8,128)S(1)}, u32[]{:S(2)}, u32[]{:S(2)}) collective-permute-start(f32[11,8,128]{2,1,0:T(8,128)S(1)} %get-tuple-element.33), channel_id=1, source_target_pairs={{0,16},{8,24},{16,0},{24,8},{1,17},{9,25},{17,1},{25,9},{2,18},{10... | collective-permute-start | bytes 135176 | tf_op jit(solution)/shard_map/ppermute | solution.py:739
  5.4 3.8 %collective-permute-start = (f32[6,8,128]{2,1,0:T(8,128)S(1)}, f32[6,8,128]{2,1,0:T(8,128)S(1)}, u32[]{:S(2)}, u32[]{:S(2)}) collective-permute-start(f32[6,8,128]{2,1,0:T(8,128)S(1)} %get-tuple-element.32), channel_id=1, source_target_pairs={{0,8},{8,0},{16,24},{24,16},{1,9},{9,1},{17,25},{25,17},{2,10},{10... | collective-permute-start | bytes 73736 | tf_op jit(solution)/shard_map/ppermute | solution.py:739
  6.9 4.7 %collective-permute-start.2 = (f32[6,8,128]{2,1,0:T(8,128)S(1)}, f32[6,8,128]{2,1,0:T(8,128)S(1)}, u32[]{:S(2)}, u32[]{:S(2)}) collective-permute-start(f32[6,8,128]{2,1,0:T(8,128)S(1)} %get-tuple-element.34), channel_id=1, source_target_pairs={{0,24},{8,16},{16,8},{24,0},{1,25},{9,17},{17,9},{25,1},{2,26},{10... | collective-permute-start | bytes 73736 | tf_op jit(solution)/shard_map/ppermute | solution.py:739
  12.1 4.7 %collective-permute-start.3 = (f32[15,16,128]{2,1,0:T(8,128)S(1)}, f32[15,16,128]{2,1,0:T(8,128)S(1)}, u32[]{:S(2)}, u32[]{:S(2)}) collective-permute-start(f32[15,16,128]{2,1,0:T(8,128)S(1)} %get-tuple-element.37), channel_id=1, source_target_pairs={{0,1},{1,0},{2,3},{3,2},{4,5},{5,4},{6,7},{7,6},{8,9},{9,8},{10,11... | collective-permute-start | bytes 368648 | tf_op jit(solution)/shard_map/ppermute | solution.py:764
  12.2 6.8 %collective-permute-start.4 = (f32[15,16,128]{2,1,0:T(8,128)S(1)}, f32[15,16,128]{2,1,0:T(8,128)S(1)}, u32[]{:S(2)}, u32[]{:S(2)}) collective-permute-start(f32[15,16,128]{2,1,0:T(8,128)S(1)} %get-tuple-element.38), channel_id=1, source_target_pairs={{0,7},{1,2},{2,1},{3,4},{4,3},{5,6},{6,5},{7,0},{8,15},{9,10},{10,... | collective-permute-start | bytes 368648 | tf_op jit(solution)/shard_map/ppermute | solution.py:763
  19.5 5.9 %collective-permute-start.6 = (f32[12,8,128]{2,1,0:T(8,128)S(1)}, f32[12,8,128]{2,1,0:T(8,128)S(1)}, u32[]{:S(2)}, u32[]{:S(2)}) collective-permute-start(f32[12,8,128]{2,1,0:T(8,128)S(1)} %get-tuple-element.47), channel_id=1, source_target_pairs={{0,16},{8,24},{16,0},{24,8},{1,17},{9,25},{17,1},{25,9},{2,18},{10... | collective-permute-start | bytes 147464 | tf_op jit(solution)/shard_map/ppermute | solution.py:739
  20.0 3.9 %collective-permute-start.5 = (f32[7,8,128]{2,1,0:T(8,128)S(1)}, f32[7,8,128]{2,1,0:T(8,128)S(1)}, u32[]{:S(2)}, u32[]{:S(2)}) collective-permute-start(f32[7,8,128]{2,1,0:T(8,128)S(1)} %get-tuple-element.46), channel_id=1, source_target_pairs={{0,8},{8,0},{16,24},{24,16},{1,9},{9,1},{17,25},{25,17},{2,10},{10... | collective-permute-start | bytes 86024 | tf_op jit(solution)/shard_map/ppermute | solution.py:739
  20.6 4.8 %collective-permute-start.7 = (f32[7,8,128]{2,1,0:T(8,128)S(1)}, f32[7,8,128]{2,1,0:T(8,128)S(1)}, u32[]{:S(2)}, u32[]{:S(2)}) collective-permute-start(f32[7,8,128]{2,1,0:T(8,128)S(1)} %get-tuple-element.48), channel_id=1, source_target_pairs={{0,24},{8,16},{16,8},{24,0},{1,25},{9,17},{17,9},{25,1},{2,26},{10... | collective-permute-start | bytes 86024 | tf_op jit(solution)/shard_map/ppermute | solution.py:739
